TPU v7x, 32 devices: a whole 2x2x4 slice. The times are simulated.
32 devices in a mesh: row: 2 (over x), col: 8 (over z, core), pair: 2 (over y).
Axes of the slice: x: 2, y: 2, z: 4, core: 2. Of those that a mesh axis runs over, the one named last changes fastest.
Arguments:
- integrals: bfloat16 [1024, 4096], P('row', 'col'), may hold values from -0.09375 to 0.09375
- kept_tiles: int32 [64, 256], P('row', 'col'), may hold values 0 or 1
- amplitudes: bfloat16 [4096, 1536], P(('col', 'row'), 'pair'), may hold values from -6 to 6
- driver: bfloat16 [1024, 1536], P(('row', 'col', 'pair')), may hold values from -6 to 6
- vir_energy: float32 [1024], P(('row', 'col', 'pair')), may hold values from 1 to 3
- occ_energy: float32 [1536], replicated, may hold values from -1.5 to -0.25
- occ_coupling: bfloat16 [1536, 1536], replicated, may hold values from -0.15625 to 0.15625
Outputs:
- increment: float32 [1024, 1536], P(('row', 'col', 'pair'))
All inputs are finite; a program needn't handle non-finite values. No bound on the sum of `kept_tiles` on one device may be relied on, other than what follows from the above.
Results may differ from a plain program's by a relative error of at most 0.0011.
Values may be sent and summed in bfloat16 or wider, within the bound.
No kernel may reach another device: no remote copies, remote signals or barrier semaphores. Data moves between devices by JAX's collectives and lax.ppermute only.
A program may use at most 64 MiB of HBM per device.

v0:
```python
import jax
import jax.numpy as jnp
from jax import lax
from jax.experimental import pallas as pl
from jax.experimental.pallas import tpu as pltpu
from jax.sharding import PartitionSpec as P


SCALE = 8.0


def flip(value, axes, sizes, steps):
    pairs = []
    total = 1
    for size in sizes:
        total *= size
    for source in range(total):
        rest, target, scale = source, 0, 1
        for size, step in zip(reversed(sizes), reversed(steps)):
            target += ((rest % size) ^ step) * scale
            rest //= size
            scale *= size
        pairs.append((source, target))
    return lax.ppermute(value, axes, pairs)


def update_kernel(ladder, driver, vir, occ, coupling, out):
    denom = vir[...] - occ[...]
    residual = driver[...].astype(jnp.float32) + ladder[...] * (1 / SCALE)
    scaled = (residual / denom).astype(jnp.bfloat16)
    coupled = jnp.dot(scaled, coupling[...], preferred_element_type=jnp.float32)
    out[...] = -(residual - coupled) / denom


def update(ladder, driver, vir_energy, occ_energy, occ_coupling):
    rows, columns = ladder.shape
    return pl.pallas_call(
        update_kernel,
        out_shape=jax.ShapeDtypeStruct((rows, columns), jnp.float32),
        compiler_params=pltpu.CompilerParams(vmem_limit_bytes=16 * 2**20),
        name="update",
    )(ladder, driver, vir_energy[:, None], occ_energy[None, :], occ_coupling)


def halves(value, bit, axis):
    low, high = jnp.split(value, 2, axis)
    return jnp.where(bit == 0, low, high), jnp.where(bit == 0, high, low)


def chunk_bounds(columns):
    return [(0, columns)]


def z_order(chips):
    return [chips // 2] + [s for s in range(1, chips) if s != chips // 2] if chips > 1 else []


def solution(mesh):
    rows_n, cols_n, pair_n = mesh.shape["row"], mesh.shape["col"], mesh.shape["pair"]
    chips = cols_n // 2

    def body(integrals, kept_tiles, amplitudes, driver, vir_energy, occ_energy, occ_coupling):
        row, col, pair = (lax.axis_index(a) for a in ("row", "col", "pair"))
        core, chip = col & 1, col >> 1
        depth, width = amplitudes.shape
        own_rows = driver.shape[0]
        bounds = chunk_bounds(width)

        mine, others = [], []
        for low, high in bounds:
            a, b = halves(amplitudes[:, low:high], core, 1)
            mine.append(a)
            others.append(b)
        far, near = [], []
        for a, b in zip(mine, others):
            blocks = []
            for step in range(1, rows_n):
                blocks.append(flip(a, ("row", "col"), (rows_n, cols_n), (step, 0)))
                blocks.append(flip(b, ("row", "col"), (rows_n, cols_n), (step, 1)))
            far.append(blocks)
        tiles_2 = flip(kept_tiles, "col", (cols_n,), (1,))
        integrals_2 = flip(integrals, "col", (cols_n,), (1,))
        for b in others:
            near.append(flip(b, "col", (cols_n,), (1,)))

        bra, tile = integrals.shape[0], integrals.shape[0] // kept_tiles.shape[0]
        group = bra // chips

        def screened(values, tiles):
            keep = jnp.repeat(tiles.astype(jnp.bfloat16) * SCALE, tile, axis=1)
            values = values * jnp.repeat(keep, tile, axis=0)
            values = jnp.concatenate(
                [lax.dynamic_slice_in_dim(values, (chip ^ o) * group, group, 0) for o in range(chips)], 0
            )
            return [lax.dynamic_slice_in_dim(values, (row ^ s) * depth, depth, 1) for s in range(rows_n)]

        first, second = screened(integrals, kept_tiles), screened(integrals_2, tiles_2)
        left = [m for pairing in zip(first, second) for m in pairing]

        def dot(a, b):
            return jnp.dot(a, b, preferred_element_type=jnp.float32)

        early = []
        for a, b in zip(mine, near):
            early.append(dot(left[0], a) + dot(left[1], b))
        parts = []
        for i, blocks in enumerate(far):
            late = dot(jnp.concatenate(left[2:], 1), jnp.concatenate(blocks, 0))
            parts.append(early[i] + late)

        for i, part in enumerate(parts):
            total = part[:group]
            for step in z_order(chips):
                send = part[step * group : (step + 1) * group].astype(jnp.float16)
                got = flip(send, "col", (cols_n,), (2 * step,))
                total += got.astype(jnp.float32)
            parts[i] = total

        share = width // 2
        blocks = jnp.concatenate([t.astype(jnp.float16) for t in parts], 1)
        blocks = blocks.reshape(2, pair_n, own_rows, share)
        got = []
        for step in range(pair_n):
            sent = lax.dynamic_index_in_dim(blocks, pair ^ step, 1, False)
            got.append(sent if step == 0 else flip(sent, "pair", (pair_n,), (step,)))
        keep = [jnp.where(core == 0, g[0], g[1]) for g in got]
        send = jnp.stack([jnp.where(core == 0, g[1], g[0]) for g in got])
        back = flip(send, "col", (cols_n,), (1,))
        columns = []
        for i in range(pair_n):
            halves_of = []
            for first_half in (True, False):
                candidates = [jnp.where((core == 0) == first_half, keep[s], back[s]) for s in range(pair_n)]
                chosen = candidates[0]
                for s in range(1, pair_n):
                    chosen = jnp.where(pair == i ^ s, candidates[s], chosen)
                halves_of.append(chosen)
            for low, high in bounds:
                columns += [h[:, low // 2 : high // 2] for h in halves_of]
        ladder = jnp.concatenate(columns, 1).astype(jnp.float32)
        return update(ladder, driver, vir_energy, occ_energy, occ_coupling)

    return jax.shard_map(
        body,
        mesh=mesh,
        in_specs=(
            P("row", "col"),
            P("row", "col"),
            P(("col", "row"), "pair"),
            P(("row", "col", "pair"), None),
            P(("row", "col", "pair")),
            P(),
            P(),
        ),
        out_specs=P(("row", "col", "pair"), None),
        check_vma=False,
    )
```

profile of v0, /device:TPU:0, one launch (start us, length us, event | category | flops | bytes accessed | tf_op | source)
XLA Modules:
  0.0 35.0 jit_solution(2874063087628817297)
XLA Ops:
  0.0 1.1 %broadcast_select_fusion = (bf16[256,384]{1,0:T(8,128)(2,1)S(1)}, bf16[256,384]{1,0:T(8,128)(2,1)S(1)}) fusion(pred[]{:T(512)S(6)} %eq.9, bf16[256,768]{1,0:T(8,128)(2,1)} %param.9), kind=kLoop, calls=%fused_computation.19 | loop fusion | flops 196608 | bytes 786433 | tf_op jit(solution)/shard_map/jit(_where)/select_n | solution.py:47
  1.1 0.6 %collective-permute-start.2 = (bf16[256,384]{1,0:T(8,128)(2,1)S(1)}, bf16[256,384]{1,0:T(8,128)(2,1)S(1)}, u32[]{:S(2)}, u32[]{:S(2)}) collective-permute-start(bf16[256,384]{1,0:T(8,128)(2,1)S(1)} %get-tuple-element.19), channel_id=1, source_target_pairs={{0,2},{2,0},{4,6},{6,4},{8,10},{10,8},{12,14},{14,12},{1,3},{3,1},... | collective-permute-start | bytes 589832 | tf_op jit(solution)/shard_map/ppermute | solution.py:24
  1.6 2.6 %collective-permute-start.4 = (bf16[256,384]{1,0:T(8,128)(2,1)S(1)}, bf16[256,384]{1,0:T(8,128)(2,1)S(1)}, u32[]{:S(2)}, u32[]{:S(2)}) collective-permute-start(bf16[256,384]{1,0:T(8,128)(2,1)S(1)} %get-tuple-element.19), channel_id=1, source_target_pairs={{0,18},{2,16},{4,22},{6,20},{8,26},{10,24},{12,30},{14,28},{16,2},... | collective-permute-start | bytes 589832 | tf_op jit(solution)/shard_map/ppermute | solution.py:24
  4.2 0.1 collective-permute-start
  4.3 0.4 %collective-permute-start.1 = (s32[32,32]{1,0:T(8,128)}, s32[32,32]{1,0:T(8,128)S(1)}, u32[]{:S(2)}, u32[]{:S(2)}) collective-permute-start(s32[32,32]{1,0:T(8,128)} %param.8), channel_id=1, source_target_pairs={{0,2},{2,0},{4,6},{6,4},{8,10},{10,8},{12,14},{14,12},{1,3},{3,1},... | collective-permute-start | bytes 12296 | tf_op jit(solution)/shard_map/ppermute | solution.py:24
  4.7 0.0 collective-permute-start.3
  4.8 0.7 %convert_multiply_fusion.1 = bf16[32,32]{1,0:T(8,128)(2,1)S(1)} fusion(s32[32,32]{1,0:T(8,128)} %param.8), kind=kLoop, calls=%fused_computation.38 | loop fusion | flops 2048 | bytes 6144 | tf_op jit(solution)/shard_map/mul | solution.py:90
  5.5 0.1 copy.9
  5.6 0.1 copy.10
  5.7 1.1 %bitcast_multiply_fusion.1 = bf16[512,512]{1,0:T(8,128)(2,1)S(1)} fusion(bf16[512,512]{1,0:T(8,128)(2,1)} %param.7, bf16[32,512]{1,0:T(8,128)(2,1)S(1)} %copy.10), kind=kLoop, calls=%fused_computation.8 | loop fusion | flops 262144 | bytes 1081344 | tf_op jit(solution)/shard_map/mul | solution.py:91
  6.9 0.3 fusion.7
  7.3 0.1 copy.11
  7.4 0.1 copy.12
  7.5 0.1 bitcast_multiply_fusion
  7.5 0.0 copy-start.3
  7.7 0.3 convolution_add_fusion.1
  8.0 5.9 %collective-permute-done.3 = bf16[256,384]{1,0:T(8,128)(2,1)S(1)} collective-permute-done((bf16[256,384]{1,0:T(8,128)(2,1)S(1)}, bf16[256,384]{1,0:T(8,128)(2,1)S(1)}, u32[]{:S(2)}, u32[]{:S(2)}) %collective-permute-start.3) | collective-permute-done | bytes 196640 | tf_op jit(solution)/shard_map/ppermute | solution.py:24
  13.9 0.4 %fusion.16 = (f16[512,384]{1,0:T(8,128)(2,1)S(1)}, f32[512,384]{1,0:T(8,128)S(1)}) fusion(f32[512,384]{1,0:T(8,128)S(1)} %convolution_add_fusion.1, bf16[256,384]{1,0:T(8,128)(2,1)S(1)} %collective-permute-done.4, bf16[256,384]{1,0:T(8,128)(2,1)S(1)} %collective-permute-done.3, bf16[512,256]{1,0:T(8,128)(2,1)S(1)} %get-tuple-element.26, ...), kind=kOutput, calls=%fused_computation.53 | convolution fusion | flops 203554816 | bytes 2883584 | tf_op jit(solution)/shard_map/dot_general | solution.py:101
  14.3 0.1 fusion.15
  14.4 2.9 %collective-permute-start.5 = (f16[128,384]{1,0:T(8,128)(2,1)S(1)}, f16[128,384]{1,0:T(8,128)(2,1)S(1)}, u32[]{:S(2)}, u32[]{:S(2)}) collective-permute-start(f16[128,384]{1,0:T(8,128)(2,1)S(1)} %get-tuple-element.16), channel_id=1, source_target_pairs={{0,8},{2,10},{4,12},{6,14},{8,0},{10,2},{12,4},{14,6},{1,9},{3,11}... | collective-permute-start | bytes 294920 | tf_op jit(solution)/shard_map/ppermute | solution.py:24
  17.3 1.6 %collective-permute-start.6 = (f16[128,384]{1,0:T(8,128)(2,1)S(1)}, f16[128,384]{1,0:T(8,128)(2,1)S(1)}, u32[]{:S(2)}, u32[]{:S(2)}) collective-permute-start(f16[128,384]{1,0:T(8,128)(2,1)S(1)} %get-tuple-element.18), channel_id=1, source_target_pairs={{0,4},{2,6},{4,0},{6,2},{8,12},{10,14},{12,8},{14,10},{1,5},{3,7},... | collective-permute-start | bytes 294920 | tf_op jit(solution)/shard_map/ppermute | solution.py:24
  18.8 0.0 collective-permute-start.7
  18.9 4.5 %collective-permute-done.5 = f16[128,384]{1,0:T(8,128)(2,1)S(1)} collective-permute-done((f16[128,384]{1,0:T(8,128)(2,1)S(1)}, f16[128,384]{1,0:T(8,128)(2,1)S(1)}, u32[]{:S(2)}, u32[]{:S(2)}) %collective-permute-start.5) | collective-permute-done | bytes 98336 | tf_op jit(solution)/shard_map/ppermute | solution.py:24
  23.4 1.9 %collective-permute-done.7 = f16[128,384]{1,0:T(8,128)(2,1)S(1)} collective-permute-done((f16[128,384]{1,0:T(8,128)(2,1)S(1)}, f16[128,384]{1,0:T(8,128)(2,1)S(1)}, u32[]{:S(2)}, u32[]{:S(2)}) %collective-permute-start.7) | collective-permute-done | bytes 98336 | tf_op jit(solution)/shard_map/ppermute | solution.py:24
  25.3 0.1 fusion.11
  25.4 1.6 %collective-permute-start.8 = (f16[2,32,384]{2,1,0:T(8,128)(2,1)S(1)}, f16[2,32,384]{2,1,0:T(8,128)(2,1)S(1)}, u32[]{:S(2)}, u32[]{:S(2)}) collective-permute-start(f16[2,32,384]{2,1,0:T(8,128)(2,1)S(1)} %dynamic-slice_bitcast_fusion), channel_id=1, source_target_pairs={{0,1},{1,0},{2,3},{3,2},{4,5},{5,4},{6,7},{7,6},{8,9},{9,8},{10,11... | collective-permute-start | bytes 147464 | tf_op jit(solution)/shard_map/ppermute | solution.py:24
  27.0 2.6 %collective-permute-done.8 = f16[2,32,384]{2,1,0:T(8,128)(2,1)S(1)} collective-permute-done((f16[2,32,384]{2,1,0:T(8,128)(2,1)S(1)}, f16[2,32,384]{2,1,0:T(8,128)(2,1)S(1)}, u32[]{:S(2)}, u32[]{:S(2)}) %collective-permute-start.8) | collective-permute-done | bytes 49184 | tf_op jit(solution)/shard_map/ppermute | solution.py:24
  29.5 0.1 collective-permute-start.9
  29.6 0.1 copy.13.vir
  29.7 1.1 %collective-permute-done.9 = f16[2,32,384]{2,1,0:T(8,128)(2,1)S(1)} collective-permute-done((f16[2,32,384]{2,1,0:T(8,128)(2,1)S(1)}, f16[2,32,384]{2,1,0:T(8,128)(2,1)S(1)}, u32[]{:S(2)}, u32[]{:S(2)}) %collective-permute-start.9) | collective-permute-done | bytes 49184 | tf_op jit(solution)/shard_map/ppermute | solution.py:24
  31.0 2.3 %copy-done = bf16[1536,1536]{1,0:T(8,128)(2,1)S(1)} copy-done((bf16[1536,1536]{1,0:T(8,128)(2,1)S(1)}, bf16[1536,1536]{1,0:T(8,128)(2,1)}, u32[]{:S(2)}) %copy-start) | copy-done | bytes 4718616
  33.3 1.6 %update.1 = f32[32,1536]{1,0:T(8,128)} custom-call(f32[32,1536]{1,0:T(8,128)S(1)} %maximum_convert_fusion.ladder, bf16[32,1536]{1,0:T(8,128)(2,1)S(1)} %copy-done.1, f32[32,1]{1,0:T(8,128)S(1)} %copy.13.vir, f32[1,1536]{1,0:T(1,128)S(1)} %broadcast_in_dim.23.occ, bf16[1536,1536]{1,0:T(8,128)(2,1)S(1)} %copy-done), custom_call_target="tpu_custom_call" | custom-call | tf_op jit(solution)/shard_map/update/pallas_call | solution.py:37
  (27 shorter events, 0.5 us)
Async XLA Ops:
  1.1 6.6 %collective-permute-start.2 = (bf16[256,384]{1,0:T(8,128)(2,1)S(1)}, bf16[256,384]{1,0:T(8,128)(2,1)S(1)}, u32[]{:S(2)}, u32[]{:S(2)}) collective-permute-start(bf16[256,384]{1,0:T(8,128)(2,1)S(1)} %get-tuple-element.19), channel_id=1, source_target_pairs={{0,2},{2,0},{4,6},{6,4},{8,10},{10,8},{12,14},{14,12},{1,3},{3,1},... | collective-permute-start | bytes 589832 | tf_op jit(solution)/shard_map/ppermute | solution.py:24
  1.6 12.3 %collective-permute-start.4 = (bf16[256,384]{1,0:T(8,128)(2,1)S(1)}, bf16[256,384]{1,0:T(8,128)(2,1)S(1)}, u32[]{:S(2)}, u32[]{:S(2)}) collective-permute-start(bf16[256,384]{1,0:T(8,128)(2,1)S(1)} %get-tuple-element.19), channel_id=1, source_target_pairs={{0,18},{2,16},{4,22},{6,20},{8,26},{10,24},{12,30},{14,28},{16,2},... | collective-permute-start | bytes 589832 | tf_op jit(solution)/shard_map/ppermute | solution.py:24
  4.2 3.2 %collective-permute-start = (bf16[512,512]{1,0:T(8,128)(2,1)}, bf16[512,512]{1,0:T(8,128)(2,1)S(1)}, u32[]{:S(2)}, u32[]{:S(2)}) collective-permute-start(bf16[512,512]{1,0:T(8,128)(2,1)} %param.7), channel_id=1, source_target_pairs={{0,2},{2,0},{4,6},{6,4},{8,10},{10,8},{12,14},{14,12},{1,3},{3,1},... | collective-permute-start | bytes 1572872 | tf_op jit(solution)/shard_map/ppermute | solution.py:24
  4.3 2.9 %collective-permute-start.1 = (s32[32,32]{1,0:T(8,128)}, s32[32,32]{1,0:T(8,128)S(1)}, u32[]{:S(2)}, u32[]{:S(2)}) collective-permute-start(s32[32,32]{1,0:T(8,128)} %param.8), channel_id=1, source_target_pairs={{0,2},{2,0},{4,6},{6,4},{8,10},{10,8},{12,14},{14,12},{1,3},{3,1},... | collective-permute-start | bytes 12296 | tf_op jit(solution)/shard_map/ppermute | solution.py:24
  4.7 9.2 %collective-permute-start.3 = (bf16[256,384]{1,0:T(8,128)(2,1)S(1)}, bf16[256,384]{1,0:T(8,128)(2,1)S(1)}, u32[]{:S(2)}, u32[]{:S(2)}) collective-permute-start(bf16[256,384]{1,0:T(8,128)(2,1)S(1)} %get-tuple-element.20), channel_id=1, source_target_pairs={{0,16},{2,18},{4,20},{6,22},{8,24},{10,26},{12,28},{14,30},{16,0},... | collective-permute-start | bytes 589832 | tf_op jit(solution)/shard_map/ppermute | solution.py:24
  7.5 22.1 %copy-start.3 = (f32[32]{0:T(128)S(1)}, f32[32]{0:T(128)}, u32[]{:S(2)}) copy-start(f32[32]{0:T(128)} %param.11) | copy-start | bytes 388
  7.5 22.2 %copy-start.2 = (f32[1536]{0:T(1024)S(1)}, f32[1536]{0:T(1024)}, u32[]{:S(2)}) copy-start(f32[1536]{0:T(1024)} %param.12) | copy-start | bytes 18436
  7.6 23.4 %copy-start.1 = (bf16[32,1536]{1,0:T(8,128)(2,1)S(1)}, bf16[32,1536]{1,0:T(8,128)(2,1)}, u32[]{:S(2)}) copy-start(bf16[32,1536]{1,0:T(8,128)(2,1)} %driver.1) | copy-start | bytes 294916
  14.4 9.0 %collective-permute-start.5 = (f16[128,384]{1,0:T(8,128)(2,1)S(1)}, f16[128,384]{1,0:T(8,128)(2,1)S(1)}, u32[]{:S(2)}, u32[]{:S(2)}) collective-permute-start(f16[128,384]{1,0:T(8,128)(2,1)S(1)} %get-tuple-element.16), channel_id=1, source_target_pairs={{0,8},{2,10},{4,12},{6,14},{8,0},{10,2},{12,4},{14,6},{1,9},{3,11}... | collective-permute-start | bytes 294920 | tf_op jit(solution)/shard_map/ppermute | solution.py:24
  17.3 6.1 %collective-permute-start.6 = (f16[128,384]{1,0:T(8,128)(2,1)S(1)}, f16[128,384]{1,0:T(8,128)(2,1)S(1)}, u32[]{:S(2)}, u32[]{:S(2)}) collective-permute-start(f16[128,384]{1,0:T(8,128)(2,1)S(1)} %get-tuple-element.18), channel_id=1, source_target_pairs={{0,4},{2,6},{4,0},{6,2},{8,12},{10,14},{12,8},{14,10},{1,5},{3,7},... | collective-permute-start | bytes 294920 | tf_op jit(solution)/shard_map/ppermute | solution.py:24
  18.8 6.4 %collective-permute-start.7 = (f16[128,384]{1,0:T(8,128)(2,1)S(1)}, f16[128,384]{1,0:T(8,128)(2,1)S(1)}, u32[]{:S(2)}, u32[]{:S(2)}) collective-permute-start(f16[128,384]{1,0:T(8,128)(2,1)S(1)} %get-tuple-element.17), channel_id=1, source_target_pairs={{0,12},{2,14},{4,8},{6,10},{8,4},{10,6},{12,0},{14,2},{1,13},{3,15... | collective-permute-start | bytes 294920 | tf_op jit(solution)/shard_map/ppermute | solution.py:24
  25.4 4.2 %collective-permute-start.8 = (f16[2,32,384]{2,1,0:T(8,128)(2,1)S(1)}, f16[2,32,384]{2,1,0:T(8,128)(2,1)S(1)}, u32[]{:S(2)}, u32[]{:S(2)}) collective-permute-start(f16[2,32,384]{2,1,0:T(8,128)(2,1)S(1)} %dynamic-slice_bitcast_fusion), channel_id=1, source_target_pairs={{0,1},{1,0},{2,3},{3,2},{4,5},{5,4},{6,7},{7,6},{8,9},{9,8},{10,11... | collective-permute-start | bytes 147464 | tf_op jit(solution)/shard_map/ppermute | solution.py:24
  29.5 1.3 %collective-permute-start.9 = (f16[2,32,384]{2,1,0:T(8,128)(2,1)S(1)}, f16[2,32,384]{2,1,0:T(8,128)(2,1)S(1)}, u32[]{:S(2)}, u32[]{:S(2)}) collective-permute-start(f16[2,32,384]{2,1,0:T(8,128)(2,1)S(1)} %pad_maximum_fusion.2), channel_id=1, source_target_pairs={{0,2},{2,0},{4,6},{6,4},{8,10},{10,8},{12,14},{14,12},{1,3},{3,1},... | collective-permute-start | bytes 147464 | tf_op jit(solution)/shard_map/ppermute | solution.py:24
  31.0 2.3 %copy-start = (bf16[1536,1536]{1,0:T(8,128)(2,1)S(1)}, bf16[1536,1536]{1,0:T(8,128)(2,1)}, u32[]{:S(2)}) copy-start(bf16[1536,1536]{1,0:T(8,128)(2,1)} %coupling.1) | copy-start | bytes 14155780
where the time goes:
time: 35.2 us; the launch traced here: 35 us
  waiting for transfers between devices  15.9 us (45%)
  starting transfers between devices  9.81 us (28%)
  other arithmetic  3.2 us (9%)
  local copies, waits for them, and re-layouts  3.04 us (9%)
  Pallas kernels  1.65 us (5%)
  matrix products  1.03 us (3%)
    ppermute x10, waiting for transfers between devices, flip(): return lax.ppermute(value, axes, pairs)  15.9 us
    ppermute x10, starting transfers between devices, flip(): return lax.ppermute(value, axes, pairs)  9.81 us
    unnamed x8, local copies, waits for them, and re-layouts  2.35 us
    pallas_call x1, Pallas kernels, update(): pl.pallas_call(update_kernel, out_shape=jax.ShapeDtypeStruct((rows, colum...  1.65 us
    mul x2, other arithmetic, screened(): values = values * jnp.repeat(keep, tile, axis=0)  1.14 us
    select_n x1, other arithmetic, halves(): return (jnp.where(bit == 0, low, high), jnp.where(bit == 0, high, low))  1.06 us
    dot_general x3, matrix products, dot(): return jnp.dot(a, b, preferred_element_type=jnp.float32)  1.03 us
    mul x2, other arithmetic, screened(): keep = jnp.repeat(tiles.astype(jnp.bfloat16) * SCALE, tile, axis=1)  0.73 us
  transfers between devices with their start and end apart: 10, of which 5 were waited for; matrix products, arithmetic and copies ran while one was open for 9% of the time, Pallas kernels for 0%

commit v1 on v0

--- a/solution.py
+++ b/solution.py
@@ -25,7 +25,10 @@
 
 
 def update_kernel(ladder, driver, vir, occ, coupling, out):
-    denom = vir[...] - occ[...]
+    count = vir.shape[1]
+    diagonal = lax.broadcasted_iota(jnp.int32, (count, count), 0) == lax.broadcasted_iota(jnp.int32, (count, count), 1)
+    tall = jnp.sum(jnp.where(diagonal, vir[...], 0.0), axis=1, keepdims=True)
+    denom = tall - occ[...]
     residual = driver[...].astype(jnp.float32) + ladder[...] * (1 / SCALE)
     scaled = (residual / denom).astype(jnp.bfloat16)
     coupled = jnp.dot(scaled, coupling[...], preferred_element_type=jnp.float32)
@@ -39,12 +42,19 @@
         out_shape=jax.ShapeDtypeStruct((rows, columns), jnp.float32),
         compiler_params=pltpu.CompilerParams(vmem_limit_bytes=16 * 2**20),
         name="update",
-    )(ladder, driver, vir_energy[:, None], occ_energy[None, :], occ_coupling)
+    )(ladder, driver, vir_energy[None, :], occ_energy[None, :], occ_coupling)
 
 
-def halves(value, bit, axis):
+def halves(value, first, axis):
     low, high = jnp.split(value, 2, axis)
-    return jnp.where(bit == 0, low, high), jnp.where(bit == 0, high, low)
+    return jnp.where(first, low, high), jnp.where(first, high, low)
+
+
+def pick(at, options):
+    chosen = options[0]
+    for here, option in zip(at[1:], options[1:]):
+        chosen = jnp.where(here, option, chosen)
+    return chosen
 
 
 def chunk_bounds(columns):
@@ -66,11 +76,14 @@
         own_rows = driver.shape[0]
         bounds = chunk_bounds(width)
 
+        first_core = core == 0
+        at_pair = [pair == i for i in range(pair_n)]
         mine, others = [], []
         for low, high in bounds:
-            a, b = halves(amplitudes[:, low:high], core, 1)
+            a, b = halves(amplitudes[:, low:high], first_core, 1)
             mine.append(a)
             others.append(b)
+        mine, others, first_core, at_pair = lax.optimization_barrier((mine, others, first_core, at_pair))
         far, near = [], []
         for a, b in zip(mine, others):
             blocks = []
@@ -121,22 +134,18 @@
         blocks = blocks.reshape(2, pair_n, own_rows, share)
         got = []
         for step in range(pair_n):
-            sent = lax.dynamic_index_in_dim(blocks, pair ^ step, 1, False)
+            sent = pick(at_pair, [blocks[:, i ^ step] for i in range(pair_n)])
             got.append(sent if step == 0 else flip(sent, "pair", (pair_n,), (step,)))
-        keep = [jnp.where(core == 0, g[0], g[1]) for g in got]
-        send = jnp.stack([jnp.where(core == 0, g[1], g[0]) for g in got])
+        keep = [jnp.where(first_core, g[0], g[1]) for g in got]
+        send = jnp.stack([jnp.where(first_core, g[1], g[0]) for g in got])
         back = flip(send, "col", (cols_n,), (1,))
         columns = []
         for i in range(pair_n):
-            halves_of = []
-            for first_half in (True, False):
-                candidates = [jnp.where((core == 0) == first_half, keep[s], back[s]) for s in range(pair_n)]
-                chosen = candidates[0]
-                for s in range(1, pair_n):
-                    chosen = jnp.where(pair == i ^ s, candidates[s], chosen)
-                halves_of.append(chosen)
+            low_core = [jnp.where(first_core, keep[s], back[s]) for s in range(pair_n)]
+            high_core = [jnp.where(first_core, back[s], keep[s]) for s in range(pair_n)]
+            both = [pick(at_pair, [c[i ^ p] for p in range(pair_n)]) for c in (low_core, high_core)]
             for low, high in bounds:
-                columns += [h[:, low // 2 : high // 2] for h in halves_of]
+                columns += [h[:, low // 2 : high // 2] for h in both]
         ladder = jnp.concatenate(columns, 1).astype(jnp.float32)
         return update(ladder, driver, vir_energy, occ_energy, occ_coupling)
 

time: 35.2 us -> 32.9 us (0.935)
  local copies, waits for them, and re-layouts: 3.04 us -> 0.62 us
    unnamed x8 -> x10, local copies, waits for them, and re-layouts: 2.35 us -> 0.03 us
    select_n x5 -> x6, other arithmetic: 1.16 us -> 1.18 us  [the longest x1 1.06 us: halves(): return (jnp.where(first, low, high), jnp.where(first, high, low))]
where the time goes in v1:
time: 32.9 us; the launch traced here: 32.7 us
  waiting for transfers between devices  16 us (49%)
  starting transfers between devices  9.81 us (30%)
  other arithmetic  3.22 us (10%)
  Pallas kernels  1.66 us (5%)
  matrix products  1.04 us (3%)
  local copies, waits for them, and re-layouts  0.62 us (2%)
  between operations  0.33 us (1%)
    ppermute x10, waiting for transfers between devices, flip(): return lax.ppermute(value, axes, pairs)  16 us
    ppermute x10, starting transfers between devices, flip(): return lax.ppermute(value, axes, pairs)  9.81 us
    pallas_call x1, Pallas kernels, update(): pl.pallas_call(update_kernel, out_shape=jax.ShapeDtypeStruct((rows, colum...  1.66 us
    mul x2, other arithmetic, screened(): values = values * jnp.repeat(keep, tile, axis=0)  1.14 us
    select_n x1, other arithmetic, halves(): return (jnp.where(first, low, high), jnp.where(first, high, low))  1.06 us
    dot_general x3, matrix products, dot(): return jnp.dot(a, b, preferred_element_type=jnp.float32)  1.04 us
    mul x2, other arithmetic, screened(): keep = jnp.repeat(tiles.astype(jnp.bfloat16) * SCALE, tile, axis=1)  0.73 us
  transfers between devices with their start and end apart: 10, of which 5 were waited for; matrix products, arithmetic and copies ran while one was open for 9% of the time, Pallas kernels for 0%

profile of v1, /device:TPU:0, one launch (start us, length us, event | category | flops | bytes accessed | tf_op | source)
XLA Modules:
  0.0 32.7 jit_solution(16598482299182645126)
XLA Ops:
  0.0 1.1 %broadcast_select_fusion = (bf16[256,384]{1,0:T(8,128)(2,1)S(1)}, bf16[256,384]{1,0:T(8,128)(2,1)S(1)}) fusion(pred[]{:T(512)S(6)} %eq.7, bf16[256,768]{1,0:T(8,128)(2,1)} %param.9), kind=kLoop, calls=%fused_computation.19 | loop fusion | flops 196608 | bytes 786433 | tf_op jit(solution)/shard_map/jit(_where)/select_n | solution.py:50
  1.1 0.6 %collective-permute-start.2 = (bf16[256,384]{1,0:T(8,128)(2,1)S(1)}, bf16[256,384]{1,0:T(8,128)(2,1)S(1)}, u32[]{:S(2)}, u32[]{:S(2)}) collective-permute-start(bf16[256,384]{1,0:T(8,128)(2,1)S(1)} %get-tuple-element.12), channel_id=1, source_target_pairs={{0,2},{2,0},{4,6},{6,4},{8,10},{10,8},{12,14},{14,12},{1,3},{3,1},... | collective-permute-start | bytes 589832 | tf_op jit(solution)/shard_map/ppermute | solution.py:24
  1.6 2.6 %collective-permute-start.4 = (bf16[256,384]{1,0:T(8,128)(2,1)S(1)}, bf16[256,384]{1,0:T(8,128)(2,1)S(1)}, u32[]{:S(2)}, u32[]{:S(2)}) collective-permute-start(bf16[256,384]{1,0:T(8,128)(2,1)S(1)} %get-tuple-element.12), channel_id=1, source_target_pairs={{0,18},{2,16},{4,22},{6,20},{8,26},{10,24},{12,30},{14,28},{16,2},... | collective-permute-start | bytes 589832 | tf_op jit(solution)/shard_map/ppermute | solution.py:24
  4.2 0.1 collective-permute-start
  4.3 0.4 %collective-permute-start.1 = (s32[32,32]{1,0:T(8,128)}, s32[32,32]{1,0:T(8,128)S(1)}, u32[]{:S(2)}, u32[]{:S(2)}) collective-permute-start(s32[32,32]{1,0:T(8,128)} %param.8), channel_id=1, source_target_pairs={{0,2},{2,0},{4,6},{6,4},{8,10},{10,8},{12,14},{14,12},{1,3},{3,1},... | collective-permute-start | bytes 12296 | tf_op jit(solution)/shard_map/ppermute | solution.py:24
  4.7 0.0 collective-permute-start.3
  4.8 0.7 %convert_multiply_fusion.1 = bf16[32,32]{1,0:T(8,128)(2,1)S(1)} fusion(s32[32,32]{1,0:T(8,128)} %param.8), kind=kLoop, calls=%fused_computation.40 | loop fusion | flops 2048 | bytes 6144 | tf_op jit(solution)/shard_map/mul | solution.py:103
  5.5 0.1 copy.8
  5.6 0.1 copy.9
  5.7 1.1 %bitcast_multiply_fusion.1 = bf16[512,512]{1,0:T(8,128)(2,1)S(1)} fusion(bf16[512,512]{1,0:T(8,128)(2,1)} %param.7, bf16[32,512]{1,0:T(8,128)(2,1)S(1)} %copy.9), kind=kLoop, calls=%fused_computation.8 | loop fusion | flops 262144 | bytes 1081344 | tf_op jit(solution)/shard_map/mul | solution.py:104
  6.9 0.0 slice-start
  6.9 0.3 fusion.7
  7.3 0.1 copy.10
  7.4 0.1 copy.11
  7.5 0.1 bitcast_multiply_fusion
  7.6 0.0 copy-start.1
  7.7 0.0 slice-start.1
  7.7 0.3 convolution_add_fusion.1
  8.1 5.8 %collective-permute-done.3 = bf16[256,384]{1,0:T(8,128)(2,1)S(1)} collective-permute-done((bf16[256,384]{1,0:T(8,128)(2,1)S(1)}, bf16[256,384]{1,0:T(8,128)(2,1)S(1)}, u32[]{:S(2)}, u32[]{:S(2)}) %collective-permute-start.3) | collective-permute-done | bytes 196640 | tf_op jit(solution)/shard_map/ppermute | solution.py:24
  13.9 0.4 %fusion.16 = (f16[512,384]{1,0:T(8,128)(2,1)S(1)}, f32[512,384]{1,0:T(8,128)S(1)}) fusion(f32[512,384]{1,0:T(8,128)S(1)} %convolution_add_fusion.1, bf16[256,384]{1,0:T(8,128)(2,1)S(1)} %collective-permute-done.4, bf16[256,384]{1,0:T(8,128)(2,1)S(1)} %collective-permute-done.3, bf16[512,256]{1,0:T(8,128)(2,1)S(1)} %get-tuple-element.36, ...), kind=kOutput, calls=%fused_computation.55 | convolution fusion | flops 203554816 | bytes 2883584 | tf_op jit(solution)/shard_map/dot_general | solution.py:114
  14.3 0.1 fusion.15
  14.4 2.9 %collective-permute-start.5 = (f16[128,384]{1,0:T(8,128)(2,1)S(1)}, f16[128,384]{1,0:T(8,128)(2,1)S(1)}, u32[]{:S(2)}, u32[]{:S(2)}) collective-permute-start(f16[128,384]{1,0:T(8,128)(2,1)S(1)} %get-tuple-element.24), channel_id=1, source_target_pairs={{0,8},{2,10},{4,12},{6,14},{8,0},{10,2},{12,4},{14,6},{1,9},{3,11}... | collective-permute-start | bytes 294920 | tf_op jit(solution)/shard_map/ppermute | solution.py:24
  17.3 1.6 %collective-permute-start.6 = (f16[128,384]{1,0:T(8,128)(2,1)S(1)}, f16[128,384]{1,0:T(8,128)(2,1)S(1)}, u32[]{:S(2)}, u32[]{:S(2)}) collective-permute-start(f16[128,384]{1,0:T(8,128)(2,1)S(1)} %get-tuple-element.26), channel_id=1, source_target_pairs={{0,4},{2,6},{4,0},{6,2},{8,12},{10,14},{12,8},{14,10},{1,5},{3,7},... | collective-permute-start | bytes 294920 | tf_op jit(solution)/shard_map/ppermute | solution.py:24
  18.8 0.0 collective-permute-start.7
  18.9 4.5 %collective-permute-done.5 = f16[128,384]{1,0:T(8,128)(2,1)S(1)} collective-permute-done((f16[128,384]{1,0:T(8,128)(2,1)S(1)}, f16[128,384]{1,0:T(8,128)(2,1)S(1)}, u32[]{:S(2)}, u32[]{:S(2)}) %collective-permute-start.5) | collective-permute-done | bytes 98336 | tf_op jit(solution)/shard_map/ppermute | solution.py:24
  23.4 1.9 %collective-permute-done.7 = f16[128,384]{1,0:T(8,128)(2,1)S(1)} collective-permute-done((f16[128,384]{1,0:T(8,128)(2,1)S(1)}, f16[128,384]{1,0:T(8,128)(2,1)S(1)}, u32[]{:S(2)}, u32[]{:S(2)}) %collective-permute-start.7) | collective-permute-done | bytes 98336 | tf_op jit(solution)/shard_map/ppermute | solution.py:24
  25.3 0.1 fusion.11
  25.4 1.6 %collective-permute-start.8 = (f16[2,32,384]{2,1,0:T(8,128)(2,1)S(1)}, f16[2,32,384]{2,1,0:T(8,128)(2,1)S(1)}, u32[]{:S(2)}, u32[]{:S(2)}) collective-permute-start(f16[2,32,384]{2,1,0:T(8,128)(2,1)S(1)} %get-tuple-element.33), channel_id=1, source_target_pairs={{0,1},{1,0},{2,3},{3,2},{4,5},{5,4},{6,7},{7,6},{8,9},{9,8},{10,11... | collective-permute-start | bytes 147464 | tf_op jit(solution)/shard_map/ppermute | solution.py:24
  27.0 2.6 %collective-permute-done.8 = f16[2,32,384]{2,1,0:T(8,128)(2,1)S(1)} collective-permute-done((f16[2,32,384]{2,1,0:T(8,128)(2,1)S(1)}, f16[2,32,384]{2,1,0:T(8,128)(2,1)S(1)}, u32[]{:S(2)}, u32[]{:S(2)}) %collective-permute-start.8) | collective-permute-done | bytes 49184 | tf_op jit(solution)/shard_map/ppermute | solution.py:24
  29.6 0.1 collective-permute-start.9
  29.7 1.2 %collective-permute-done.9 = f16[2,32,384]{2,1,0:T(8,128)(2,1)S(1)} collective-permute-done((f16[2,32,384]{2,1,0:T(8,128)(2,1)S(1)}, f16[2,32,384]{2,1,0:T(8,128)(2,1)S(1)}, u32[]{:S(2)}, u32[]{:S(2)}) %collective-permute-start.9) | collective-permute-done | bytes 49184 | tf_op jit(solution)/shard_map/ppermute | solution.py:24
  31.0 1.7 %update.1 = f32[32,1536]{1,0:T(8,128)} custom-call(f32[32,1536]{1,0:T(8,128)S(1)} %maximum_convert_fusion.ladder, bf16[32,1536]{1,0:T(8,128)(2,1)S(1)} %copy-done, f32[1,32]{1,0:T(1,128)S(1)} %bitcast.47, f32[1,1536]{1,0:T(1,128)S(1)} %broadcast_in_dim.23.occ, bf16[1536,1536]{1,0:T(8,128)(2,1)S(1)} %bitcast.46), custom_call_target="tpu_custom_call" | custom-call | tf_op jit(solution)/shard_map/update/pallas_call | solution.py:40
  (29 shorter events, 0.5 us)
Async XLA Ops:
  1.1 6.6 %collective-permute-start.2 = (bf16[256,384]{1,0:T(8,128)(2,1)S(1)}, bf16[256,384]{1,0:T(8,128)(2,1)S(1)}, u32[]{:S(2)}, u32[]{:S(2)}) collective-permute-start(bf16[256,384]{1,0:T(8,128)(2,1)S(1)} %get-tuple-element.12), channel_id=1, source_target_pairs={{0,2},{2,0},{4,6},{6,4},{8,10},{10,8},{12,14},{14,12},{1,3},{3,1},... | collective-permute-start | bytes 589832 | tf_op jit(solution)/shard_map/ppermute | solution.py:24
  1.6 12.3 %collective-permute-start.4 = (bf16[256,384]{1,0:T(8,128)(2,1)S(1)}, bf16[256,384]{1,0:T(8,128)(2,1)S(1)}, u32[]{:S(2)}, u32[]{:S(2)}) collective-permute-start(bf16[256,384]{1,0:T(8,128)(2,1)S(1)} %get-tuple-element.12), channel_id=1, source_target_pairs={{0,18},{2,16},{4,22},{6,20},{8,26},{10,24},{12,30},{14,28},{16,2},... | collective-permute-start | bytes 589832 | tf_op jit(solution)/shard_map/ppermute | solution.py:24
  4.2 3.3 %collective-permute-start = (bf16[512,512]{1,0:T(8,128)(2,1)}, bf16[512,512]{1,0:T(8,128)(2,1)S(1)}, u32[]{:S(2)}, u32[]{:S(2)}) collective-permute-start(bf16[512,512]{1,0:T(8,128)(2,1)} %param.7), channel_id=1, source_target_pairs={{0,2},{2,0},{4,6},{6,4},{8,10},{10,8},{12,14},{14,12},{1,3},{3,1},... | collective-permute-start | bytes 1572872 | tf_op jit(solution)/shard_map/ppermute | solution.py:24
  4.3 3.0 %collective-permute-start.1 = (s32[32,32]{1,0:T(8,128)}, s32[32,32]{1,0:T(8,128)S(1)}, u32[]{:S(2)}, u32[]{:S(2)}) collective-permute-start(s32[32,32]{1,0:T(8,128)} %param.8), channel_id=1, source_target_pairs={{0,2},{2,0},{4,6},{6,4},{8,10},{10,8},{12,14},{14,12},{1,3},{3,1},... | collective-permute-start | bytes 12296 | tf_op jit(solution)/shard_map/ppermute | solution.py:24
  4.7 9.2 %collective-permute-start.3 = (bf16[256,384]{1,0:T(8,128)(2,1)S(1)}, bf16[256,384]{1,0:T(8,128)(2,1)S(1)}, u32[]{:S(2)}, u32[]{:S(2)}) collective-permute-start(bf16[256,384]{1,0:T(8,128)(2,1)S(1)} %get-tuple-element.11), channel_id=1, source_target_pairs={{0,16},{2,18},{4,20},{6,22},{8,24},{10,26},{12,28},{14,30},{16,0},... | collective-permute-start | bytes 589832 | tf_op jit(solution)/shard_map/ppermute | solution.py:24
  6.9 24.0 %slice-start = ((s8[4718592]{0:T(1024)(128)(4,1)}), s8[524288]{0:T(1024)(128)(4,1)S(1)}, s32[]{:S(2)}) async-start(s8[4718592]{0:T(1024)(128)(4,1)} %bitcast.45), calls=%async_computation | async-start | bytes 1048576
  7.5 22.1 %copy-start.2 = (f32[1536]{0:T(1024)S(1)}, f32[1536]{0:T(1024)}, u32[]{:S(2)}) copy-start(f32[1536]{0:T(1024)} %param.12) | copy-start | bytes 18436
  7.6 23.4 %copy-start = (bf16[32,1536]{1,0:T(8,128)(2,1)S(1)}, bf16[32,1536]{1,0:T(8,128)(2,1)}, u32[]{:S(2)}) copy-start(bf16[32,1536]{1,0:T(8,128)(2,1)} %driver.1) | copy-start | bytes 294916
  7.6 23.4 %copy-start.1 = (f32[32]{0:T(128)S(1)}, f32[32]{0:T(128)}, u32[]{:S(2)}) copy-start(f32[32]{0:T(128)} %param.11) | copy-start | bytes 388
  7.7 23.3 %slice-start.1 = ((s8[4718592]{0:T(1024)(128)(4,1)}), s8[4194304]{0:T(1024)(128)(4,1)S(1)}, s32[]{:S(2)}) async-start(s8[4718592]{0:T(1024)(128)(4,1)} %bitcast.45), calls=%async_computation.1 | async-start | bytes 8388608
  14.4 9.0 %collective-permute-start.5 = (f16[128,384]{1,0:T(8,128)(2,1)S(1)}, f16[128,384]{1,0:T(8,128)(2,1)S(1)}, u32[]{:S(2)}, u32[]{:S(2)}) collective-permute-start(f16[128,384]{1,0:T(8,128)(2,1)S(1)} %get-tuple-element.24), channel_id=1, source_target_pairs={{0,8},{2,10},{4,12},{6,14},{8,0},{10,2},{12,4},{14,6},{1,9},{3,11}... | collective-permute-start | bytes 294920 | tf_op jit(solution)/shard_map/ppermute | solution.py:24
  17.3 6.1 %collective-permute-start.6 = (f16[128,384]{1,0:T(8,128)(2,1)S(1)}, f16[128,384]{1,0:T(8,128)(2,1)S(1)}, u32[]{:S(2)}, u32[]{:S(2)}) collective-permute-start(f16[128,384]{1,0:T(8,128)(2,1)S(1)} %get-tuple-element.26), channel_id=1, source_target_pairs={{0,4},{2,6},{4,0},{6,2},{8,12},{10,14},{12,8},{14,10},{1,5},{3,7},... | collective-permute-start | bytes 294920 | tf_op jit(solution)/shard_map/ppermute | solution.py:24
  18.8 6.4 %collective-permute-start.7 = (f16[128,384]{1,0:T(8,128)(2,1)S(1)}, f16[128,384]{1,0:T(8,128)(2,1)S(1)}, u32[]{:S(2)}, u32[]{:S(2)}) collective-permute-start(f16[128,384]{1,0:T(8,128)(2,1)S(1)} %get-tuple-element.25), channel_id=1, source_target_pairs={{0,12},{2,14},{4,8},{6,10},{8,4},{10,6},{12,0},{14,2},{1,13},{3,15... | collective-permute-start | bytes 294920 | tf_op jit(solution)/shard_map/ppermute | solution.py:24
  25.4 4.2 %collective-permute-start.8 = (f16[2,32,384]{2,1,0:T(8,128)(2,1)S(1)}, f16[2,32,384]{2,1,0:T(8,128)(2,1)S(1)}, u32[]{:S(2)}, u32[]{:S(2)}) collective-permute-start(f16[2,32,384]{2,1,0:T(8,128)(2,1)S(1)} %get-tuple-element.33), channel_id=1, source_target_pairs={{0,1},{1,0},{2,3},{3,2},{4,5},{5,4},{6,7},{7,6},{8,9},{9,8},{10,11... | collective-permute-start | bytes 147464 | tf_op jit(solution)/shard_map/ppermute | solution.py:24
  29.6 1.3 %collective-permute-start.9 = (f16[2,32,384]{2,1,0:T(8,128)(2,1)S(1)}, f16[2,32,384]{2,1,0:T(8,128)(2,1)S(1)}, u32[]{:S(2)}, u32[]{:S(2)}) collective-permute-start(f16[2,32,384]{2,1,0:T(8,128)(2,1)S(1)} %pad_maximum_fusion.2), channel_id=1, source_target_pairs={{0,2},{2,0},{4,6},{6,4},{8,10},{10,8},{12,14},{14,12},{1,3},{3,1},... | collective-permute-start | bytes 147464 | tf_op jit(solution)/shard_map/ppermute | solution.py:24

commit v2 on v1

v2 whole, which is shorter than its diff:
```python
import functools

import jax
import jax.numpy as jnp
from jax import lax
from jax.experimental.layout import Layout, with_layout_constraint
from jax.experimental import pallas as pl
from jax.experimental.pallas import tpu as pltpu
from jax.sharding import PartitionSpec as P


LANES = 128
SCALE = 8.0


def flip(value, axes, sizes, steps):
    pairs = []
    total = 1
    for size in sizes:
        total *= size
    for source in range(total):
        rest, target, scale = source, 0, 1
        for size, step in zip(reversed(sizes), reversed(steps)):
            target += ((rest % size) ^ step) * scale
            rest //= size
            scale *= size
        pairs.append((source, target))
    return lax.ppermute(value, axes, pairs)


def tall(row):
    count = row.shape[1]
    diagonal = lax.broadcasted_iota(jnp.int32, (count, count), 0) == lax.broadcasted_iota(jnp.int32, (count, count), 1)
    return jnp.sum(jnp.where(diagonal, row[...], 0.0), axis=1, keepdims=True)


def spans(side, share, count):
    return [pl.ds(pl.multiple_of((2 * i + side) * share, LANES), share) for i in range(count)]


def terms(ladder, driver, vir, occ, span, i, share):
    denom = vir - occ[:, span]
    residual = driver[:, span].astype(jnp.float32) + ladder[:, i * share : (i + 1) * share] * (1 / SCALE)
    return residual, denom


def couple(ladder, driver, vir, occ, coupling, columns):
    total, share = None, ladder.shape[1] // len(columns)
    for i, span in enumerate(columns):
        residual, denom = terms(ladder, driver, vir, occ, span, i, share)
        scaled = (residual / denom).astype(jnp.bfloat16)
        product = jnp.dot(scaled, coupling[span, :], preferred_element_type=jnp.float32)
        total = product if total is None else total + product
    return total


def begin_kernel(share, ladder, driver, vir, occ, coupling, out):
    core = lax.axis_index("col") & 1
    columns = spans(core, share, ladder.shape[1] // share)
    out[...] = couple(ladder, driver, tall(vir), occ, coupling, columns)


def finish_kernel(share, mine, others, driver, vir, occ, coupling, begun, out, coupled):
    core = lax.axis_index("col") & 1
    count = mine.shape[1] // share
    here, there = spans(core, share, count), spans(1 - core, share, count)
    column = tall(vir)
    coupled[...] = begun[...] + couple(others, driver, column, occ, coupling, there)
    for ladder, columns in ((mine, here), (others, there)):
        for i, span in enumerate(columns):
            residual, denom = terms(ladder, driver, column, occ, span, i, share)
            out[:, span] = -(residual - coupled[:, span]) / denom


def update_call(kernel, rows, columns, scratch, *args):
    return pl.pallas_call(
        kernel,
        out_shape=jax.ShapeDtypeStruct((rows, columns), jnp.float32),
        scratch_shapes=scratch,
        compiler_params=pltpu.CompilerParams(vmem_limit_bytes=16 * 2**20),
    )(*args)


def fetch_kernel(share, bounds, whole, *refs):
    count = 2 * len(bounds)
    extra = (len(refs) - 1 - count) // 2
    others, outs, sems = refs[:extra], refs[extra:-1], refs[-1]
    core = lax.axis_index("col") & 1
    sources = []
    for low, high in bounds:
        for side in (core, 1 - core):
            start = pl.multiple_of(side * share + low, LANES)
            sources.append(whole.at[:, pl.ds(start, high - low)])
    sources += others
    copies = [pltpu.make_async_copy(source, out, sems.at[i]) for i, (source, out) in enumerate(zip(sources, outs))]
    for copy in copies:
        copy.start()
    for copy in copies:
        copy.wait()


def fetch(value, bounds, *others):
    rows, columns = value.shape
    shapes = [pltpu.VMEM((rows, high - low), value.dtype) for low, high in bounds for _ in range(2)]
    shapes += [pltpu.VMEM(o.shape, o.dtype) for o in others]
    outs = pl.pallas_call(
        functools.partial(fetch_kernel, columns // 2, bounds),
        out_shape=shapes,
        in_specs=[pl.BlockSpec(memory_space=pltpu.HBM)] * (1 + len(others)),
        out_specs=[pl.BlockSpec(memory_space=pltpu.VMEM)] * len(shapes),
        scratch_shapes=[pltpu.SemaphoreType.DMA((len(shapes),))],
        compiler_params=pltpu.CompilerParams(vmem_limit_bytes=4 * 2**20),
        name="fetch",
    )(*[pltpu.with_memory_space_constraint(v, pltpu.HBM) for v in (value, *others)])
    count = 2 * len(bounds)
    return outs[0:count:2], outs[1:count:2]


def pick(at, options):
    chosen = options[0]
    for here, option in zip(at[1:], options[1:]):
        chosen = jnp.where(here, option, chosen)
    return chosen


FIRST = 2
EARLY = "21"
REST = ((2, 1), (3, None), (1, 1))


def chunk_bounds(share):
    first = FIRST * LANES
    return [(0, first), (first, share)] if first < share else [(0, share)]


def sends(chips, chunks):
    if chips == 4 and chunks == 2:
        return [(int(e), 0) for e in EARLY] + list(REST)
    steps = sorted(range(1, chips), key=lambda s: (s != chips // 2, s))
    return [(s, None) for s in steps]


def solution(mesh):
    rows_n, cols_n, pair_n = mesh.shape["row"], mesh.shape["col"], mesh.shape["pair"]
    chips = cols_n // 2

    def body(integrals, kept_tiles, amplitudes, driver, vir_energy, occ_energy, occ_coupling):
        row, col, pair = (lax.axis_index(a) for a in ("row", "col", "pair"))
        core, chip = col & 1, col >> 1
        depth, width = amplitudes.shape
        own_rows = driver.shape[0]
        share = width // 2
        bounds = chunk_bounds(share)

        first_core = core == 0
        at_pair = [pair == i for i in range(pair_n)]
        mine, others = fetch(amplitudes, bounds)
        mine, others, first_core, at_pair = lax.optimization_barrier((list(mine), list(others), first_core, at_pair))
        far, near = [], []
        for a, b in zip(mine, others):
            blocks = []
            for step in range(1, rows_n):
                blocks.append(flip(a, ("row", "col"), (rows_n, cols_n), (step, 0)))
                blocks.append(flip(b, ("row", "col"), (rows_n, cols_n), (step, 1)))
            far.append(blocks)
        tiles_2 = flip(kept_tiles, "col", (cols_n,), (1,))
        integrals_2 = flip(integrals, "col", (cols_n,), (1,))
        for b in others:
            near.append(flip(b, "col", (cols_n,), (1,)))

        bra, tile = integrals.shape[0], integrals.shape[0] // kept_tiles.shape[0]
        group = bra // chips

        def screened(values, tiles):
            keep = jnp.repeat(tiles.astype(jnp.bfloat16) * SCALE, tile, axis=1)
            values = values * jnp.repeat(keep, tile, axis=0)
            values = jnp.concatenate(
                [lax.dynamic_slice_in_dim(values, (chip ^ o) * group, group, 0) for o in range(chips)], 0
            )
            return [lax.dynamic_slice_in_dim(values, (row ^ s) * depth, depth, 1) for s in range(rows_n)]

        first, second = screened(integrals, kept_tiles), screened(integrals_2, tiles_2)
        left = [m for pairing in zip(first, second) for m in pairing]

        def dot(a, b):
            return with_layout_constraint(jnp.dot(a, b, preferred_element_type=jnp.float32), Layout((0, 1)))

        early = []
        for a, b in zip(mine, near):
            early.append(dot(left[0], a) + dot(left[1], b))
        parts, halved = [], []
        for i, blocks in enumerate(far):
            late = dot(jnp.concatenate(left[2:], 1), jnp.concatenate(blocks, 0))
            parts.append(early[i] + late)
            halved.append(parts[-1].astype(jnp.float16))

        def rows_for(value, step):
            return value[step * group : (step + 1) * group]

        totals = [rows_for(p, 0) for p in parts]
        for step, chunk in sends(chips, len(bounds)):
            if chunk is None:
                sent = jnp.concatenate([rows_for(h, step) for h in halved], 1)
            else:
                sent = rows_for(halved[chunk], step)
            got = flip(sent, "col", (cols_n,), (2 * step,))
            if chunk is None:
                got = [got[:, low:high].astype(jnp.float32) for low, high in bounds]
                totals = [t + g for t, g in zip(totals, got)]
            else:
                totals[chunk] += got.astype(jnp.float32)
        total = jnp.concatenate([t.astype(jnp.float16) for t in totals], 1)

        blocks = total.reshape(2, pair_n, own_rows, share)
        got = []
        for step in range(pair_n):
            sent = pick(at_pair, [blocks[:, i ^ step] for i in range(pair_n)])
            got.append(sent if step == 0 else flip(sent, "pair", (pair_n,), (step,)))
        keep = [jnp.where(first_core, g[0], g[1]) for g in got]
        send = jnp.stack([jnp.where(first_core, g[1], g[0]) for g in got])
        back = flip(send, "col", (cols_n,), (1,))

        def in_order(values):
            parts = [pick(at_pair, [values[i ^ p] for p in range(pair_n)]) for i in range(pair_n)]
            return jnp.concatenate(parts, 1).astype(jnp.float32)

        rest = (driver, vir_energy[None, :], occ_energy[None, :], occ_coupling)
        columns = occ_energy.shape[0]
        here = in_order(keep)
        begun = update_call(functools.partial(begin_kernel, share), own_rows, columns, [], here, *rest)
        there = in_order(back)
        scratch = [pltpu.VMEM((own_rows, columns), jnp.float32)]
        kernel = functools.partial(finish_kernel, share)
        return update_call(kernel, own_rows, columns, scratch, here, there, *rest, begun)

    return jax.shard_map(
        body,
        mesh=mesh,
        in_specs=(
            P("row", "col"),
            P("row", "col"),
            P(("col", "row"), "pair"),
            P(("row", "col", "pair"), None),
            P(("row", "col", "pair")),
            P(),
            P(),
        ),
        out_specs=P(("row", "col", "pair"), None),
        check_vma=False,
    )
```

time: 32.9 us -> 35.7 us (1.085)
  starting transfers between devices: 9.81 us -> 16.3 us
  waiting for transfers between devices: 16 us -> 11.5 us
  Pallas kernels: 1.66 us -> 2.9 us
  other arithmetic: 3.22 us -> 2.2 us
  matrix products: 1.04 us -> 1.51 us
    ppermute x10 -> x15, starting transfers between devices: 9.81 us -> 16.3 us  [flip(): return lax.ppermute(value, axes, pairs)]
    ppermute x10 -> x15, waiting for transfers between devices: 16 us -> 11.5 us  [flip(): return lax.ppermute(value, axes, pairs)]
    pallas_call x1 -> x3, Pallas kernels: 1.66 us -> 2.9 us  [the longest x2 1.86 us: update_call(): pl.pallas_call(kernel, out_shape=jax.ShapeDtypeStruct((rows, columns), jn...]
    select_n x1 -> x0, other arithmetic: 1.06 us -> none  [halves(): return (jnp.where(first, low, high), jnp.where(first, high, low))]
    dot_general x3 -> x6, matrix products: 1.04 us -> 1.51 us  [dot(): jnp.dot(a, b, preferred_element_type=jnp.float32)]
  transfers between devices with their start and end apart: 10 -> 15, of which waited for: 5 -> 5; matrix products, arithmetic and copies ran while one was open for 9% -> 11% of each run, Pallas kernels for 0% -> 2%
where the time goes in v2:
time: 35.7 us; the launch traced here: 35.5 us
  starting transfers between devices  16.3 us (46%)
  waiting for transfers between devices  11.5 us (32%)
  Pallas kernels  2.9 us (8%)
  other arithmetic  2.2 us (6%)
  matrix products  1.51 us (4%)
  local copies, waits for them, and re-layouts  0.62 us (2%)
  between operations  0.41 us (1%)
    ppermute x15, starting transfers between devices, flip(): return lax.ppermute(value, axes, pairs)  16.3 us
    ppermute x15, waiting for transfers between devices, flip(): return lax.ppermute(value, axes, pairs)  11.5 us
    pallas_call x2, Pallas kernels, update_call(): pl.pallas_call(kernel, out_shape=jax.ShapeDtypeStruct((rows, columns), jn...  1.86 us
    dot_general x6, matrix products, dot(): jnp.dot(a, b, preferred_element_type=jnp.float32)  1.51 us
    mul x2, other arithmetic, screened(): values = values * jnp.repeat(keep, tile, axis=0)  1.14 us
    pallas_call x1, Pallas kernels, fetch(): pl.pallas_call(functools.partial(fetch_kernel, columns // 2, bounds), out...  1.04 us
    mul x2, other arithmetic, screened(): keep = jnp.repeat(tiles.astype(jnp.bfloat16) * SCALE, tile, axis=1)  0.73 us
  transfers between devices with their start and end apart: 15, of which 5 were waited for; matrix products, arithmetic and copies ran while one was open for 11% of the time, Pallas kernels for 2%

profile of v2, /device:TPU:0, one launch (start us, length us, event | category | flops | bytes accessed | tf_op | source)
XLA Modules:
  0.0 35.5 jit_solution(7313534990174755400)
XLA Ops:
  0.0 1.0 %fetch.1 = (bf16[256,256]{1,0:T(8,128)(2,1)S(1)}, bf16[256,256]{1,0:T(8,128)(2,1)S(1)}, bf16[256,128]{1,0:T(8,128)(2,1)S(1)}, bf16[256,128]{1,0:T(8,128)(2,1)S(1)}) custom-call(bf16[256,768]{1,0:T(8,128)(2,1)} %whole.1), custom_call_target="tpu_custom_call" | custom-call | tf_op jit(solution)/shard_map/fetch/pallas_call | solution.py:106
  1.1 0.6 %collective-permute-start.7 = (bf16[256,128]{1,0:T(8,128)(2,1)S(1)}, bf16[256,128]{1,0:T(8,128)(2,1)S(1)}, u32[]{:S(2)}, u32[]{:S(2)}) collective-permute-start(bf16[256,128]{1,0:T(8,128)(2,1)S(1)} %get-tuple-element.24), channel_id=1, source_target_pairs={{0,2},{2,0},{4,6},{6,4},{8,10},{10,8},{12,14},{14,12},{1,3},{3,1},... | collective-permute-start | bytes 196616 | tf_op jit(solution)/shard_map/ppermute | solution.py:28
  1.6 2.6 %collective-permute-start.9 = (bf16[256,128]{1,0:T(8,128)(2,1)S(1)}, bf16[256,128]{1,0:T(8,128)(2,1)S(1)}, u32[]{:S(2)}, u32[]{:S(2)}) collective-permute-start(bf16[256,128]{1,0:T(8,128)(2,1)S(1)} %get-tuple-element.24), channel_id=1, source_target_pairs={{0,18},{2,16},{4,22},{6,20},{8,26},{10,24},{12,30},{14,28},{16,2},... | collective-permute-start | bytes 196616 | tf_op jit(solution)/shard_map/ppermute | solution.py:28
  4.2 0.1 collective-permute-start
  4.3 0.4 %collective-permute-start.1 = (s32[32,32]{1,0:T(8,128)}, s32[32,32]{1,0:T(8,128)S(1)}, u32[]{:S(2)}, u32[]{:S(2)}) collective-permute-start(s32[32,32]{1,0:T(8,128)} %param.8), channel_id=1, source_target_pairs={{0,2},{2,0},{4,6},{6,4},{8,10},{10,8},{12,14},{14,12},{1,3},{3,1},... | collective-permute-start | bytes 12296 | tf_op jit(solution)/shard_map/ppermute | solution.py:28
  4.8 0.7 %convert_multiply_fusion.1 = bf16[32,32]{1,0:T(8,128)(2,1)S(1)} fusion(s32[32,32]{1,0:T(8,128)} %param.8), kind=kLoop, calls=%fused_computation.48 | loop fusion | flops 2048 | bytes 6144 | tf_op jit(solution)/shard_map/mul | solution.py:175
  5.5 0.1 copy.8
  5.6 0.1 copy.9
  5.7 1.1 %bitcast_multiply_fusion.1 = bf16[512,512]{1,0:T(8,128)(2,1)S(1)} fusion(bf16[512,512]{1,0:T(8,128)(2,1)} %param.7, bf16[32,512]{1,0:T(8,128)(2,1)S(1)} %copy.9), kind=kLoop, calls=%fused_computation.8 | loop fusion | flops 262144 | bytes 1081344 | tf_op jit(solution)/shard_map/mul | solution.py:176
  6.9 0.2 fusion.9
  7.1 0.2 fusion.7
  7.4 2.0 %collective-permute-start.3 = (bf16[256,256]{1,0:T(8,128)(2,1)S(1)}, bf16[256,256]{1,0:T(8,128)(2,1)S(1)}, u32[]{:S(2)}, u32[]{:S(2)}) collective-permute-start(bf16[256,256]{1,0:T(8,128)(2,1)S(1)} %get-tuple-element.21), channel_id=1, source_target_pairs={{0,16},{2,18},{4,20},{6,22},{8,24},{10,26},{12,28},{14,30},{16,0},... | collective-permute-start | bytes 393224 | tf_op jit(solution)/shard_map/ppermute | solution.py:28
  9.4 0.1 copy.10
  9.6 0.1 copy.11
  9.7 0.1 collective-permute-start.4
  9.9 0.2 collective-permute-start.2
  10.1 0.2 convolution_add_fusion.2
  10.5 0.3 fusion.30
  10.8 4.7 %collective-permute-done.4 = bf16[256,256]{1,0:T(8,128)(2,1)S(1)} collective-permute-done((bf16[256,256]{1,0:T(8,128)(2,1)S(1)}, bf16[256,256]{1,0:T(8,128)(2,1)S(1)}, u32[]{:S(2)}, u32[]{:S(2)}) %collective-permute-start.4) | collective-permute-done | bytes 131104 | tf_op jit(solution)/shard_map/ppermute | solution.py:28
  15.5 0.3 fusion.1
  15.8 0.3 fusion.31
  16.2 3.7 %collective-permute-start.10 = (f16[128,384]{1,0:T(8,128)(2,1)S(1)}, f16[128,384]{1,0:T(8,128)(2,1)S(1)}, u32[]{:S(2)}, u32[]{:S(2)}) collective-permute-start(f16[128,384]{1,0:T(8,128)(2,1)S(1)} %pad_maximum_fusion.5), channel_id=1, source_target_pairs={{0,12},{2,14},{4,8},{6,10},{8,4},{10,6},{12,0},{14,2},{1,13},{3,15... | collective-permute-start | bytes 294920 | tf_op jit(solution)/shard_map/ppermute | solution.py:28
  19.8 0.8 %collective-permute-start.11 = (f16[128,128]{1,0:T(8,128)(2,1)S(1)}, f16[128,128]{1,0:T(8,128)(2,1)S(1)}, u32[]{:S(2)}, u32[]{:S(2)}) collective-permute-start(f16[128,128]{1,0:T(8,128)(2,1)S(1)} %get-tuple-element.38), channel_id=1, source_target_pairs={{0,8},{2,10},{4,12},{6,14},{8,0},{10,2},{12,4},{14,6},{1,9},{3,11}... | collective-permute-start | bytes 98312 | tf_op jit(solution)/shard_map/ppermute | solution.py:28
  20.6 1.3 %collective-permute-start.6 = (f16[128,256]{1,0:T(8,128)(2,1)S(1)}, f16[128,256]{1,0:T(8,128)(2,1)S(1)}, u32[]{:S(2)}, u32[]{:S(2)}) collective-permute-start(f16[128,256]{1,0:T(8,128)(2,1)S(1)} %get-tuple-element.35), channel_id=1, source_target_pairs={{0,4},{2,6},{4,0},{6,2},{8,12},{10,14},{12,8},{14,10},{1,5},{3,7},... | collective-permute-start | bytes 196616 | tf_op jit(solution)/shard_map/ppermute | solution.py:28
  22.0 2.9 %collective-permute-start.5 = (f16[128,256]{1,0:T(8,128)(2,1)S(1)}, f16[128,256]{1,0:T(8,128)(2,1)S(1)}, u32[]{:S(2)}, u32[]{:S(2)}) collective-permute-start(f16[128,256]{1,0:T(8,128)(2,1)S(1)} %get-tuple-element.33), channel_id=1, source_target_pairs={{0,8},{2,10},{4,12},{6,14},{8,0},{10,2},{12,4},{14,6},{1,9},{3,11}... | collective-permute-start | bytes 196616 | tf_op jit(solution)/shard_map/ppermute | solution.py:28
  24.9 2.0 %collective-permute-done.11 = f16[128,128]{1,0:T(8,128)(2,1)S(1)} collective-permute-done((f16[128,128]{1,0:T(8,128)(2,1)S(1)}, f16[128,128]{1,0:T(8,128)(2,1)S(1)}, u32[]{:S(2)}, u32[]{:S(2)}) %collective-permute-start.11) | collective-permute-done | bytes 32800 | tf_op jit(solution)/shard_map/ppermute | solution.py:28
  26.9 1.6 %collective-permute-done.5 = f16[128,256]{1,0:T(8,128)(2,1)S(1)} collective-permute-done((f16[128,256]{1,0:T(8,128)(2,1)S(1)}, f16[128,256]{1,0:T(8,128)(2,1)S(1)}, u32[]{:S(2)}, u32[]{:S(2)}) %collective-permute-start.5) | collective-permute-done | bytes 65568 | tf_op jit(solution)/shard_map/ppermute | solution.py:28
  28.7 1.6 %collective-permute-start.13 = (f16[2,32,384]{2,1,0:T(8,128)(2,1)S(1)}, f16[2,32,384]{2,1,0:T(8,128)(2,1)S(1)}, u32[]{:S(2)}, u32[]{:S(2)}) collective-permute-start(f16[2,32,384]{2,1,0:T(8,128)(2,1)S(1)} %get-tuple-element.42), channel_id=1, source_target_pairs={{0,1},{1,0},{2,3},{3,2},{4,5},{5,4},{6,7},{7,6},{8,9},{9,8},{10,11... | collective-permute-start | bytes 147464 | tf_op jit(solution)/shard_map/ppermute | solution.py:28
  30.3 2.6 %collective-permute-done.13 = f16[2,32,384]{2,1,0:T(8,128)(2,1)S(1)} collective-permute-done((f16[2,32,384]{2,1,0:T(8,128)(2,1)S(1)}, f16[2,32,384]{2,1,0:T(8,128)(2,1)S(1)}, u32[]{:S(2)}, u32[]{:S(2)}) %collective-permute-start.13) | collective-permute-done | bytes 49184 | tf_op jit(solution)/shard_map/ppermute | solution.py:28
  33.0 0.6 %shard_map.73.begun = f32[32,1536]{1,0:T(8,128)S(1)} custom-call(f32[32,768]{1,0:T(8,128)S(1)} %maximum_convert_fusion.ladder.mine, bf16[32,1536]{1,0:T(8,128)(2,1)S(1)} %copy-done, f32[1,32]{1,0:T(1,128)S(1)} %bitcast.33, f32[1,1536]{1,0:T(1,128)S(1)} %broadcast_in_dim.23.occ, bf16[1536,1536]{1,0:T(8,128)(2,1)S(1)} %bitcast.32), custom_call_target="tpu_custom_call" | custom-call | tf_op jit(solution)/shard_map/pallas_call | solution.py:76
  33.6 0.6 %collective-permute-done.14 = f16[2,32,384]{2,1,0:T(8,128)(2,1)S(1)} collective-permute-done((f16[2,32,384]{2,1,0:T(8,128)(2,1)S(1)}, f16[2,32,384]{2,1,0:T(8,128)(2,1)S(1)}, u32[]{:S(2)}, u32[]{:S(2)}) %collective-permute-start.14) | collective-permute-done | bytes 49184 | tf_op jit(solution)/shard_map/ppermute | solution.py:28
  34.2 1.3 %shard_map.74 = f32[32,1536]{1,0:T(8,128)} custom-call(f32[32,768]{1,0:T(8,128)S(1)} %maximum_convert_fusion.ladder.mine, f32[32,768]{1,0:T(8,128)S(1)} %maximum_convert_fusion.1.others, bf16[32,1536]{1,0:T(8,128)(2,1)S(1)} %copy-done, f32[1,32]{1,0:T(1,128)S(1)} %bitcast.34, f32[1,1536]{1,0:T(1,128)S(1)} %broadcast_in_dim.23.occ, ...), custom_call_target="tpu_custom_call" | custom-call | tf_op jit(solution)/shard_map/pallas_call | solution.py:76
  (47 shorter events, 0.8 us)
Async XLA Ops:
  1.1 8.9 %collective-permute-start.7 = (bf16[256,128]{1,0:T(8,128)(2,1)S(1)}, bf16[256,128]{1,0:T(8,128)(2,1)S(1)}, u32[]{:S(2)}, u32[]{:S(2)}) collective-permute-start(bf16[256,128]{1,0:T(8,128)(2,1)S(1)} %get-tuple-element.24), channel_id=1, source_target_pairs={{0,2},{2,0},{4,6},{6,4},{8,10},{10,8},{12,14},{14,12},{1,3},{3,1},... | collective-permute-start | bytes 196616 | tf_op jit(solution)/shard_map/ppermute | solution.py:28
  1.6 8.8 %collective-permute-start.9 = (bf16[256,128]{1,0:T(8,128)(2,1)S(1)}, bf16[256,128]{1,0:T(8,128)(2,1)S(1)}, u32[]{:S(2)}, u32[]{:S(2)}) collective-permute-start(bf16[256,128]{1,0:T(8,128)(2,1)S(1)} %get-tuple-element.24), channel_id=1, source_target_pairs={{0,18},{2,16},{4,22},{6,20},{8,26},{10,24},{12,30},{14,28},{16,2},... | collective-permute-start | bytes 196616 | tf_op jit(solution)/shard_map/ppermute | solution.py:28
  4.2 5.5 %collective-permute-start = (bf16[512,512]{1,0:T(8,128)(2,1)}, bf16[512,512]{1,0:T(8,128)(2,1)S(1)}, u32[]{:S(2)}, u32[]{:S(2)}) collective-permute-start(bf16[512,512]{1,0:T(8,128)(2,1)} %param.7), channel_id=1, source_target_pairs={{0,2},{2,0},{4,6},{6,4},{8,10},{10,8},{12,14},{14,12},{1,3},{3,1},... | collective-permute-start | bytes 1572872 | tf_op jit(solution)/shard_map/ppermute | solution.py:28
  4.3 3.1 %collective-permute-start.1 = (s32[32,32]{1,0:T(8,128)}, s32[32,32]{1,0:T(8,128)S(1)}, u32[]{:S(2)}, u32[]{:S(2)}) collective-permute-start(s32[32,32]{1,0:T(8,128)} %param.8), channel_id=1, source_target_pairs={{0,2},{2,0},{4,6},{6,4},{8,10},{10,8},{12,14},{14,12},{1,3},{3,1},... | collective-permute-start | bytes 12296 | tf_op jit(solution)/shard_map/ppermute | solution.py:28
  4.7 5.7 %collective-permute-start.8 = (bf16[256,128]{1,0:T(8,128)(2,1)S(1)}, bf16[256,128]{1,0:T(8,128)(2,1)S(1)}, u32[]{:S(2)}, u32[]{:S(2)}) collective-permute-start(bf16[256,128]{1,0:T(8,128)(2,1)S(1)} %get-tuple-element.23), channel_id=1, source_target_pairs={{0,16},{2,18},{4,20},{6,22},{8,24},{10,26},{12,28},{14,30},{16,0},... | collective-permute-start | bytes 196616 | tf_op jit(solution)/shard_map/ppermute | solution.py:28
  6.9 26.1 %slice-start = ((s8[4718592]{0:T(1024)(128)(4,1)}), s8[524288]{0:T(1024)(128)(4,1)S(1)}, s32[]{:S(2)}) async-start(s8[4718592]{0:T(1024)(128)(4,1)} %bitcast.31), calls=%async_computation | async-start | bytes 1048576
  7.4 8.1 %collective-permute-start.3 = (bf16[256,256]{1,0:T(8,128)(2,1)S(1)}, bf16[256,256]{1,0:T(8,128)(2,1)S(1)}, u32[]{:S(2)}, u32[]{:S(2)}) collective-permute-start(bf16[256,256]{1,0:T(8,128)(2,1)S(1)} %get-tuple-element.21), channel_id=1, source_target_pairs={{0,16},{2,18},{4,20},{6,22},{8,24},{10,26},{12,28},{14,30},{16,0},... | collective-permute-start | bytes 393224 | tf_op jit(solution)/shard_map/ppermute | solution.py:28
  9.7 5.9 %collective-permute-start.4 = (bf16[256,256]{1,0:T(8,128)(2,1)S(1)}, bf16[256,256]{1,0:T(8,128)(2,1)S(1)}, u32[]{:S(2)}, u32[]{:S(2)}) collective-permute-start(bf16[256,256]{1,0:T(8,128)(2,1)S(1)} %get-tuple-element.22), channel_id=1, source_target_pairs={{0,18},{2,16},{4,22},{6,20},{8,26},{10,24},{12,30},{14,28},{16,2},... | collective-permute-start | bytes 393224 | tf_op jit(solution)/shard_map/ppermute | solution.py:28
  9.9 10.8 %copy-start.2 = (f32[1536]{0:T(1024)S(1)}, f32[1536]{0:T(1024)}, u32[]{:S(2)}) copy-start(f32[1536]{0:T(1024)} %param.12) | copy-start | bytes 18436
  9.9 23.1 %copy-start = (bf16[32,1536]{1,0:T(8,128)(2,1)S(1)}, bf16[32,1536]{1,0:T(8,128)(2,1)}, u32[]{:S(2)}) copy-start(bf16[32,1536]{1,0:T(8,128)(2,1)} %driver.3) | copy-start | bytes 294916
  9.9 23.1 %copy-start.1 = (f32[32]{0:T(128)S(1)}, f32[32]{0:T(128)}, u32[]{:S(2)}) copy-start(f32[32]{0:T(128)} %param.11) | copy-start | bytes 388
  9.9 5.9 %collective-permute-start.2 = (bf16[256,256]{1,0:T(8,128)(2,1)S(1)}, bf16[256,256]{1,0:T(8,128)(2,1)S(1)}, u32[]{:S(2)}, u32[]{:S(2)}) collective-permute-start(bf16[256,256]{1,0:T(8,128)(2,1)S(1)} %get-tuple-element.22), channel_id=1, source_target_pairs={{0,2},{2,0},{4,6},{6,4},{8,10},{10,8},{12,14},{14,12},{1,3},{3,1},... | collective-permute-start | bytes 393224 | tf_op jit(solution)/shard_map/ppermute | solution.py:28
  10.4 22.6 %slice-start.1 = ((s8[4718592]{0:T(1024)(128)(4,1)}), s8[4194304]{0:T(1024)(128)(4,1)S(1)}, s32[]{:S(2)}) async-start(s8[4718592]{0:T(1024)(128)(4,1)} %bitcast.31), calls=%async_computation.1 | async-start | bytes 8388608
  16.2 10.7 %collective-permute-start.10 = (f16[128,384]{1,0:T(8,128)(2,1)S(1)}, f16[128,384]{1,0:T(8,128)(2,1)S(1)}, u32[]{:S(2)}, u32[]{:S(2)}) collective-permute-start(f16[128,384]{1,0:T(8,128)(2,1)S(1)} %pad_maximum_fusion.5), channel_id=1, source_target_pairs={{0,12},{2,14},{4,8},{6,10},{8,4},{10,6},{12,0},{14,2},{1,13},{3,15... | collective-permute-start | bytes 294920 | tf_op jit(solution)/shard_map/ppermute | solution.py:28
  19.8 5.0 %collective-permute-start.12 = (f16[128,128]{1,0:T(8,128)(2,1)S(1)}, f16[128,128]{1,0:T(8,128)(2,1)S(1)}, u32[]{:S(2)}, u32[]{:S(2)}) collective-permute-start(f16[128,128]{1,0:T(8,128)(2,1)S(1)} %get-tuple-element.37), channel_id=1, source_target_pairs={{0,4},{2,6},{4,0},{6,2},{8,12},{10,14},{12,8},{14,10},{1,5},{3,7},... | collective-permute-start | bytes 98312 | tf_op jit(solution)/shard_map/ppermute | solution.py:28
  19.8 7.0 %collective-permute-start.11 = (f16[128,128]{1,0:T(8,128)(2,1)S(1)}, f16[128,128]{1,0:T(8,128)(2,1)S(1)}, u32[]{:S(2)}, u32[]{:S(2)}) collective-permute-start(f16[128,128]{1,0:T(8,128)(2,1)S(1)} %get-tuple-element.38), channel_id=1, source_target_pairs={{0,8},{2,10},{4,12},{6,14},{8,0},{10,2},{12,4},{14,6},{1,9},{3,11}... | collective-permute-start | bytes 98312 | tf_op jit(solution)/shard_map/ppermute | solution.py:28
  20.6 6.2 %collective-permute-start.6 = (f16[128,256]{1,0:T(8,128)(2,1)S(1)}, f16[128,256]{1,0:T(8,128)(2,1)S(1)}, u32[]{:S(2)}, u32[]{:S(2)}) collective-permute-start(f16[128,256]{1,0:T(8,128)(2,1)S(1)} %get-tuple-element.35), channel_id=1, source_target_pairs={{0,4},{2,6},{4,0},{6,2},{8,12},{10,14},{12,8},{14,10},{1,5},{3,7},... | collective-permute-start | bytes 196616 | tf_op jit(solution)/shard_map/ppermute | solution.py:28
  22.0 6.6 %collective-permute-start.5 = (f16[128,256]{1,0:T(8,128)(2,1)S(1)}, f16[128,256]{1,0:T(8,128)(2,1)S(1)}, u32[]{:S(2)}, u32[]{:S(2)}) collective-permute-start(f16[128,256]{1,0:T(8,128)(2,1)S(1)} %get-tuple-element.33), channel_id=1, source_target_pairs={{0,8},{2,10},{4,12},{6,14},{8,0},{10,2},{12,4},{14,6},{1,9},{3,11}... | collective-permute-start | bytes 196616 | tf_op jit(solution)/shard_map/ppermute | solution.py:28
  28.7 4.2 %collective-permute-start.13 = (f16[2,32,384]{2,1,0:T(8,128)(2,1)S(1)}, f16[2,32,384]{2,1,0:T(8,128)(2,1)S(1)}, u32[]{:S(2)}, u32[]{:S(2)}) collective-permute-start(f16[2,32,384]{2,1,0:T(8,128)(2,1)S(1)} %get-tuple-element.42), channel_id=1, source_target_pairs={{0,1},{1,0},{2,3},{3,2},{4,5},{5,4},{6,7},{7,6},{8,9},{9,8},{10,11... | collective-permute-start | bytes 147464 | tf_op jit(solution)/shard_map/ppermute | solution.py:28
  32.9 1.3 %collective-permute-start.14 = (f16[2,32,384]{2,1,0:T(8,128)(2,1)S(1)}, f16[2,32,384]{2,1,0:T(8,128)(2,1)S(1)}, u32[]{:S(2)}, u32[]{:S(2)}) collective-permute-start(f16[2,32,384]{2,1,0:T(8,128)(2,1)S(1)} %pad_maximum_fusion.7), channel_id=1, source_target_pairs={{0,2},{2,0},{4,6},{6,4},{8,10},{10,8},{12,14},{14,12},{1,3},{3,1},... | collective-permute-start | bytes 147464 | tf_op jit(solution)/shard_map/ppermute | solution.py:28

commit v3 on v2

--- a/solution.py
+++ b/solution.py
@@ -34,41 +34,38 @@
     return jnp.sum(jnp.where(diagonal, row[...], 0.0), axis=1, keepdims=True)
 
 
-def spans(side, share, count):
-    return [pl.ds(pl.multiple_of((2 * i + side) * share, LANES), share) for i in range(count)]
-
-
-def terms(ladder, driver, vir, occ, span, i, share):
-    denom = vir - occ[:, span]
-    residual = driver[:, span].astype(jnp.float32) + ladder[:, i * share : (i + 1) * share] * (1 / SCALE)
-    return residual, denom
-
-
-def couple(ladder, driver, vir, occ, coupling, columns):
-    total, share = None, ladder.shape[1] // len(columns)
-    for i, span in enumerate(columns):
-        residual, denom = terms(ladder, driver, vir, occ, span, i, share)
-        scaled = (residual / denom).astype(jnp.bfloat16)
-        product = jnp.dot(scaled, coupling[span, :], preferred_element_type=jnp.float32)
-        total = product if total is None else total + product
+def terms(piece, share, ladder, driver, vir, occ):
+    mine, low, high = piece
+    size = high - low
+    core = lax.axis_index("col") & 1
+    side = core if mine else 1 - core
+    for i in range(ladder.shape[1] // size):
+        span = pl.ds(pl.multiple_of((2 * i + side) * share + low, LANES), size)
+        residual = driver[:, span].astype(jnp.float32) + ladder[:, i * size : (i + 1) * size] * (1 / SCALE)
+        yield span, residual, vir - occ[:, span]
+
+
+def couple(total, pieces, share, ladders, driver, vir, occ, coupling):
+    for piece, ladder in zip(pieces, ladders):
+        for span, residual, denom in terms(piece, share, ladder, driver, vir, occ):
+            scaled = (residual / denom).astype(jnp.bfloat16)
+            product = jnp.dot(scaled, coupling[span, :], preferred_element_type=jnp.float32)
+            total = product if total is None else total + product
     return total
 
 
-def begin_kernel(share, ladder, driver, vir, occ, coupling, out):
-    core = lax.axis_index("col") & 1
-    columns = spans(core, share, ladder.shape[1] // share)
-    out[...] = couple(ladder, driver, tall(vir), occ, coupling, columns)
-
-
-def finish_kernel(share, mine, others, driver, vir, occ, coupling, begun, out, coupled):
-    core = lax.axis_index("col") & 1
-    count = mine.shape[1] // share
-    here, there = spans(core, share, count), spans(1 - core, share, count)
+def begin_kernel(pieces, share, carried, driver, vir, occ, coupling, *refs):
+    ladders, out = refs[: len(pieces)], refs[-1]
+    total = refs[len(pieces)][...] if carried else None
+    out[...] = couple(total, pieces, share, ladders, driver, tall(vir), occ, coupling)
+
+
+def finish_kernel(pieces, share, last, driver, vir, occ, coupling, *refs):
+    ladders, begun, out, coupled = refs[: len(pieces)], *refs[len(pieces) :]
     column = tall(vir)
-    coupled[...] = begun[...] + couple(others, driver, column, occ, coupling, there)
-    for ladder, columns in ((mine, here), (others, there)):
-        for i, span in enumerate(columns):
-            residual, denom = terms(ladder, driver, column, occ, span, i, share)
+    coupled[...] = couple(begun[...], pieces[last:], share, ladders[last:], driver, column, occ, coupling)
+    for piece, ladder in zip(pieces, ladders):
+        for span, residual, denom in terms(piece, share, ladder, driver, column, occ):
             out[:, span] = -(residual - coupled[:, span]) / denom
 
 
@@ -124,8 +121,8 @@
 
 
 FIRST = 2
-EARLY = "21"
-REST = ((2, 1), (3, None), (1, 1))
+EARLY = "213"
+REST = ((2, 1), (3, 1), (1, 1))
 
 
 def chunk_bounds(share):
@@ -185,12 +182,14 @@
         def dot(a, b):
             return with_layout_constraint(jnp.dot(a, b, preferred_element_type=jnp.float32), Layout((0, 1)))
 
+        near_left, far_left = jnp.concatenate(left[:2], 1), jnp.concatenate(left[2:], 1)
         early = []
         for a, b in zip(mine, near):
-            early.append(dot(left[0], a) + dot(left[1], b))
+            early.append(dot(near_left, jnp.concatenate([a, b], 0)))
+        early, far[0] = lax.optimization_barrier((early, far[0]))
         parts, halved = [], []
         for i, blocks in enumerate(far):
-            late = dot(jnp.concatenate(left[2:], 1), jnp.concatenate(blocks, 0))
+            late = dot(far_left, jnp.concatenate(blocks, 0))
             parts.append(early[i] + late)
             halved.append(parts[-1].astype(jnp.float16))
 
@@ -198,6 +197,7 @@
             return value[step * group : (step + 1) * group]
 
         totals = [rows_for(p, 0) for p in parts]
+        arrived = [[] for _ in parts]
         for step, chunk in sends(chips, len(bounds)):
             if chunk is None:
                 sent = jnp.concatenate([rows_for(h, step) for h in halved], 1)
@@ -205,33 +205,41 @@
                 sent = rows_for(halved[chunk], step)
             got = flip(sent, "col", (cols_n,), (2 * step,))
             if chunk is None:
-                got = [got[:, low:high].astype(jnp.float32) for low, high in bounds]
-                totals = [t + g for t, g in zip(totals, got)]
+                for i, (low, high) in enumerate(bounds):
+                    arrived[i].append(got[:, low:high])
             else:
-                totals[chunk] += got.astype(jnp.float32)
-        total = jnp.concatenate([t.astype(jnp.float16) for t in totals], 1)
-
-        blocks = total.reshape(2, pair_n, own_rows, share)
-        got = []
-        for step in range(pair_n):
-            sent = pick(at_pair, [blocks[:, i ^ step] for i in range(pair_n)])
-            got.append(sent if step == 0 else flip(sent, "pair", (pair_n,), (step,)))
-        keep = [jnp.where(first_core, g[0], g[1]) for g in got]
-        send = jnp.stack([jnp.where(first_core, g[1], g[0]) for g in got])
-        back = flip(send, "col", (cols_n,), (1,))
-
-        def in_order(values):
-            parts = [pick(at_pair, [values[i ^ p] for p in range(pair_n)]) for i in range(pair_n)]
-            return jnp.concatenate(parts, 1).astype(jnp.float32)
+                arrived[chunk].append(got)
 
         rest = (driver, vir_energy[None, :], occ_energy[None, :], occ_coupling)
+        pieces, ladders = [], []
+        for c, (low, high) in enumerate(bounds):
+            total = totals[c]
+            for value in arrived[c]:
+                total += value.astype(jnp.float32)
+            blocks = total.astype(jnp.float16).reshape(2, pair_n, own_rows, high - low)
+            outgoing = [pick(at_pair, [blocks[:, i ^ s] for i in range(pair_n)]) for s in range(pair_n)]
+            got = outgoing[:1]
+            for step in range(1, pair_n):
+                got.append(flip(outgoing[step], "pair", (pair_n,), (step,)))
+            keep = [jnp.where(first_core, g[0], g[1]) for g in got]
+            send = jnp.stack([jnp.where(first_core, g[1], g[0]) for g in got])
+            back = flip(send, "col", (cols_n,), (1,))
+            for mine_side, values in ((True, keep), (False, back)):
+                in_order = [pick(at_pair, [values[i ^ p] for p in range(pair_n)]) for i in range(pair_n)]
+                ladders.append(jnp.concatenate(in_order, 1).astype(jnp.float32))
+                pieces.append((mine_side, low, high))
+
         columns = occ_energy.shape[0]
-        here = in_order(keep)
-        begun = update_call(functools.partial(begin_kernel, share), own_rows, columns, [], here, *rest)
-        there = in_order(back)
+        begun, done = None, 0
+        for c in range(len(bounds)):
+            upto = 2 * c + 1
+            kernel = functools.partial(begin_kernel, tuple(pieces[done:upto]), share, begun is not None)
+            carried = [] if begun is None else [begun]
+            begun = update_call(kernel, own_rows, columns, [], *rest, *ladders[done:upto], *carried)
+            done = upto
+        kernel = functools.partial(finish_kernel, tuple(pieces), share, done)
         scratch = [pltpu.VMEM((own_rows, columns), jnp.float32)]
-        kernel = functools.partial(finish_kernel, share)
-        return update_call(kernel, own_rows, columns, scratch, here, there, *rest, begun)
+        return update_call(kernel, own_rows, columns, scratch, *rest, *ladders, begun)
 
     return jax.shard_map(
         body,

time: 35.7 us -> 39.6 us (1.11)
  starting transfers between devices: 16.3 us -> 18 us
  waiting for transfers between devices: 11.5 us -> 13 us
  local copies, waits for them, and re-layouts: 0.62 us -> 1.36 us
    ppermute x15 -> x18, starting transfers between devices: 16.3 us -> 18 us  [flip(): return lax.ppermute(value, axes, pairs)]
    ppermute x15 -> x18, waiting for transfers between devices: 11.5 us -> 13 us  [flip(): return lax.ppermute(value, axes, pairs)]
    broadcast_in_dim x1, local copies, waits for them, and re-layouts: 0.01 us -> 0.7 us  [body(): rest = (driver, vir_energy[None, :], occ_energy[None, :], occ_coupling)]
    dot_general x6 -> x4, matrix products: 1.51 us -> 1.19 us  [dot(): jnp.dot(a, b, preferred_element_type=jnp.float32)]
    pallas_call x2 -> x3, Pallas kernels: 1.86 us -> 2 us  [update_call(): pl.pallas_call(kernel, out_shape=jax.ShapeDtypeStruct((rows, columns), jn...]
  transfers between devices with their start and end apart: 15 -> 18, of which waited for: 5 -> 5; matrix products, arithmetic and copies ran while one was open for 11% -> 11% of each run, Pallas kernels for 2% -> 1%
where the time goes in v3:
time: 39.6 us; the launch traced here: 39.3 us
  starting transfers between devices  18 us (45%)
  waiting for transfers between devices  13 us (33%)
  Pallas kernels  3.04 us (8%)
  other arithmetic  2.28 us (6%)
  local copies, waits for them, and re-layouts  1.36 us (3%)
  matrix products  1.19 us (3%)
  between operations  0.43 us (1%)
    ppermute x18, starting transfers between devices, flip(): return lax.ppermute(value, axes, pairs)  18 us
    ppermute x18, waiting for transfers between devices, flip(): return lax.ppermute(value, axes, pairs)  13 us
    pallas_call x3, Pallas kernels, update_call(): pl.pallas_call(kernel, out_shape=jax.ShapeDtypeStruct((rows, columns), jn...  2 us
    dot_general x4, matrix products, dot(): jnp.dot(a, b, preferred_element_type=jnp.float32)  1.19 us
    mul x2, other arithmetic, screened(): values = values * jnp.repeat(keep, tile, axis=0)  1.15 us
    pallas_call x1, Pallas kernels, fetch(): pl.pallas_call(functools.partial(fetch_kernel, columns // 2, bounds), out...  1.04 us
  transfers between devices with their start and end apart: 18, of which 5 were waited for; matrix products, arithmetic and copies ran while one was open for 11% of the time, Pallas kernels for 1%

profile of v3, /device:TPU:0, one launch (start us, length us, event | category | flops | bytes accessed | tf_op | source)
XLA Modules:
  0.0 39.3 jit_solution(5890724096909229410)
XLA Ops:
  0.0 1.0 %fetch.1 = (bf16[256,256]{1,0:T(8,128)(2,1)S(1)}, bf16[256,256]{1,0:T(8,128)(2,1)S(1)}, bf16[256,128]{1,0:T(8,128)(2,1)S(1)}, bf16[256,128]{1,0:T(8,128)(2,1)S(1)}) custom-call(bf16[256,768]{1,0:T(8,128)(2,1)} %whole.1), custom_call_target="tpu_custom_call" | custom-call | tf_op jit(solution)/shard_map/fetch/pallas_call | solution.py:103
  1.1 2.5 %collective-permute-start.12 = (bf16[256,128]{1,0:T(8,128)(2,1)S(1)}, bf16[256,128]{1,0:T(8,128)(2,1)S(1)}, u32[]{:S(2)}, u32[]{:S(2)}) collective-permute-start(bf16[256,128]{1,0:T(8,128)(2,1)S(1)} %get-tuple-element.28), channel_id=1, source_target_pairs={{0,18},{2,16},{4,22},{6,20},{8,26},{10,24},{12,30},{14,28},{16,2},... | collective-permute-start | bytes 196616 | tf_op jit(solution)/shard_map/ppermute | solution.py:28
  3.5 0.7 %collective-permute-start.3 = (bf16[256,128]{1,0:T(8,128)(2,1)S(1)}, bf16[256,128]{1,0:T(8,128)(2,1)S(1)}, u32[]{:S(2)}, u32[]{:S(2)}) collective-permute-start(bf16[256,128]{1,0:T(8,128)(2,1)S(1)} %get-tuple-element.28), channel_id=1, source_target_pairs={{0,2},{2,0},{4,6},{6,4},{8,10},{10,8},{12,14},{14,12},{1,3},{3,1},... | collective-permute-start | bytes 196616 | tf_op jit(solution)/shard_map/ppermute | solution.py:28
  4.2 0.5 %collective-permute-start.1 = (s32[32,32]{1,0:T(8,128)}, s32[32,32]{1,0:T(8,128)S(1)}, u32[]{:S(2)}, u32[]{:S(2)}) collective-permute-start(s32[32,32]{1,0:T(8,128)} %param.8), channel_id=1, source_target_pairs={{0,2},{2,0},{4,6},{6,4},{8,10},{10,8},{12,14},{14,12},{1,3},{3,1},... | collective-permute-start | bytes 12296 | tf_op jit(solution)/shard_map/ppermute | solution.py:28
  4.7 0.7 %convert_multiply_fusion.1 = bf16[32,32]{1,0:T(8,128)(2,1)S(1)} fusion(s32[32,32]{1,0:T(8,128)} %param.8), kind=kLoop, calls=%fused_computation.58 | loop fusion | flops 2048 | bytes 6144 | tf_op jit(solution)/shard_map/mul | solution.py:172
  5.4 0.1 copy.8
  5.6 1.1 %bitcast_multiply_fusion.1 = bf16[512,512]{1,0:T(8,128)(2,1)S(1)} fusion(bf16[512,512]{1,0:T(8,128)(2,1)} %param.7, bf16[32,512]{1,0:T(8,128)(2,1)S(1)} %copy.9), kind=kLoop, calls=%fused_computation.5 | loop fusion | flops 262144 | bytes 1081344 | tf_op jit(solution)/shard_map/mul | solution.py:173
  6.9 0.7 %broadcast_in_dim.19.occ = f32[1,1536]{1,0:T(1,128)S(1)} reshape(f32[1536]{0:T(1024)} %param.12) | data formatting | bytes 12288 | tf_op jit(solution)/shard_map/broadcast_in_dim | solution.py:213
  7.6 0.2 collective-permute-start.5
  7.7 0.1 copy.10
  8.0 2.0 %collective-permute-start.11 = (bf16[256,128]{1,0:T(8,128)(2,1)S(1)}, bf16[256,128]{1,0:T(8,128)(2,1)S(1)}, u32[]{:S(2)}, u32[]{:S(2)}) collective-permute-start(bf16[256,128]{1,0:T(8,128)(2,1)S(1)} %get-tuple-element.27), channel_id=1, source_target_pairs={{0,16},{2,18},{4,20},{6,22},{8,24},{10,26},{12,28},{14,30},{16,0},... | collective-permute-start | bytes 196616 | tf_op jit(solution)/shard_map/ppermute | solution.py:28
  10.3 0.1 collective-permute-start.4
  10.4 0.3 fusion.3
  10.7 0.3 fusion.2
  11.0 6.6 %collective-permute-done.4 = bf16[256,256]{1,0:T(8,128)(2,1)S(1)} collective-permute-done((bf16[256,256]{1,0:T(8,128)(2,1)S(1)}, bf16[256,256]{1,0:T(8,128)(2,1)S(1)}, u32[]{:S(2)}, u32[]{:S(2)}) %collective-permute-start.4) | collective-permute-done | bytes 131104 | tf_op jit(solution)/shard_map/ppermute | solution.py:28
  17.6 0.3 fusion
  18.0 2.7 %collective-permute-start.13 = (f16[128,128]{1,0:T(8,128)(2,1)S(1)}, f16[128,128]{1,0:T(8,128)(2,1)S(1)}, u32[]{:S(2)}, u32[]{:S(2)}) collective-permute-start(f16[128,128]{1,0:T(8,128)(2,1)S(1)} %get-tuple-element.52), channel_id=1, source_target_pairs={{0,8},{2,10},{4,12},{6,14},{8,0},{10,2},{12,4},{14,6},{1,9},{3,11}... | collective-permute-start | bytes 98312 | tf_op jit(solution)/shard_map/ppermute | solution.py:28
  20.7 1.3 %collective-permute-start.14 = (f16[128,128]{1,0:T(8,128)(2,1)S(1)}, f16[128,128]{1,0:T(8,128)(2,1)S(1)}, u32[]{:S(2)}, u32[]{:S(2)}) collective-permute-start(f16[128,128]{1,0:T(8,128)(2,1)S(1)} %get-tuple-element.54), channel_id=1, source_target_pairs={{0,12},{2,14},{4,8},{6,10},{8,4},{10,6},{12,0},{14,2},{1,13},{3,15... | collective-permute-start | bytes 98312 | tf_op jit(solution)/shard_map/ppermute | solution.py:28
  22.0 0.2 collective-permute-start.15
  22.2 0.3 fusion.1
  22.7 2.9 %collective-permute-start.6 = (f16[128,256]{1,0:T(8,128)(2,1)S(1)}, f16[128,256]{1,0:T(8,128)(2,1)S(1)}, u32[]{:S(2)}, u32[]{:S(2)}) collective-permute-start(f16[128,256]{1,0:T(8,128)(2,1)S(1)} %get-tuple-element.49), channel_id=1, source_target_pairs={{0,8},{2,10},{4,12},{6,14},{8,0},{10,2},{12,4},{14,6},{1,9},{3,11}... | collective-permute-start | bytes 196616 | tf_op jit(solution)/shard_map/ppermute | solution.py:28
  25.6 0.7 %collective-permute-start.7 = (f16[128,256]{1,0:T(8,128)(2,1)S(1)}, f16[128,256]{1,0:T(8,128)(2,1)S(1)}, u32[]{:S(2)}, u32[]{:S(2)}) collective-permute-start(f16[128,256]{1,0:T(8,128)(2,1)S(1)} %get-tuple-element.51), channel_id=1, source_target_pairs={{0,4},{2,6},{4,0},{6,2},{8,12},{10,14},{12,8},{14,10},{1,5},{3,7},... | collective-permute-start | bytes 196616 | tf_op jit(solution)/shard_map/ppermute | solution.py:28
  26.2 0.9 %collective-permute-start.8 = (f16[128,256]{1,0:T(8,128)(2,1)S(1)}, f16[128,256]{1,0:T(8,128)(2,1)S(1)}, u32[]{:S(2)}, u32[]{:S(2)}) collective-permute-start(f16[128,256]{1,0:T(8,128)(2,1)S(1)} %get-tuple-element.50), channel_id=1, source_target_pairs={{0,12},{2,14},{4,8},{6,10},{8,4},{10,6},{12,0},{14,2},{1,13},{3,15... | collective-permute-start | bytes 196616 | tf_op jit(solution)/shard_map/ppermute | solution.py:28
  27.2 1.6 %collective-permute-start.16 = (f16[2,32,128]{2,1,0:T(8,128)(2,1)S(1)}, f16[2,32,128]{2,1,0:T(8,128)(2,1)S(1)}, u32[]{:S(2)}, u32[]{:S(2)}) collective-permute-start(f16[2,32,128]{2,1,0:T(8,128)(2,1)S(1)} %get-tuple-element.62), channel_id=1, source_target_pairs={{0,1},{1,0},{2,3},{3,2},{4,5},{5,4},{6,7},{7,6},{8,9},{9,8},{10,11... | collective-permute-start | bytes 49160 | tf_op jit(solution)/shard_map/ppermute | solution.py:28
  28.8 2.2 %collective-permute-done.16 = f16[2,32,128]{2,1,0:T(8,128)(2,1)S(1)} collective-permute-done((f16[2,32,128]{2,1,0:T(8,128)(2,1)S(1)}, f16[2,32,128]{2,1,0:T(8,128)(2,1)S(1)}, u32[]{:S(2)}, u32[]{:S(2)}) %collective-permute-start.16) | collective-permute-done | bytes 16416 | tf_op jit(solution)/shard_map/ppermute | solution.py:28
  31.1 1.1 %collective-permute-done.8 = f16[128,256]{1,0:T(8,128)(2,1)S(1)} collective-permute-done((f16[128,256]{1,0:T(8,128)(2,1)S(1)}, f16[128,256]{1,0:T(8,128)(2,1)S(1)}, u32[]{:S(2)}, u32[]{:S(2)}) %collective-permute-start.8) | collective-permute-done | bytes 65568 | tf_op jit(solution)/shard_map/ppermute | solution.py:28
  32.4 1.6 %collective-permute-start.9 = (f16[2,32,256]{2,1,0:T(8,128)(2,1)S(1)}, f16[2,32,256]{2,1,0:T(8,128)(2,1)S(1)}, u32[]{:S(2)}, u32[]{:S(2)}) collective-permute-start(f16[2,32,256]{2,1,0:T(8,128)(2,1)S(1)} %get-tuple-element.58), channel_id=1, source_target_pairs={{0,1},{1,0},{2,3},{3,2},{4,5},{5,4},{6,7},{7,6},{8,9},{9,8},{10,11... | collective-permute-start | bytes 98312 | tf_op jit(solution)/shard_map/ppermute | solution.py:28
  34.0 2.3 %collective-permute-done.9 = f16[2,32,256]{2,1,0:T(8,128)(2,1)S(1)} collective-permute-done((f16[2,32,256]{2,1,0:T(8,128)(2,1)S(1)}, f16[2,32,256]{2,1,0:T(8,128)(2,1)S(1)}, u32[]{:S(2)}, u32[]{:S(2)}) %collective-permute-start.9) | collective-permute-done | bytes 32800 | tf_op jit(solution)/shard_map/ppermute | solution.py:28
  36.5 0.4 %shard_map.73.refs_2_ = f32[32,1536]{1,0:T(8,128)S(1)} custom-call(bf16[32,1536]{1,0:T(8,128)(2,1)S(1)} %copy-done, f32[1,32]{1,0:T(1,128)S(1)} %bitcast.49, f32[1,1536]{1,0:T(1,128)S(1)} %broadcast_in_dim.19.occ, bf16[1536,1536]{1,0:T(8,128)(2,1)S(1)} %bitcast.48, f32[32,512]{1,0:T(8,128)S(1)} %maximum_convert_fusion.refs_0_), custom_call_target="tpu_custom_call" | custom-call | tf_op jit(solution)/shard_map/pallas_call | solution.py:73
  36.9 0.7 %collective-permute-done.10 = f16[2,32,256]{2,1,0:T(8,128)(2,1)S(1)} collective-permute-done((f16[2,32,256]{2,1,0:T(8,128)(2,1)S(1)}, f16[2,32,256]{2,1,0:T(8,128)(2,1)S(1)}, u32[]{:S(2)}, u32[]{:S(2)}) %collective-permute-start.10) | collective-permute-done | bytes 32800 | tf_op jit(solution)/shard_map/ppermute | solution.py:28
  37.7 0.5 %shard_map.74.refs_4_ = f32[32,1536]{1,0:T(8,128)S(1)} custom-call(bf16[32,1536]{1,0:T(8,128)(2,1)S(1)} %copy-done, f32[1,32]{1,0:T(1,128)S(1)} %bitcast.50, f32[1,1536]{1,0:T(1,128)S(1)} %broadcast_in_dim.19.occ, bf16[1536,1536]{1,0:T(8,128)(2,1)S(1)} %bitcast.48, f32[32,512]{1,0:T(8,128)S(1)} %maximum_convert_fusion.1.refs_0_.refs_1_, ...), custom_call_target="tpu_custom_call" | custom-call | tf_op jit(solution)/shard_map/pallas_call | solution.py:73
  38.2 1.0 %shard_map.75 = f32[32,1536]{1,0:T(8,128)} custom-call(bf16[32,1536]{1,0:T(8,128)(2,1)S(1)} %copy-done, f32[1,32]{1,0:T(1,128)S(1)} %bitcast.51, f32[1,1536]{1,0:T(1,128)S(1)} %broadcast_in_dim.19.occ, bf16[1536,1536]{1,0:T(8,128)(2,1)S(1)} %bitcast.48, f32[32,512]{1,0:T(8,128)S(1)} %maximum_convert_fusion.refs_0_, ...), custom_call_target="tpu_custom_call" | custom-call | tf_op jit(solution)/shard_map/pallas_call | solution.py:73
  (57 shorter events, 1.1 us)
Async XLA Ops:
  1.1 16.6 %collective-permute-start.12 = (bf16[256,128]{1,0:T(8,128)(2,1)S(1)}, bf16[256,128]{1,0:T(8,128)(2,1)S(1)}, u32[]{:S(2)}, u32[]{:S(2)}) collective-permute-start(bf16[256,128]{1,0:T(8,128)(2,1)S(1)} %get-tuple-element.28), channel_id=1, source_target_pairs={{0,18},{2,16},{4,22},{6,20},{8,26},{10,24},{12,30},{14,28},{16,2},... | collective-permute-start | bytes 196616 | tf_op jit(solution)/shard_map/ppermute | solution.py:28
  3.5 7.2 %collective-permute-start.3 = (bf16[256,128]{1,0:T(8,128)(2,1)S(1)}, bf16[256,128]{1,0:T(8,128)(2,1)S(1)}, u32[]{:S(2)}, u32[]{:S(2)}) collective-permute-start(bf16[256,128]{1,0:T(8,128)(2,1)S(1)} %get-tuple-element.28), channel_id=1, source_target_pairs={{0,2},{2,0},{4,6},{6,4},{8,10},{10,8},{12,14},{14,12},{1,3},{3,1},... | collective-permute-start | bytes 196616 | tf_op jit(solution)/shard_map/ppermute | solution.py:28
  4.2 3.8 %collective-permute-start = (bf16[512,512]{1,0:T(8,128)(2,1)}, bf16[512,512]{1,0:T(8,128)(2,1)S(1)}, u32[]{:S(2)}, u32[]{:S(2)}) collective-permute-start(bf16[512,512]{1,0:T(8,128)(2,1)} %param.7), channel_id=1, source_target_pairs={{0,2},{2,0},{4,6},{6,4},{8,10},{10,8},{12,14},{14,12},{1,3},{3,1},... | collective-permute-start | bytes 1572872 | tf_op jit(solution)/shard_map/ppermute | solution.py:28
  4.2 3.4 %collective-permute-start.1 = (s32[32,32]{1,0:T(8,128)}, s32[32,32]{1,0:T(8,128)S(1)}, u32[]{:S(2)}, u32[]{:S(2)}) collective-permute-start(s32[32,32]{1,0:T(8,128)} %param.8), channel_id=1, source_target_pairs={{0,2},{2,0},{4,6},{6,4},{8,10},{10,8},{12,14},{14,12},{1,3},{3,1},... | collective-permute-start | bytes 12296 | tf_op jit(solution)/shard_map/ppermute | solution.py:28
  4.7 5.6 %collective-permute-start.2 = (bf16[256,256]{1,0:T(8,128)(2,1)S(1)}, bf16[256,256]{1,0:T(8,128)(2,1)S(1)}, u32[]{:S(2)}, u32[]{:S(2)}) collective-permute-start(bf16[256,256]{1,0:T(8,128)(2,1)S(1)} %get-tuple-element.26), channel_id=1, source_target_pairs={{0,2},{2,0},{4,6},{6,4},{8,10},{10,8},{12,14},{14,12},{1,3},{3,1},... | collective-permute-start | bytes 393224 | tf_op jit(solution)/shard_map/ppermute | solution.py:28
  7.6 10.0 %collective-permute-start.5 = (bf16[256,256]{1,0:T(8,128)(2,1)S(1)}, bf16[256,256]{1,0:T(8,128)(2,1)S(1)}, u32[]{:S(2)}, u32[]{:S(2)}) collective-permute-start(bf16[256,256]{1,0:T(8,128)(2,1)S(1)} %get-tuple-element.26), channel_id=1, source_target_pairs={{0,18},{2,16},{4,22},{6,20},{8,26},{10,24},{12,30},{14,28},{16,2},... | collective-permute-start | bytes 393224 | tf_op jit(solution)/shard_map/ppermute | solution.py:28
  8.0 9.6 %collective-permute-start.11 = (bf16[256,128]{1,0:T(8,128)(2,1)S(1)}, bf16[256,128]{1,0:T(8,128)(2,1)S(1)}, u32[]{:S(2)}, u32[]{:S(2)}) collective-permute-start(bf16[256,128]{1,0:T(8,128)(2,1)S(1)} %get-tuple-element.27), channel_id=1, source_target_pairs={{0,16},{2,18},{4,20},{6,22},{8,24},{10,26},{12,28},{14,30},{16,0},... | collective-permute-start | bytes 196616 | tf_op jit(solution)/shard_map/ppermute | solution.py:28
  10.1 26.4 %slice-start = ((s8[4718592]{0:T(1024)(128)(4,1)}), s8[4194304]{0:T(1024)(128)(4,1)S(1)}, s32[]{:S(2)}) async-start(s8[4718592]{0:T(1024)(128)(4,1)} %bitcast.47), calls=%async_computation | async-start | bytes 8388608
  10.3 7.3 %collective-permute-start.4 = (bf16[256,256]{1,0:T(8,128)(2,1)S(1)}, bf16[256,256]{1,0:T(8,128)(2,1)S(1)}, u32[]{:S(2)}, u32[]{:S(2)}) collective-permute-start(bf16[256,256]{1,0:T(8,128)(2,1)S(1)} %get-tuple-element.25), channel_id=1, source_target_pairs={{0,16},{2,18},{4,20},{6,22},{8,24},{10,26},{12,28},{14,30},{16,0},... | collective-permute-start | bytes 393224 | tf_op jit(solution)/shard_map/ppermute | solution.py:28
  10.7 25.8 %copy-start = (bf16[32,1536]{1,0:T(8,128)(2,1)S(1)}, bf16[32,1536]{1,0:T(8,128)(2,1)}, u32[]{:S(2)}) copy-start(bf16[32,1536]{1,0:T(8,128)(2,1)} %driver.5) | copy-start | bytes 294916
  10.7 25.8 %copy-start.1 = (f32[32]{0:T(128)S(1)}, f32[32]{0:T(128)}, u32[]{:S(2)}) copy-start(f32[32]{0:T(128)} %param.11) | copy-start | bytes 388
  17.6 18.9 %slice-start.1 = ((s8[4718592]{0:T(1024)(128)(4,1)}), s8[524288]{0:T(1024)(128)(4,1)S(1)}, s32[]{:S(2)}) async-start(s8[4718592]{0:T(1024)(128)(4,1)} %bitcast.47), calls=%async_computation.1 | async-start | bytes 1048576
  18.0 8.2 %collective-permute-start.13 = (f16[128,128]{1,0:T(8,128)(2,1)S(1)}, f16[128,128]{1,0:T(8,128)(2,1)S(1)}, u32[]{:S(2)}, u32[]{:S(2)}) collective-permute-start(f16[128,128]{1,0:T(8,128)(2,1)S(1)} %get-tuple-element.52), channel_id=1, source_target_pairs={{0,8},{2,10},{4,12},{6,14},{8,0},{10,2},{12,4},{14,6},{1,9},{3,11}... | collective-permute-start | bytes 98312 | tf_op jit(solution)/shard_map/ppermute | solution.py:28
  20.7 6.5 %collective-permute-start.14 = (f16[128,128]{1,0:T(8,128)(2,1)S(1)}, f16[128,128]{1,0:T(8,128)(2,1)S(1)}, u32[]{:S(2)}, u32[]{:S(2)}) collective-permute-start(f16[128,128]{1,0:T(8,128)(2,1)S(1)} %get-tuple-element.54), channel_id=1, source_target_pairs={{0,12},{2,14},{4,8},{6,10},{8,4},{10,6},{12,0},{14,2},{1,13},{3,15... | collective-permute-start | bytes 98312 | tf_op jit(solution)/shard_map/ppermute | solution.py:28
  22.0 5.1 %collective-permute-start.15 = (f16[128,128]{1,0:T(8,128)(2,1)S(1)}, f16[128,128]{1,0:T(8,128)(2,1)S(1)}, u32[]{:S(2)}, u32[]{:S(2)}) collective-permute-start(f16[128,128]{1,0:T(8,128)(2,1)S(1)} %get-tuple-element.53), channel_id=1, source_target_pairs={{0,4},{2,6},{4,0},{6,2},{8,12},{10,14},{12,8},{14,10},{1,5},{3,7},... | collective-permute-start | bytes 98312 | tf_op jit(solution)/shard_map/ppermute | solution.py:28
  22.7 8.5 %collective-permute-start.6 = (f16[128,256]{1,0:T(8,128)(2,1)S(1)}, f16[128,256]{1,0:T(8,128)(2,1)S(1)}, u32[]{:S(2)}, u32[]{:S(2)}) collective-permute-start(f16[128,256]{1,0:T(8,128)(2,1)S(1)} %get-tuple-element.49), channel_id=1, source_target_pairs={{0,8},{2,10},{4,12},{6,14},{8,0},{10,2},{12,4},{14,6},{1,9},{3,11}... | collective-permute-start | bytes 196616 | tf_op jit(solution)/shard_map/ppermute | solution.py:28
  25.6 5.6 %collective-permute-start.7 = (f16[128,256]{1,0:T(8,128)(2,1)S(1)}, f16[128,256]{1,0:T(8,128)(2,1)S(1)}, u32[]{:S(2)}, u32[]{:S(2)}) collective-permute-start(f16[128,256]{1,0:T(8,128)(2,1)S(1)} %get-tuple-element.51), channel_id=1, source_target_pairs={{0,4},{2,6},{4,0},{6,2},{8,12},{10,14},{12,8},{14,10},{1,5},{3,7},... | collective-permute-start | bytes 196616 | tf_op jit(solution)/shard_map/ppermute | solution.py:28
  26.2 6.1 %collective-permute-start.8 = (f16[128,256]{1,0:T(8,128)(2,1)S(1)}, f16[128,256]{1,0:T(8,128)(2,1)S(1)}, u32[]{:S(2)}, u32[]{:S(2)}) collective-permute-start(f16[128,256]{1,0:T(8,128)(2,1)S(1)} %get-tuple-element.50), channel_id=1, source_target_pairs={{0,12},{2,14},{4,8},{6,10},{8,4},{10,6},{12,0},{14,2},{1,13},{3,15... | collective-permute-start | bytes 196616 | tf_op jit(solution)/shard_map/ppermute | solution.py:28
  27.2 3.8 %collective-permute-start.16 = (f16[2,32,128]{2,1,0:T(8,128)(2,1)S(1)}, f16[2,32,128]{2,1,0:T(8,128)(2,1)S(1)}, u32[]{:S(2)}, u32[]{:S(2)}) collective-permute-start(f16[2,32,128]{2,1,0:T(8,128)(2,1)S(1)} %get-tuple-element.62), channel_id=1, source_target_pairs={{0,1},{1,0},{2,3},{3,2},{4,5},{5,4},{6,7},{7,6},{8,9},{9,8},{10,11... | collective-permute-start | bytes 49160 | tf_op jit(solution)/shard_map/ppermute | solution.py:28
  31.0 2.9 %collective-permute-start.17 = (f16[2,32,128]{2,1,0:T(8,128)(2,1)S(1)}, f16[2,32,128]{2,1,0:T(8,128)(2,1)S(1)}, u32[]{:S(2)}, u32[]{:S(2)}) collective-permute-start(f16[2,32,128]{2,1,0:T(8,128)(2,1)S(1)} %pad_maximum_fusion.9), channel_id=1, source_target_pairs={{0,2},{2,0},{4,6},{6,4},{8,10},{10,8},{12,14},{14,12},{1,3},{3,1},... | collective-permute-start | bytes 49160 | tf_op jit(solution)/shard_map/ppermute | solution.py:28
  32.4 4.0 %collective-permute-start.9 = (f16[2,32,256]{2,1,0:T(8,128)(2,1)S(1)}, f16[2,32,256]{2,1,0:T(8,128)(2,1)S(1)}, u32[]{:S(2)}, u32[]{:S(2)}) collective-permute-start(f16[2,32,256]{2,1,0:T(8,128)(2,1)S(1)} %get-tuple-element.58), channel_id=1, source_target_pairs={{0,1},{1,0},{2,3},{3,2},{4,5},{5,4},{6,7},{7,6},{8,9},{9,8},{10,11... | collective-permute-start | bytes 98312 | tf_op jit(solution)/shard_map/ppermute | solution.py:28
  36.4 1.3 %collective-permute-start.10 = (f16[2,32,256]{2,1,0:T(8,128)(2,1)S(1)}, f16[2,32,256]{2,1,0:T(8,128)(2,1)S(1)}, u32[]{:S(2)}, u32[]{:S(2)}) collective-permute-start(f16[2,32,256]{2,1,0:T(8,128)(2,1)S(1)} %pad_maximum_fusion.8), channel_id=1, source_target_pairs={{0,2},{2,0},{4,6},{6,4},{8,10},{10,8},{12,14},{14,12},{1,3},{3,1},... | collective-permute-start | bytes 98312 | tf_op jit(solution)/shard_map/ppermute | solution.py:28

commit v4 on v3

--- a/solution.py
+++ b/solution.py
@@ -35,22 +35,20 @@
 
 
 def terms(piece, share, ladder, driver, vir, occ):
-    mine, low, high = piece
-    size = high - low
-    core = lax.axis_index("col") & 1
-    side = core if mine else 1 - core
-    for i in range(ladder.shape[1] // size):
-        span = pl.ds(pl.multiple_of((2 * i + side) * share + low, LANES), size)
-        residual = driver[:, span].astype(jnp.float32) + ladder[:, i * size : (i + 1) * size] * (1 / SCALE)
-        yield span, residual, vir - occ[:, span]
+    mine, step, low, high = piece
+    core, pair = lax.axis_index("col") & 1, lax.axis_index("pair")
+    part = 2 * (pair ^ step) + (core if mine else 1 - core)
+    span = pl.ds(pl.multiple_of(part * share + low, LANES), high - low)
+    residual = driver[:, span].astype(jnp.float32) + ladder[...] * (1 / SCALE)
+    return span, residual, vir - occ[:, span]
 
 
 def couple(total, pieces, share, ladders, driver, vir, occ, coupling):
     for piece, ladder in zip(pieces, ladders):
-        for span, residual, denom in terms(piece, share, ladder, driver, vir, occ):
-            scaled = (residual / denom).astype(jnp.bfloat16)
-            product = jnp.dot(scaled, coupling[span, :], preferred_element_type=jnp.float32)
-            total = product if total is None else total + product
+        span, residual, denom = terms(piece, share, ladder, driver, vir, occ)
+        scaled = (residual / denom).astype(jnp.bfloat16)
+        product = jnp.dot(scaled, coupling[span, :], preferred_element_type=jnp.float32)
+        total = product if total is None else total + product
     return total
 
 
@@ -65,8 +63,8 @@
     column = tall(vir)
     coupled[...] = couple(begun[...], pieces[last:], share, ladders[last:], driver, column, occ, coupling)
     for piece, ladder in zip(pieces, ladders):
-        for span, residual, denom in terms(piece, share, ladder, driver, column, occ):
-            out[:, span] = -(residual - coupled[:, span]) / denom
+        span, residual, denom = terms(piece, share, ladder, driver, column, occ)
+        out[:, span] = -(residual - coupled[:, span]) / denom
 
 
 def update_call(kernel, rows, columns, scratch, *args):
@@ -211,34 +209,49 @@
                 arrived[chunk].append(got)
 
         rest = (driver, vir_energy[None, :], occ_energy[None, :], occ_coupling)
-        pieces, ladders = [], []
+        stages = [[], [], []]
         for c, (low, high) in enumerate(bounds):
+            final = c == len(bounds) - 1
             total = totals[c]
             for value in arrived[c]:
                 total += value.astype(jnp.float32)
             blocks = total.astype(jnp.float16).reshape(2, pair_n, own_rows, high - low)
             outgoing = [pick(at_pair, [blocks[:, i ^ s] for i in range(pair_n)]) for s in range(pair_n)]
-            got = outgoing[:1]
-            for step in range(1, pair_n):
-                got.append(flip(outgoing[step], "pair", (pair_n,), (step,)))
-            keep = [jnp.where(first_core, g[0], g[1]) for g in got]
-            send = jnp.stack([jnp.where(first_core, g[1], g[0]) for g in got])
-            back = flip(send, "col", (cols_n,), (1,))
-            for mine_side, values in ((True, keep), (False, back)):
-                in_order = [pick(at_pair, [values[i ^ p] for p in range(pair_n)]) for i in range(pair_n)]
-                ladders.append(jnp.concatenate(in_order, 1).astype(jnp.float32))
-                pieces.append((mine_side, low, high))
+            own = [jnp.where(first_core, o[0], o[1]) for o in outgoing]
+            cross = [jnp.where(first_core, o[1], o[0]) for o in outgoing]
+
+            def add(stage, mine_side, step, value):
+                stages[stage].append(((mine_side, step, low, high), value.astype(jnp.float32)))
+
+            add(0, True, 0, own[0])
+            if final:
+                add(1, False, 0, flip(cross[0], "col", (cols_n,), (1,)))
+                for step in range(1, pair_n):
+                    add(2, True, step, flip(own[step], "pair", (pair_n,), (step,)))
+                for step in range(1, pair_n):
+                    got = flip(cross[step], ("col", "pair"), (cols_n, pair_n), (1, step))
+                    add(2, False, step, got)
+            else:
+                send = [cross[0]]
+                for step in range(1, pair_n):
+                    got = flip(outgoing[step], "pair", (pair_n,), (step,))
+                    add(0, True, step, jnp.where(first_core, got[0], got[1]))
+                    send.append(jnp.where(first_core, got[1], got[0]))
+                back = flip(jnp.stack(send), "col", (cols_n,), (1,))
+                for step in range(pair_n):
+                    add(1, False, step, back[step])
 
         columns = occ_energy.shape[0]
-        begun, done = None, 0
-        for c in range(len(bounds)):
-            upto = 2 * c + 1
-            kernel = functools.partial(begin_kernel, tuple(pieces[done:upto]), share, begun is not None)
+        begun = None
+        for c in range(2):
+            kernel = functools.partial(begin_kernel, tuple(p for p, _ in stages[c]), share, begun is not None)
             carried = [] if begun is None else [begun]
-            begun = update_call(kernel, own_rows, columns, [], *rest, *ladders[done:upto], *carried)
-            done = upto
-        kernel = functools.partial(finish_kernel, tuple(pieces), share, done)
+            begun = update_call(kernel, own_rows, columns, [], *rest, *(v for _, v in stages[c]), *carried)
+        pieces = sum(stages, [])
+        last = len(stages[0]) + len(stages[1])
+        kernel = functools.partial(finish_kernel, tuple(p for p, _ in pieces), share, last)
         scratch = [pltpu.VMEM((own_rows, columns), jnp.float32)]
+        ladders = [v for _, v in pieces]
         return update_call(kernel, own_rows, columns, scratch, *rest, *ladders, begun)
 
     return jax.shard_map(

time: 39.6 us -> 42.8 us (1.081)
  waiting for transfers between devices: 13 us -> 16.7 us
  local copies, waits for them, and re-layouts: 1.36 us -> 0.66 us
    ppermute x18 -> x19, waiting for transfers between devices: 13 us -> 16.7 us  [flip(): return lax.ppermute(value, axes, pairs)]
    broadcast_in_dim x1, local copies, waits for them, and re-layouts: 0.7 us -> 0.01 us  [body(): rest = (driver, vir_energy[None, :], occ_energy[None, :], occ_coupling)]
    ppermute x18 -> x19, starting transfers between devices: 18 us -> 18.4 us  [flip(): return lax.ppermute(value, axes, pairs)]
  transfers between devices with their start and end apart: 18 -> 19, of which waited for: 5 -> 7; matrix products, arithmetic and copies ran while one was open for 11% -> 9% of each run, Pallas kernels for 1% -> 1%
where the time goes in v4:
time: 42.8 us; the launch traced here: 42.6 us
  starting transfers between devices  18.4 us (43%)
  waiting for transfers between devices  16.7 us (39%)
  Pallas kernels  3.06 us (7%)
  other arithmetic  2.24 us (5%)
  matrix products  1.19 us (3%)
  local copies, waits for them, and re-layouts  0.66 us (2%)
    ppermute x19, starting transfers between devices, flip(): return lax.ppermute(value, axes, pairs)  18.4 us
    ppermute x19, waiting for transfers between devices, flip(): return lax.ppermute(value, axes, pairs)  16.7 us
    pallas_call x3, Pallas kernels, update_call(): pl.pallas_call(kernel, out_shape=jax.ShapeDtypeStruct((rows, columns), jn...  2.03 us
    dot_general x4, matrix products, dot(): jnp.dot(a, b, preferred_element_type=jnp.float32)  1.19 us
    mul x2, other arithmetic, screened(): values = values * jnp.repeat(keep, tile, axis=0)  1.14 us
    pallas_call x1, Pallas kernels, fetch(): pl.pallas_call(functools.partial(fetch_kernel, columns // 2, bounds), out...  1.04 us
  transfers between devices with their start and end apart: 19, of which 7 were waited for; matrix products, arithmetic and copies ran while one was open for 9% of the time, Pallas kernels for 1%

profile of v4, /device:TPU:0, one launch (start us, length us, event | category | flops | bytes accessed | tf_op | source)
XLA Modules:
  0.0 42.6 jit_solution(7671829770006692176)
XLA Ops:
  0.0 1.0 %fetch.1 = (bf16[256,256]{1,0:T(8,128)(2,1)S(1)}, bf16[256,256]{1,0:T(8,128)(2,1)S(1)}, bf16[256,128]{1,0:T(8,128)(2,1)S(1)}, bf16[256,128]{1,0:T(8,128)(2,1)S(1)}) custom-call(bf16[256,768]{1,0:T(8,128)(2,1)} %whole.1), custom_call_target="tpu_custom_call" | custom-call | tf_op jit(solution)/shard_map/fetch/pallas_call | solution.py:101
  1.1 2.5 %collective-permute-start.11 = (bf16[256,128]{1,0:T(8,128)(2,1)S(1)}, bf16[256,128]{1,0:T(8,128)(2,1)S(1)}, u32[]{:S(2)}, u32[]{:S(2)}) collective-permute-start(bf16[256,128]{1,0:T(8,128)(2,1)S(1)} %get-tuple-element.28), channel_id=1, source_target_pairs={{0,18},{2,16},{4,22},{6,20},{8,26},{10,24},{12,30},{14,28},{16,2},... | collective-permute-start | bytes 196616 | tf_op jit(solution)/shard_map/ppermute | solution.py:28
  3.5 0.7 %collective-permute-start.3 = (bf16[256,128]{1,0:T(8,128)(2,1)S(1)}, bf16[256,128]{1,0:T(8,128)(2,1)S(1)}, u32[]{:S(2)}, u32[]{:S(2)}) collective-permute-start(bf16[256,128]{1,0:T(8,128)(2,1)S(1)} %get-tuple-element.28), channel_id=1, source_target_pairs={{0,2},{2,0},{4,6},{6,4},{8,10},{10,8},{12,14},{14,12},{1,3},{3,1},... | collective-permute-start | bytes 196616 | tf_op jit(solution)/shard_map/ppermute | solution.py:28
  4.2 0.5 %collective-permute-start.1 = (s32[32,32]{1,0:T(8,128)}, s32[32,32]{1,0:T(8,128)S(1)}, u32[]{:S(2)}, u32[]{:S(2)}) collective-permute-start(s32[32,32]{1,0:T(8,128)} %param.8), channel_id=1, source_target_pairs={{0,2},{2,0},{4,6},{6,4},{8,10},{10,8},{12,14},{14,12},{1,3},{3,1},... | collective-permute-start | bytes 12296 | tf_op jit(solution)/shard_map/ppermute | solution.py:28
  4.7 0.7 %convert_multiply_fusion.1 = bf16[32,32]{1,0:T(8,128)(2,1)S(1)} fusion(s32[32,32]{1,0:T(8,128)} %param.8), kind=kLoop, calls=%fused_computation.50 | loop fusion | flops 2048 | bytes 6144 | tf_op jit(solution)/shard_map/mul | solution.py:170
  5.6 1.1 %bitcast_multiply_fusion.1 = bf16[512,512]{1,0:T(8,128)(2,1)S(1)} fusion(bf16[512,512]{1,0:T(8,128)(2,1)} %param.7, bf16[32,512]{1,0:T(8,128)(2,1)S(1)} %copy.9), kind=kLoop, calls=%fused_computation.5 | loop fusion | flops 262144 | bytes 1081344 | tf_op jit(solution)/shard_map/mul | solution.py:171
  6.9 0.2 collective-permute-start.5
  7.3 2.0 %collective-permute-start.10 = (bf16[256,128]{1,0:T(8,128)(2,1)S(1)}, bf16[256,128]{1,0:T(8,128)(2,1)S(1)}, u32[]{:S(2)}, u32[]{:S(2)}) collective-permute-start(bf16[256,128]{1,0:T(8,128)(2,1)S(1)} %get-tuple-element.27), channel_id=1, source_target_pairs={{0,16},{2,18},{4,20},{6,22},{8,24},{10,26},{12,28},{14,30},{16,0},... | collective-permute-start | bytes 196616 | tf_op jit(solution)/shard_map/ppermute | solution.py:28
  9.6 0.1 collective-permute-start.4
  9.7 0.3 fusion.3
  10.1 0.3 fusion.2
  10.4 6.6 %collective-permute-done.4 = bf16[256,256]{1,0:T(8,128)(2,1)S(1)} collective-permute-done((bf16[256,256]{1,0:T(8,128)(2,1)S(1)}, bf16[256,256]{1,0:T(8,128)(2,1)S(1)}, u32[]{:S(2)}, u32[]{:S(2)}) %collective-permute-start.4) | collective-permute-done | bytes 131104 | tf_op jit(solution)/shard_map/ppermute | solution.py:28
  17.0 0.3 fusion
  17.4 2.7 %collective-permute-start.12 = (f16[128,128]{1,0:T(8,128)(2,1)S(1)}, f16[128,128]{1,0:T(8,128)(2,1)S(1)}, u32[]{:S(2)}, u32[]{:S(2)}) collective-permute-start(f16[128,128]{1,0:T(8,128)(2,1)S(1)} %get-tuple-element.52), channel_id=1, source_target_pairs={{0,8},{2,10},{4,12},{6,14},{8,0},{10,2},{12,4},{14,6},{1,9},{3,11}... | collective-permute-start | bytes 98312 | tf_op jit(solution)/shard_map/ppermute | solution.py:28
  20.0 1.3 %collective-permute-start.13 = (f16[128,128]{1,0:T(8,128)(2,1)S(1)}, f16[128,128]{1,0:T(8,128)(2,1)S(1)}, u32[]{:S(2)}, u32[]{:S(2)}) collective-permute-start(f16[128,128]{1,0:T(8,128)(2,1)S(1)} %get-tuple-element.54), channel_id=1, source_target_pairs={{0,12},{2,14},{4,8},{6,10},{8,4},{10,6},{12,0},{14,2},{1,13},{3,15... | collective-permute-start | bytes 98312 | tf_op jit(solution)/shard_map/ppermute | solution.py:28
  21.4 0.2 collective-permute-start.14
  21.6 0.3 fusion.1
  22.0 2.9 %collective-permute-start.6 = (f16[128,256]{1,0:T(8,128)(2,1)S(1)}, f16[128,256]{1,0:T(8,128)(2,1)S(1)}, u32[]{:S(2)}, u32[]{:S(2)}) collective-permute-start(f16[128,256]{1,0:T(8,128)(2,1)S(1)} %get-tuple-element.49), channel_id=1, source_target_pairs={{0,8},{2,10},{4,12},{6,14},{8,0},{10,2},{12,4},{14,6},{1,9},{3,11}... | collective-permute-start | bytes 196616 | tf_op jit(solution)/shard_map/ppermute | solution.py:28
  24.9 0.7 %collective-permute-start.7 = (f16[128,256]{1,0:T(8,128)(2,1)S(1)}, f16[128,256]{1,0:T(8,128)(2,1)S(1)}, u32[]{:S(2)}, u32[]{:S(2)}) collective-permute-start(f16[128,256]{1,0:T(8,128)(2,1)S(1)} %get-tuple-element.51), channel_id=1, source_target_pairs={{0,4},{2,6},{4,0},{6,2},{8,12},{10,14},{12,8},{14,10},{1,5},{3,7},... | collective-permute-start | bytes 196616 | tf_op jit(solution)/shard_map/ppermute | solution.py:28
  25.6 0.9 %collective-permute-start.8 = (f16[128,256]{1,0:T(8,128)(2,1)S(1)}, f16[128,256]{1,0:T(8,128)(2,1)S(1)}, u32[]{:S(2)}, u32[]{:S(2)}) collective-permute-start(f16[128,256]{1,0:T(8,128)(2,1)S(1)} %get-tuple-element.50), channel_id=1, source_target_pairs={{0,12},{2,14},{4,8},{6,10},{8,4},{10,6},{12,0},{14,2},{1,13},{3,15... | collective-permute-start | bytes 196616 | tf_op jit(solution)/shard_map/ppermute | solution.py:28
  26.6 1.1 %collective-permute-done.6 = f16[128,256]{1,0:T(8,128)(2,1)S(1)} collective-permute-done((f16[128,256]{1,0:T(8,128)(2,1)S(1)}, f16[128,256]{1,0:T(8,128)(2,1)S(1)}, u32[]{:S(2)}, u32[]{:S(2)}) %collective-permute-start.6) | collective-permute-done | bytes 65568 | tf_op jit(solution)/shard_map/ppermute | solution.py:28
  27.8 1.9 %collective-permute-done.7 = f16[128,256]{1,0:T(8,128)(2,1)S(1)} collective-permute-done((f16[128,256]{1,0:T(8,128)(2,1)S(1)}, f16[128,256]{1,0:T(8,128)(2,1)S(1)}, u32[]{:S(2)}, u32[]{:S(2)}) %collective-permute-start.7) | collective-permute-done | bytes 65568 | tf_op jit(solution)/shard_map/ppermute | solution.py:28
  29.7 2.0 %collective-permute-done.8 = f16[128,256]{1,0:T(8,128)(2,1)S(1)} collective-permute-done((f16[128,256]{1,0:T(8,128)(2,1)S(1)}, f16[128,256]{1,0:T(8,128)(2,1)S(1)}, u32[]{:S(2)}, u32[]{:S(2)}) %collective-permute-start.8) | collective-permute-done | bytes 65568 | tf_op jit(solution)/shard_map/ppermute | solution.py:28
  31.7 1.6 %collective-permute-start.9 = (f16[2,32,256]{2,1,0:T(8,128)(2,1)S(1)}, f16[2,32,256]{2,1,0:T(8,128)(2,1)S(1)}, u32[]{:S(2)}, u32[]{:S(2)}) collective-permute-start(f16[2,32,256]{2,1,0:T(8,128)(2,1)S(1)} %get-tuple-element.55), channel_id=1, source_target_pairs={{0,1},{1,0},{2,3},{3,2},{4,5},{5,4},{6,7},{7,6},{8,9},{9,8},{10,11... | collective-permute-start | bytes 98312 | tf_op jit(solution)/shard_map/ppermute | solution.py:28
  33.3 2.4 %collective-permute-done.9 = f16[2,32,256]{2,1,0:T(8,128)(2,1)S(1)} collective-permute-done((f16[2,32,256]{2,1,0:T(8,128)(2,1)S(1)}, f16[2,32,256]{2,1,0:T(8,128)(2,1)S(1)}, u32[]{:S(2)}, u32[]{:S(2)}) %collective-permute-start.9) | collective-permute-done | bytes 32800 | tf_op jit(solution)/shard_map/ppermute | solution.py:28
  35.8 1.6 %collective-permute-start.17 = (f16[32,128]{1,0:T(8,128)(2,1)S(1)}, f16[32,128]{1,0:T(8,128)(2,1)S(1)}, u32[]{:S(2)}, u32[]{:S(2)}) collective-permute-start(f16[32,128]{1,0:T(8,128)(2,1)S(1)} %get-tuple-element.66), channel_id=1, source_target_pairs={{0,1},{1,0},{2,3},{3,2},{4,5},{5,4},{6,7},{7,6},{8,9},{9,8},{10,11... | collective-permute-start | bytes 24584 | tf_op jit(solution)/shard_map/ppermute | solution.py:28
  37.4 0.3 collective-permute-start.18
  37.8 1.8 %collective-permute-done.17 = f16[32,128]{1,0:T(8,128)(2,1)S(1)} collective-permute-done((f16[32,128]{1,0:T(8,128)(2,1)S(1)}, f16[32,128]{1,0:T(8,128)(2,1)S(1)}, u32[]{:S(2)}, u32[]{:S(2)}) %collective-permute-start.17) | collective-permute-done | bytes 8224 | tf_op jit(solution)/shard_map/ppermute | solution.py:28
  39.6 0.9 %collective-permute-done.18 = f16[32,128]{1,0:T(8,128)(2,1)S(1)} collective-permute-done((f16[32,128]{1,0:T(8,128)(2,1)S(1)}, f16[32,128]{1,0:T(8,128)(2,1)S(1)}, u32[]{:S(2)}, u32[]{:S(2)}) %collective-permute-start.18) | collective-permute-done | bytes 8224 | tf_op jit(solution)/shard_map/ppermute | solution.py:28
  40.5 0.5 %shard_map.73.refs_3_ = f32[32,1536]{1,0:T(8,128)S(1)} custom-call(bf16[32,1536]{1,0:T(8,128)(2,1)S(1)} %copy-done, f32[1,32]{1,0:T(1,128)S(1)} %bitcast.52, f32[1,1536]{1,0:T(1,128)S(1)} %broadcast_in_dim.19.occ, bf16[1536,1536]{1,0:T(8,128)(2,1)S(1)} %bitcast.51, f32[32,256]{1,0:T(8,128)S(1)} %get-tuple-element.62.refs_0_, ...), custom_call_target="tpu_custom_call" | custom-call | tf_op jit(solution)/shard_map/pallas_call | solution.py:71
  41.1 0.5 %shard_map.74.refs_8_ = f32[32,1536]{1,0:T(8,128)S(1)} custom-call(bf16[32,1536]{1,0:T(8,128)(2,1)S(1)} %copy-done, f32[1,32]{1,0:T(1,128)S(1)} %bitcast.53, f32[1,1536]{1,0:T(1,128)S(1)} %broadcast_in_dim.19.occ, bf16[1536,1536]{1,0:T(8,128)(2,1)S(1)} %bitcast.51, f32[32,256]{1,0:T(8,128)S(1)} %get-tuple-element.60.refs_0_.refs_3_, ...), custom_call_target="tpu_custom_call" | custom-call | tf_op jit(solution)/shard_map/pallas_call | solution.py:71
  41.6 1.0 %shard_map.75 = f32[32,1536]{1,0:T(8,128)} custom-call(bf16[32,1536]{1,0:T(8,128)(2,1)S(1)} %copy-done, f32[1,32]{1,0:T(1,128)S(1)} %bitcast.54, f32[1,1536]{1,0:T(1,128)S(1)} %broadcast_in_dim.19.occ, bf16[1536,1536]{1,0:T(8,128)(2,1)S(1)} %bitcast.51, f32[32,256]{1,0:T(8,128)S(1)} %get-tuple-element.62.refs_0_, f32[32,256]{1,0:T(8,128)S(1)} %get-tuple-element.64.refs_1_, ...), custom_call_target="tpu_custom_call" | custom-call | tf_op jit(solution)/shard_map/pallas_call | solution.py:71
  (58 shorter events, 1.3 us)
Async XLA Ops:
  1.1 15.9 %collective-permute-start.11 = (bf16[256,128]{1,0:T(8,128)(2,1)S(1)}, bf16[256,128]{1,0:T(8,128)(2,1)S(1)}, u32[]{:S(2)}, u32[]{:S(2)}) collective-permute-start(bf16[256,128]{1,0:T(8,128)(2,1)S(1)} %get-tuple-element.28), channel_id=1, source_target_pairs={{0,18},{2,16},{4,22},{6,20},{8,26},{10,24},{12,30},{14,28},{16,2},... | collective-permute-start | bytes 196616 | tf_op jit(solution)/shard_map/ppermute | solution.py:28
  3.5 6.6 %collective-permute-start.3 = (bf16[256,128]{1,0:T(8,128)(2,1)S(1)}, bf16[256,128]{1,0:T(8,128)(2,1)S(1)}, u32[]{:S(2)}, u32[]{:S(2)}) collective-permute-start(bf16[256,128]{1,0:T(8,128)(2,1)S(1)} %get-tuple-element.28), channel_id=1, source_target_pairs={{0,2},{2,0},{4,6},{6,4},{8,10},{10,8},{12,14},{14,12},{1,3},{3,1},... | collective-permute-start | bytes 196616 | tf_op jit(solution)/shard_map/ppermute | solution.py:28
  4.2 3.1 %collective-permute-start = (bf16[512,512]{1,0:T(8,128)(2,1)}, bf16[512,512]{1,0:T(8,128)(2,1)S(1)}, u32[]{:S(2)}, u32[]{:S(2)}) collective-permute-start(bf16[512,512]{1,0:T(8,128)(2,1)} %param.7), channel_id=1, source_target_pairs={{0,2},{2,0},{4,6},{6,4},{8,10},{10,8},{12,14},{14,12},{1,3},{3,1},... | collective-permute-start | bytes 1572872 | tf_op jit(solution)/shard_map/ppermute | solution.py:28
  4.2 2.7 %collective-permute-start.1 = (s32[32,32]{1,0:T(8,128)}, s32[32,32]{1,0:T(8,128)S(1)}, u32[]{:S(2)}, u32[]{:S(2)}) collective-permute-start(s32[32,32]{1,0:T(8,128)} %param.8), channel_id=1, source_target_pairs={{0,2},{2,0},{4,6},{6,4},{8,10},{10,8},{12,14},{14,12},{1,3},{3,1},... | collective-permute-start | bytes 12296 | tf_op jit(solution)/shard_map/ppermute | solution.py:28
  4.7 4.9 %collective-permute-start.2 = (bf16[256,256]{1,0:T(8,128)(2,1)S(1)}, bf16[256,256]{1,0:T(8,128)(2,1)S(1)}, u32[]{:S(2)}, u32[]{:S(2)}) collective-permute-start(bf16[256,256]{1,0:T(8,128)(2,1)S(1)} %get-tuple-element.26), channel_id=1, source_target_pairs={{0,2},{2,0},{4,6},{6,4},{8,10},{10,8},{12,14},{14,12},{1,3},{3,1},... | collective-permute-start | bytes 393224 | tf_op jit(solution)/shard_map/ppermute | solution.py:28
  6.9 10.1 %collective-permute-start.5 = (bf16[256,256]{1,0:T(8,128)(2,1)S(1)}, bf16[256,256]{1,0:T(8,128)(2,1)S(1)}, u32[]{:S(2)}, u32[]{:S(2)}) collective-permute-start(bf16[256,256]{1,0:T(8,128)(2,1)S(1)} %get-tuple-element.26), channel_id=1, source_target_pairs={{0,18},{2,16},{4,22},{6,20},{8,26},{10,24},{12,30},{14,28},{16,2},... | collective-permute-start | bytes 393224 | tf_op jit(solution)/shard_map/ppermute | solution.py:28
  7.3 9.6 %collective-permute-start.10 = (bf16[256,128]{1,0:T(8,128)(2,1)S(1)}, bf16[256,128]{1,0:T(8,128)(2,1)S(1)}, u32[]{:S(2)}, u32[]{:S(2)}) collective-permute-start(bf16[256,128]{1,0:T(8,128)(2,1)S(1)} %get-tuple-element.27), channel_id=1, source_target_pairs={{0,16},{2,18},{4,20},{6,22},{8,24},{10,26},{12,28},{14,30},{16,0},... | collective-permute-start | bytes 196616 | tf_op jit(solution)/shard_map/ppermute | solution.py:28
  9.4 31.1 %slice-start = ((s8[4718592]{0:T(1024)(128)(4,1)}), s8[4194304]{0:T(1024)(128)(4,1)S(1)}, s32[]{:S(2)}) async-start(s8[4718592]{0:T(1024)(128)(4,1)} %bitcast.50), calls=%async_computation | async-start | bytes 8388608
  9.6 7.3 %collective-permute-start.4 = (bf16[256,256]{1,0:T(8,128)(2,1)S(1)}, bf16[256,256]{1,0:T(8,128)(2,1)S(1)}, u32[]{:S(2)}, u32[]{:S(2)}) collective-permute-start(bf16[256,256]{1,0:T(8,128)(2,1)S(1)} %get-tuple-element.25), channel_id=1, source_target_pairs={{0,16},{2,18},{4,20},{6,22},{8,24},{10,26},{12,28},{14,30},{16,0},... | collective-permute-start | bytes 393224 | tf_op jit(solution)/shard_map/ppermute | solution.py:28
  9.7 28.0 %copy-start.2 = (f32[1536]{0:T(1024)S(1)}, f32[1536]{0:T(1024)}, u32[]{:S(2)}) copy-start(f32[1536]{0:T(1024)} %param.12) | copy-start | bytes 18436
  10.0 30.5 %slice-start.1 = ((s8[4718592]{0:T(1024)(128)(4,1)}), s8[524288]{0:T(1024)(128)(4,1)S(1)}, s32[]{:S(2)}) async-start(s8[4718592]{0:T(1024)(128)(4,1)} %bitcast.50), calls=%async_computation.1 | async-start | bytes 1048576
  10.1 30.5 %copy-start = (bf16[32,1536]{1,0:T(8,128)(2,1)S(1)}, bf16[32,1536]{1,0:T(8,128)(2,1)}, u32[]{:S(2)}) copy-start(bf16[32,1536]{1,0:T(8,128)(2,1)} %driver.5) | copy-start | bytes 294916
  10.1 30.5 %copy-start.1 = (f32[32]{0:T(128)S(1)}, f32[32]{0:T(128)}, u32[]{:S(2)}) copy-start(f32[32]{0:T(128)} %param.11) | copy-start | bytes 388
  17.4 8.2 %collective-permute-start.12 = (f16[128,128]{1,0:T(8,128)(2,1)S(1)}, f16[128,128]{1,0:T(8,128)(2,1)S(1)}, u32[]{:S(2)}, u32[]{:S(2)}) collective-permute-start(f16[128,128]{1,0:T(8,128)(2,1)S(1)} %get-tuple-element.52), channel_id=1, source_target_pairs={{0,8},{2,10},{4,12},{6,14},{8,0},{10,2},{12,4},{14,6},{1,9},{3,11}... | collective-permute-start | bytes 98312 | tf_op jit(solution)/shard_map/ppermute | solution.py:28
  20.0 6.5 %collective-permute-start.13 = (f16[128,128]{1,0:T(8,128)(2,1)S(1)}, f16[128,128]{1,0:T(8,128)(2,1)S(1)}, u32[]{:S(2)}, u32[]{:S(2)}) collective-permute-start(f16[128,128]{1,0:T(8,128)(2,1)S(1)} %get-tuple-element.54), channel_id=1, source_target_pairs={{0,12},{2,14},{4,8},{6,10},{8,4},{10,6},{12,0},{14,2},{1,13},{3,15... | collective-permute-start | bytes 98312 | tf_op jit(solution)/shard_map/ppermute | solution.py:28
  21.4 5.1 %collective-permute-start.14 = (f16[128,128]{1,0:T(8,128)(2,1)S(1)}, f16[128,128]{1,0:T(8,128)(2,1)S(1)}, u32[]{:S(2)}, u32[]{:S(2)}) collective-permute-start(f16[128,128]{1,0:T(8,128)(2,1)S(1)} %get-tuple-element.53), channel_id=1, source_target_pairs={{0,4},{2,6},{4,0},{6,2},{8,12},{10,14},{12,8},{14,10},{1,5},{3,7},... | collective-permute-start | bytes 98312 | tf_op jit(solution)/shard_map/ppermute | solution.py:28
  22.0 5.8 %collective-permute-start.6 = (f16[128,256]{1,0:T(8,128)(2,1)S(1)}, f16[128,256]{1,0:T(8,128)(2,1)S(1)}, u32[]{:S(2)}, u32[]{:S(2)}) collective-permute-start(f16[128,256]{1,0:T(8,128)(2,1)S(1)} %get-tuple-element.49), channel_id=1, source_target_pairs={{0,8},{2,10},{4,12},{6,14},{8,0},{10,2},{12,4},{14,6},{1,9},{3,11}... | collective-permute-start | bytes 196616 | tf_op jit(solution)/shard_map/ppermute | solution.py:28
  24.9 4.8 %collective-permute-start.7 = (f16[128,256]{1,0:T(8,128)(2,1)S(1)}, f16[128,256]{1,0:T(8,128)(2,1)S(1)}, u32[]{:S(2)}, u32[]{:S(2)}) collective-permute-start(f16[128,256]{1,0:T(8,128)(2,1)S(1)} %get-tuple-element.51), channel_id=1, source_target_pairs={{0,4},{2,6},{4,0},{6,2},{8,12},{10,14},{12,8},{14,10},{1,5},{3,7},... | collective-permute-start | bytes 196616 | tf_op jit(solution)/shard_map/ppermute | solution.py:28
  25.6 6.1 %collective-permute-start.8 = (f16[128,256]{1,0:T(8,128)(2,1)S(1)}, f16[128,256]{1,0:T(8,128)(2,1)S(1)}, u32[]{:S(2)}, u32[]{:S(2)}) collective-permute-start(f16[128,256]{1,0:T(8,128)(2,1)S(1)} %get-tuple-element.50), channel_id=1, source_target_pairs={{0,12},{2,14},{4,8},{6,10},{8,4},{10,6},{12,0},{14,2},{1,13},{3,15... | collective-permute-start | bytes 196616 | tf_op jit(solution)/shard_map/ppermute | solution.py:28
  26.6 11.2 %collective-permute-start.16 = (f16[32,128]{1,0:T(8,128)(2,1)S(1)}, f16[32,128]{1,0:T(8,128)(2,1)S(1)}, u32[]{:S(2)}, u32[]{:S(2)}) collective-permute-start(f16[32,128]{1,0:T(8,128)(2,1)S(1)} %get-tuple-element.67), channel_id=1, source_target_pairs={{0,2},{2,0},{4,6},{6,4},{8,10},{10,8},{12,14},{14,12},{1,3},{3,1},... | collective-permute-start | bytes 24584 | tf_op jit(solution)/shard_map/ppermute | solution.py:28
  31.7 4.0 %collective-permute-start.9 = (f16[2,32,256]{2,1,0:T(8,128)(2,1)S(1)}, f16[2,32,256]{2,1,0:T(8,128)(2,1)S(1)}, u32[]{:S(2)}, u32[]{:S(2)}) collective-permute-start(f16[2,32,256]{2,1,0:T(8,128)(2,1)S(1)} %get-tuple-element.55), channel_id=1, source_target_pairs={{0,1},{1,0},{2,3},{3,2},{4,5},{5,4},{6,7},{7,6},{8,9},{9,8},{10,11... | collective-permute-start | bytes 98312 | tf_op jit(solution)/shard_map/ppermute | solution.py:28
  35.7 5.3 %collective-permute-start.15 = (f16[2,32,256]{2,1,0:T(8,128)(2,1)S(1)}, f16[2,32,256]{2,1,0:T(8,128)(2,1)S(1)}, u32[]{:S(2)}, u32[]{:S(2)}) collective-permute-start(f16[2,32,256]{2,1,0:T(8,128)(2,1)S(1)} %pad_maximum_fusion.8), channel_id=1, source_target_pairs={{0,2},{2,0},{4,6},{6,4},{8,10},{10,8},{12,14},{14,12},{1,3},{3,1},... | collective-permute-start | bytes 98312 | tf_op jit(solution)/shard_map/ppermute | solution.py:28
  35.8 3.7 %collective-permute-start.17 = (f16[32,128]{1,0:T(8,128)(2,1)S(1)}, f16[32,128]{1,0:T(8,128)(2,1)S(1)}, u32[]{:S(2)}, u32[]{:S(2)}) collective-permute-start(f16[32,128]{1,0:T(8,128)(2,1)S(1)} %get-tuple-element.66), channel_id=1, source_target_pairs={{0,1},{1,0},{2,3},{3,2},{4,5},{5,4},{6,7},{7,6},{8,9},{9,8},{10,11... | collective-permute-start | bytes 24584 | tf_op jit(solution)/shard_map/ppermute | solution.py:28
  37.4 3.1 %collective-permute-start.18 = (f16[32,128]{1,0:T(8,128)(2,1)S(1)}, f16[32,128]{1,0:T(8,128)(2,1)S(1)}, u32[]{:S(2)}, u32[]{:S(2)}) collective-permute-start(f16[32,128]{1,0:T(8,128)(2,1)S(1)} %get-tuple-element.65), channel_id=1, source_target_pairs={{0,3},{1,2},{2,1},{3,0},{4,7},{5,6},{6,5},{7,4},{8,11},{9,10},{10,... | collective-permute-start | bytes 24584 | tf_op jit(solution)/shard_map/ppermute | solution.py:28

commit v5 on v4

--- a/solution.py
+++ b/solution.py
@@ -108,7 +108,7 @@
         name="fetch",
     )(*[pltpu.with_memory_space_constraint(v, pltpu.HBM) for v in (value, *others)])
     count = 2 * len(bounds)
-    return outs[0:count:2], outs[1:count:2]
+    return outs[0:count:2], outs[1:count:2], *outs[count:]
 
 
 def pick(at, options):
@@ -149,7 +149,7 @@
 
         first_core = core == 0
         at_pair = [pair == i for i in range(pair_n)]
-        mine, others = fetch(amplitudes, bounds)
+        mine, others, kept_tiles = fetch(amplitudes, bounds, kept_tiles)
         mine, others, first_core, at_pair = lax.optimization_barrier((list(mine), list(others), first_core, at_pair))
         far, near = [], []
         for a, b in zip(mine, others):
@@ -184,10 +184,15 @@
         early = []
         for a, b in zip(mine, near):
             early.append(dot(near_left, jnp.concatenate([a, b], 0)))
-        early, far[0] = lax.optimization_barrier((early, far[0]))
+        early, far[0][0] = lax.optimization_barrier((early, far[0][0]))
+        early[0] = early[0] + dot(left[2], far[0][0])
+        early[0], far[0][1] = lax.optimization_barrier((early[0], far[0][1]))
         parts, halved = [], []
         for i, blocks in enumerate(far):
-            late = dot(far_left, jnp.concatenate(blocks, 0))
+            if i:
+                late = dot(far_left, jnp.concatenate(blocks, 0))
+            else:
+                late = dot(jnp.concatenate(left[3:], 1), jnp.concatenate(blocks[1:], 0))
             parts.append(early[i] + late)
             halved.append(parts[-1].astype(jnp.float16))
 

time: 42.8 us -> 39.7 us (0.928)
  waiting for transfers between devices: 16.7 us -> 14.1 us
  other arithmetic: 2.24 us -> 1.58 us
    ppermute x19, waiting for transfers between devices: 16.7 us -> 14.1 us  [flip(): return lax.ppermute(value, axes, pairs)]
    mul x2, other arithmetic: 0.73 us -> 0.01 us  [screened(): keep = jnp.repeat(tiles.astype(jnp.bfloat16) * SCALE, tile, axis=1)]
    dot_general x4 -> x5, matrix products: 1.19 us -> 1.33 us  [dot(): jnp.dot(a, b, preferred_element_type=jnp.float32)]
  transfers between devices with their start and end apart: 19 -> 19, of which waited for: 7 -> 10; matrix products, arithmetic and copies ran while one was open for 9% -> 8% of each run, Pallas kernels for 1% -> 1%
where the time goes in v5:
time: 39.7 us; the launch traced here: 39.5 us
  starting transfers between devices  18.3 us (46%)
  waiting for transfers between devices  14.1 us (36%)
  Pallas kernels  3.07 us (8%)
  other arithmetic  1.58 us (4%)
  matrix products  1.33 us (3%)
  local copies, waits for them, and re-layouts  0.67 us (2%)
  between operations  0.43 us (1%)
    ppermute x19, starting transfers between devices, flip(): return lax.ppermute(value, axes, pairs)  18.3 us
    ppermute x19, waiting for transfers between devices, flip(): return lax.ppermute(value, axes, pairs)  14.1 us
    pallas_call x3, Pallas kernels, update_call(): pl.pallas_call(kernel, out_shape=jax.ShapeDtypeStruct((rows, columns), jn...  2.03 us
    dot_general x5, matrix products, dot(): jnp.dot(a, b, preferred_element_type=jnp.float32)  1.33 us
    mul x2, other arithmetic, screened(): values = values * jnp.repeat(keep, tile, axis=0)  1.14 us
    pallas_call x1, Pallas kernels, fetch(): pl.pallas_call(functools.partial(fetch_kernel, columns // 2, bounds), out...  1.05 us
  transfers between devices with their start and end apart: 19, of which 10 were waited for; matrix products, arithmetic and copies ran while one was open for 8% of the time, Pallas kernels for 1%

profile of v5, /device:TPU:0, one launch (start us, length us, event | category | flops | bytes accessed | tf_op | source)
XLA Modules:
  0.0 39.5 jit_solution(13751102433757335456)
XLA Ops:
  0.0 1.0 %fetch.1 = (bf16[256,256]{1,0:T(8,128)(2,1)S(1)}, bf16[256,256]{1,0:T(8,128)(2,1)S(1)}, bf16[256,128]{1,0:T(8,128)(2,1)S(1)}, bf16[256,128]{1,0:T(8,128)(2,1)S(1)}, s32[32,32]{1,0:T(8,128)S(1)}) custom-call(bf16[256,768]{1,0:T(8,128)(2,1)} %whole.1, s32[32,32]{1,0:T(8,128)} %refs_0_.1), custom_call_target="tpu_custom_call" | custom-call | tf_op jit(solution)/shard_map/fetch/pallas_call | solution.py:101
  1.1 0.6 %collective-permute-start.2 = (bf16[256,256]{1,0:T(8,128)(2,1)S(1)}, bf16[256,256]{1,0:T(8,128)(2,1)S(1)}, u32[]{:S(2)}, u32[]{:S(2)}) collective-permute-start(bf16[256,256]{1,0:T(8,128)(2,1)S(1)} %get-tuple-element.29), channel_id=1, source_target_pairs={{0,2},{2,0},{4,6},{6,4},{8,10},{10,8},{12,14},{14,12},{1,3},{3,1},... | collective-permute-start | bytes 393224 | tf_op jit(solution)/shard_map/ppermute | solution.py:28
  1.6 2.6 %collective-permute-start.5 = (bf16[256,256]{1,0:T(8,128)(2,1)S(1)}, bf16[256,256]{1,0:T(8,128)(2,1)S(1)}, u32[]{:S(2)}, u32[]{:S(2)}) collective-permute-start(bf16[256,256]{1,0:T(8,128)(2,1)S(1)} %get-tuple-element.29), channel_id=1, source_target_pairs={{0,18},{2,16},{4,22},{6,20},{8,26},{10,24},{12,30},{14,28},{16,2},... | collective-permute-start | bytes 393224 | tf_op jit(solution)/shard_map/ppermute | solution.py:28
  4.3 0.4 %collective-permute-start.1 = (s32[32,32]{1,0:T(8,128)S(1)}, s32[32,32]{1,0:T(8,128)S(1)}, u32[]{:S(2)}, u32[]{:S(2)}) collective-permute-start(s32[32,32]{1,0:T(8,128)S(1)} %get-tuple-element.27), channel_id=1, source_target_pairs={{0,2},{2,0},{4,6},{6,4},{8,10},{10,8},{12,14},{14,12},{1,3},{3,1},... | collective-permute-start | bytes 12296 | tf_op jit(solution)/shard_map/ppermute | solution.py:28
  5.0 1.1 %bitcast_multiply_fusion.1 = bf16[512,512]{1,0:T(8,128)(2,1)S(1)} fusion(bf16[512,512]{1,0:T(8,128)(2,1)} %param.7, bf16[32,512]{1,0:T(8,128)(2,1)S(1)} %copy.9), kind=kLoop, calls=%fused_computation.8 | loop fusion | flops 262144 | bytes 1081344 | tf_op jit(solution)/shard_map/mul | solution.py:171
  6.7 2.0 %collective-permute-start.4 = (bf16[256,256]{1,0:T(8,128)(2,1)S(1)}, bf16[256,256]{1,0:T(8,128)(2,1)S(1)}, u32[]{:S(2)}, u32[]{:S(2)}) collective-permute-start(bf16[256,256]{1,0:T(8,128)(2,1)S(1)} %get-tuple-element.28), channel_id=1, source_target_pairs={{0,16},{2,18},{4,20},{6,22},{8,24},{10,26},{12,28},{14,30},{16,0},... | collective-permute-start | bytes 393224 | tf_op jit(solution)/shard_map/ppermute | solution.py:28
  9.1 0.3 fusion.4
  9.4 0.3 fusion.5
  9.7 4.5 %collective-permute-done.4 = bf16[256,256]{1,0:T(8,128)(2,1)S(1)} collective-permute-done((bf16[256,256]{1,0:T(8,128)(2,1)S(1)}, bf16[256,256]{1,0:T(8,128)(2,1)S(1)}, u32[]{:S(2)}, u32[]{:S(2)}) %collective-permute-start.4) | collective-permute-done | bytes 131104 | tf_op jit(solution)/shard_map/ppermute | solution.py:28
  14.2 0.2 fusion.30
  14.5 0.2 fusion.31
  14.7 0.2 collective-permute-done.10
  15.0 0.3 fusion
  15.4 1.6 %collective-permute-start.14 = (f16[128,128]{1,0:T(8,128)(2,1)S(1)}, f16[128,128]{1,0:T(8,128)(2,1)S(1)}, u32[]{:S(2)}, u32[]{:S(2)}) collective-permute-start(f16[128,128]{1,0:T(8,128)(2,1)S(1)} %get-tuple-element.57), channel_id=1, source_target_pairs={{0,4},{2,6},{4,0},{6,2},{8,12},{10,14},{12,8},{14,10},{1,5},{3,7},... | collective-permute-start | bytes 98312 | tf_op jit(solution)/shard_map/ppermute | solution.py:28
  17.0 2.5 %collective-permute-start.13 = (f16[128,128]{1,0:T(8,128)(2,1)S(1)}, f16[128,128]{1,0:T(8,128)(2,1)S(1)}, u32[]{:S(2)}, u32[]{:S(2)}) collective-permute-start(f16[128,128]{1,0:T(8,128)(2,1)S(1)} %get-tuple-element.58), channel_id=1, source_target_pairs={{0,12},{2,14},{4,8},{6,10},{8,4},{10,6},{12,0},{14,2},{1,13},{3,15... | collective-permute-start | bytes 98312 | tf_op jit(solution)/shard_map/ppermute | solution.py:28
  19.5 0.1 collective-permute-start.12
  19.7 3.0 %collective-permute-start.8 = (f16[128,256]{1,0:T(8,128)(2,1)S(1)}, f16[128,256]{1,0:T(8,128)(2,1)S(1)}, u32[]{:S(2)}, u32[]{:S(2)}) collective-permute-start(f16[128,256]{1,0:T(8,128)(2,1)S(1)} %get-tuple-element.54), channel_id=1, source_target_pairs={{0,12},{2,14},{4,8},{6,10},{8,4},{10,6},{12,0},{14,2},{1,13},{3,15... | collective-permute-start | bytes 196616 | tf_op jit(solution)/shard_map/ppermute | solution.py:28
  22.7 0.4 %collective-permute-start.7 = (f16[128,256]{1,0:T(8,128)(2,1)S(1)}, f16[128,256]{1,0:T(8,128)(2,1)S(1)}, u32[]{:S(2)}, u32[]{:S(2)}) collective-permute-start(f16[128,256]{1,0:T(8,128)(2,1)S(1)} %get-tuple-element.55), channel_id=1, source_target_pairs={{0,4},{2,6},{4,0},{6,2},{8,12},{10,14},{12,8},{14,10},{1,5},{3,7},... | collective-permute-start | bytes 196616 | tf_op jit(solution)/shard_map/ppermute | solution.py:28
  23.2 1.0 %collective-permute-start.6 = (f16[128,256]{1,0:T(8,128)(2,1)S(1)}, f16[128,256]{1,0:T(8,128)(2,1)S(1)}, u32[]{:S(2)}, u32[]{:S(2)}) collective-permute-start(f16[128,256]{1,0:T(8,128)(2,1)S(1)} %get-tuple-element.53), channel_id=1, source_target_pairs={{0,8},{2,10},{4,12},{6,14},{8,0},{10,2},{12,4},{14,6},{1,9},{3,11}... | collective-permute-start | bytes 196616 | tf_op jit(solution)/shard_map/ppermute | solution.py:28
  24.2 0.8 %collective-permute-done.12 = f16[128,128]{1,0:T(8,128)(2,1)S(1)} collective-permute-done((f16[128,128]{1,0:T(8,128)(2,1)S(1)}, f16[128,128]{1,0:T(8,128)(2,1)S(1)}, u32[]{:S(2)}, u32[]{:S(2)}) %collective-permute-start.12) | collective-permute-done | bytes 32800 | tf_op jit(solution)/shard_map/ppermute | solution.py:28
  25.1 0.8 %collective-permute-done.8 = f16[128,256]{1,0:T(8,128)(2,1)S(1)} collective-permute-done((f16[128,256]{1,0:T(8,128)(2,1)S(1)}, f16[128,256]{1,0:T(8,128)(2,1)S(1)}, u32[]{:S(2)}, u32[]{:S(2)}) %collective-permute-start.8) | collective-permute-done | bytes 65568 | tf_op jit(solution)/shard_map/ppermute | solution.py:28
  25.9 1.3 %collective-permute-done.7 = f16[128,256]{1,0:T(8,128)(2,1)S(1)} collective-permute-done((f16[128,256]{1,0:T(8,128)(2,1)S(1)}, f16[128,256]{1,0:T(8,128)(2,1)S(1)}, u32[]{:S(2)}, u32[]{:S(2)}) %collective-permute-start.7) | collective-permute-done | bytes 65568 | tf_op jit(solution)/shard_map/ppermute | solution.py:28
  27.3 1.3 %collective-permute-done.6 = f16[128,256]{1,0:T(8,128)(2,1)S(1)} collective-permute-done((f16[128,256]{1,0:T(8,128)(2,1)S(1)}, f16[128,256]{1,0:T(8,128)(2,1)S(1)}, u32[]{:S(2)}, u32[]{:S(2)}) %collective-permute-start.6) | collective-permute-done | bytes 65568 | tf_op jit(solution)/shard_map/ppermute | solution.py:28
  28.6 1.6 %collective-permute-start.9 = (f16[2,32,256]{2,1,0:T(8,128)(2,1)S(1)}, f16[2,32,256]{2,1,0:T(8,128)(2,1)S(1)}, u32[]{:S(2)}, u32[]{:S(2)}) collective-permute-start(f16[2,32,256]{2,1,0:T(8,128)(2,1)S(1)} %get-tuple-element.59), channel_id=1, source_target_pairs={{0,1},{1,0},{2,3},{3,2},{4,5},{5,4},{6,7},{7,6},{8,9},{9,8},{10,11... | collective-permute-start | bytes 98312 | tf_op jit(solution)/shard_map/ppermute | solution.py:28
  30.2 2.4 %collective-permute-done.9 = f16[2,32,256]{2,1,0:T(8,128)(2,1)S(1)} collective-permute-done((f16[2,32,256]{2,1,0:T(8,128)(2,1)S(1)}, f16[2,32,256]{2,1,0:T(8,128)(2,1)S(1)}, u32[]{:S(2)}, u32[]{:S(2)}) %collective-permute-start.9) | collective-permute-done | bytes 32800 | tf_op jit(solution)/shard_map/ppermute | solution.py:28
  32.8 1.6 %collective-permute-start.17 = (f16[32,128]{1,0:T(8,128)(2,1)S(1)}, f16[32,128]{1,0:T(8,128)(2,1)S(1)}, u32[]{:S(2)}, u32[]{:S(2)}) collective-permute-start(f16[32,128]{1,0:T(8,128)(2,1)S(1)} %get-tuple-element.70), channel_id=1, source_target_pairs={{0,1},{1,0},{2,3},{3,2},{4,5},{5,4},{6,7},{7,6},{8,9},{9,8},{10,11... | collective-permute-start | bytes 24584 | tf_op jit(solution)/shard_map/ppermute | solution.py:28
  34.3 0.3 collective-permute-start.18
  34.7 1.8 %collective-permute-done.17 = f16[32,128]{1,0:T(8,128)(2,1)S(1)} collective-permute-done((f16[32,128]{1,0:T(8,128)(2,1)S(1)}, f16[32,128]{1,0:T(8,128)(2,1)S(1)}, u32[]{:S(2)}, u32[]{:S(2)}) %collective-permute-start.17) | collective-permute-done | bytes 8224 | tf_op jit(solution)/shard_map/ppermute | solution.py:28
  36.5 0.9 %collective-permute-done.18 = f16[32,128]{1,0:T(8,128)(2,1)S(1)} collective-permute-done((f16[32,128]{1,0:T(8,128)(2,1)S(1)}, f16[32,128]{1,0:T(8,128)(2,1)S(1)}, u32[]{:S(2)}, u32[]{:S(2)}) %collective-permute-start.18) | collective-permute-done | bytes 8224 | tf_op jit(solution)/shard_map/ppermute | solution.py:28
  37.5 0.5 %shard_map.73.refs_3_ = f32[32,1536]{1,0:T(8,128)S(1)} custom-call(bf16[32,1536]{1,0:T(8,128)(2,1)S(1)} %copy-done, f32[1,32]{1,0:T(1,128)S(1)} %bitcast.56, f32[1,1536]{1,0:T(1,128)S(1)} %broadcast_in_dim.19.occ, bf16[1536,1536]{1,0:T(8,128)(2,1)S(1)} %bitcast.55, f32[32,256]{1,0:T(8,128)S(1)} %get-tuple-element.66.refs_0_, ...), custom_call_target="tpu_custom_call" | custom-call | tf_op jit(solution)/shard_map/pallas_call | solution.py:71
  38.0 0.5 %shard_map.74.refs_8_ = f32[32,1536]{1,0:T(8,128)S(1)} custom-call(bf16[32,1536]{1,0:T(8,128)(2,1)S(1)} %copy-done, f32[1,32]{1,0:T(1,128)S(1)} %bitcast.57, f32[1,1536]{1,0:T(1,128)S(1)} %broadcast_in_dim.19.occ, bf16[1536,1536]{1,0:T(8,128)(2,1)S(1)} %bitcast.55, f32[32,256]{1,0:T(8,128)S(1)} %get-tuple-element.64.refs_0_.refs_3_, ...), custom_call_target="tpu_custom_call" | custom-call | tf_op jit(solution)/shard_map/pallas_call | solution.py:71
  38.5 1.0 %shard_map.75 = f32[32,1536]{1,0:T(8,128)} custom-call(bf16[32,1536]{1,0:T(8,128)(2,1)S(1)} %copy-done, f32[1,32]{1,0:T(1,128)S(1)} %bitcast.58, f32[1,1536]{1,0:T(1,128)S(1)} %broadcast_in_dim.19.occ, bf16[1536,1536]{1,0:T(8,128)(2,1)S(1)} %bitcast.55, f32[32,256]{1,0:T(8,128)S(1)} %get-tuple-element.66.refs_0_, f32[32,256]{1,0:T(8,128)S(1)} %get-tuple-element.68.refs_1_, ...), custom_call_target="tpu_custom_call" | custom-call | tf_op jit(solution)/shard_map/pallas_call | solution.py:71
  (61 shorter events, 1.7 us)
Async XLA Ops:
  1.1 8.3 %collective-permute-start.2 = (bf16[256,256]{1,0:T(8,128)(2,1)S(1)}, bf16[256,256]{1,0:T(8,128)(2,1)S(1)}, u32[]{:S(2)}, u32[]{:S(2)}) collective-permute-start(bf16[256,256]{1,0:T(8,128)(2,1)S(1)} %get-tuple-element.29), channel_id=1, source_target_pairs={{0,2},{2,0},{4,6},{6,4},{8,10},{10,8},{12,14},{14,12},{1,3},{3,1},... | collective-permute-start | bytes 393224 | tf_op jit(solution)/shard_map/ppermute | solution.py:28
  1.6 12.9 %collective-permute-start.5 = (bf16[256,256]{1,0:T(8,128)(2,1)S(1)}, bf16[256,256]{1,0:T(8,128)(2,1)S(1)}, u32[]{:S(2)}, u32[]{:S(2)}) collective-permute-start(bf16[256,256]{1,0:T(8,128)(2,1)S(1)} %get-tuple-element.29), channel_id=1, source_target_pairs={{0,18},{2,16},{4,22},{6,20},{8,26},{10,24},{12,30},{14,28},{16,2},... | collective-permute-start | bytes 393224 | tf_op jit(solution)/shard_map/ppermute | solution.py:28
  4.2 2.5 %collective-permute-start = (bf16[512,512]{1,0:T(8,128)(2,1)}, bf16[512,512]{1,0:T(8,128)(2,1)S(1)}, u32[]{:S(2)}, u32[]{:S(2)}) collective-permute-start(bf16[512,512]{1,0:T(8,128)(2,1)} %param.7), channel_id=1, source_target_pairs={{0,2},{2,0},{4,6},{6,4},{8,10},{10,8},{12,14},{14,12},{1,3},{3,1},... | collective-permute-start | bytes 1572872 | tf_op jit(solution)/shard_map/ppermute | solution.py:28
  4.3 2.1 %collective-permute-start.1 = (s32[32,32]{1,0:T(8,128)S(1)}, s32[32,32]{1,0:T(8,128)S(1)}, u32[]{:S(2)}, u32[]{:S(2)}) collective-permute-start(s32[32,32]{1,0:T(8,128)S(1)} %get-tuple-element.27), channel_id=1, source_target_pairs={{0,2},{2,0},{4,6},{6,4},{8,10},{10,8},{12,14},{14,12},{1,3},{3,1},... | collective-permute-start | bytes 12296 | tf_op jit(solution)/shard_map/ppermute | solution.py:28
  4.7 4.2 %collective-permute-start.3 = (bf16[256,128]{1,0:T(8,128)(2,1)S(1)}, bf16[256,128]{1,0:T(8,128)(2,1)S(1)}, u32[]{:S(2)}, u32[]{:S(2)}) collective-permute-start(bf16[256,128]{1,0:T(8,128)(2,1)S(1)} %get-tuple-element.31), channel_id=1, source_target_pairs={{0,2},{2,0},{4,6},{6,4},{8,10},{10,8},{12,14},{14,12},{1,3},{3,1},... | collective-permute-start | bytes 196616 | tf_op jit(solution)/shard_map/ppermute | solution.py:28
  6.4 8.4 %collective-permute-start.11 = (bf16[256,128]{1,0:T(8,128)(2,1)S(1)}, bf16[256,128]{1,0:T(8,128)(2,1)S(1)}, u32[]{:S(2)}, u32[]{:S(2)}) collective-permute-start(bf16[256,128]{1,0:T(8,128)(2,1)S(1)} %get-tuple-element.31), channel_id=1, source_target_pairs={{0,18},{2,16},{4,22},{6,20},{8,26},{10,24},{12,30},{14,28},{16,2},... | collective-permute-start | bytes 196616 | tf_op jit(solution)/shard_map/ppermute | solution.py:28
  6.7 7.5 %collective-permute-start.4 = (bf16[256,256]{1,0:T(8,128)(2,1)S(1)}, bf16[256,256]{1,0:T(8,128)(2,1)S(1)}, u32[]{:S(2)}, u32[]{:S(2)}) collective-permute-start(bf16[256,256]{1,0:T(8,128)(2,1)S(1)} %get-tuple-element.28), channel_id=1, source_target_pairs={{0,16},{2,18},{4,20},{6,22},{8,24},{10,26},{12,28},{14,30},{16,0},... | collective-permute-start | bytes 393224 | tf_op jit(solution)/shard_map/ppermute | solution.py:28
  8.8 28.6 %slice-start = ((s8[4718592]{0:T(1024)(128)(4,1)}), s8[4194304]{0:T(1024)(128)(4,1)S(1)}, s32[]{:S(2)}) async-start(s8[4718592]{0:T(1024)(128)(4,1)} %bitcast.54), calls=%async_computation | async-start | bytes 8388608
  8.9 6.0 %collective-permute-start.10 = (bf16[256,128]{1,0:T(8,128)(2,1)S(1)}, bf16[256,128]{1,0:T(8,128)(2,1)S(1)}, u32[]{:S(2)}, u32[]{:S(2)}) collective-permute-start(bf16[256,128]{1,0:T(8,128)(2,1)S(1)} %get-tuple-element.30), channel_id=1, source_target_pairs={{0,16},{2,18},{4,20},{6,22},{8,24},{10,26},{12,28},{14,30},{16,0},... | collective-permute-start | bytes 196616 | tf_op jit(solution)/shard_map/ppermute | solution.py:28
  9.7 25.0 %copy-start.2 = (f32[1536]{0:T(1024)S(1)}, f32[1536]{0:T(1024)}, u32[]{:S(2)}) copy-start(f32[1536]{0:T(1024)} %param.12) | copy-start | bytes 18436
  9.7 27.7 %copy-start = (bf16[32,1536]{1,0:T(8,128)(2,1)S(1)}, bf16[32,1536]{1,0:T(8,128)(2,1)}, u32[]{:S(2)}) copy-start(bf16[32,1536]{1,0:T(8,128)(2,1)} %driver.5) | copy-start | bytes 294916
  9.7 27.7 %copy-start.1 = (f32[32]{0:T(128)S(1)}, f32[32]{0:T(128)}, u32[]{:S(2)}) copy-start(f32[32]{0:T(128)} %param.11) | copy-start | bytes 388
  14.4 23.0 %slice-start.1 = ((s8[4718592]{0:T(1024)(128)(4,1)}), s8[524288]{0:T(1024)(128)(4,1)S(1)}, s32[]{:S(2)}) async-start(s8[4718592]{0:T(1024)(128)(4,1)} %bitcast.54), calls=%async_computation.1 | async-start | bytes 1048576
  15.4 7.8 %collective-permute-start.14 = (f16[128,128]{1,0:T(8,128)(2,1)S(1)}, f16[128,128]{1,0:T(8,128)(2,1)S(1)}, u32[]{:S(2)}, u32[]{:S(2)}) collective-permute-start(f16[128,128]{1,0:T(8,128)(2,1)S(1)} %get-tuple-element.57), channel_id=1, source_target_pairs={{0,4},{2,6},{4,0},{6,2},{8,12},{10,14},{12,8},{14,10},{1,5},{3,7},... | collective-permute-start | bytes 98312 | tf_op jit(solution)/shard_map/ppermute | solution.py:28
  17.0 7.2 %collective-permute-start.13 = (f16[128,128]{1,0:T(8,128)(2,1)S(1)}, f16[128,128]{1,0:T(8,128)(2,1)S(1)}, u32[]{:S(2)}, u32[]{:S(2)}) collective-permute-start(f16[128,128]{1,0:T(8,128)(2,1)S(1)} %get-tuple-element.58), channel_id=1, source_target_pairs={{0,12},{2,14},{4,8},{6,10},{8,4},{10,6},{12,0},{14,2},{1,13},{3,15... | collective-permute-start | bytes 98312 | tf_op jit(solution)/shard_map/ppermute | solution.py:28
  19.5 5.5 %collective-permute-start.12 = (f16[128,128]{1,0:T(8,128)(2,1)S(1)}, f16[128,128]{1,0:T(8,128)(2,1)S(1)}, u32[]{:S(2)}, u32[]{:S(2)}) collective-permute-start(f16[128,128]{1,0:T(8,128)(2,1)S(1)} %get-tuple-element.56), channel_id=1, source_target_pairs={{0,8},{2,10},{4,12},{6,14},{8,0},{10,2},{12,4},{14,6},{1,9},{3,11}... | collective-permute-start | bytes 98312 | tf_op jit(solution)/shard_map/ppermute | solution.py:28
  19.7 6.2 %collective-permute-start.8 = (f16[128,256]{1,0:T(8,128)(2,1)S(1)}, f16[128,256]{1,0:T(8,128)(2,1)S(1)}, u32[]{:S(2)}, u32[]{:S(2)}) collective-permute-start(f16[128,256]{1,0:T(8,128)(2,1)S(1)} %get-tuple-element.54), channel_id=1, source_target_pairs={{0,12},{2,14},{4,8},{6,10},{8,4},{10,6},{12,0},{14,2},{1,13},{3,15... | collective-permute-start | bytes 196616 | tf_op jit(solution)/shard_map/ppermute | solution.py:28
  22.7 4.6 %collective-permute-start.7 = (f16[128,256]{1,0:T(8,128)(2,1)S(1)}, f16[128,256]{1,0:T(8,128)(2,1)S(1)}, u32[]{:S(2)}, u32[]{:S(2)}) collective-permute-start(f16[128,256]{1,0:T(8,128)(2,1)S(1)} %get-tuple-element.55), channel_id=1, source_target_pairs={{0,4},{2,6},{4,0},{6,2},{8,12},{10,14},{12,8},{14,10},{1,5},{3,7},... | collective-permute-start | bytes 196616 | tf_op jit(solution)/shard_map/ppermute | solution.py:28
  23.2 5.4 %collective-permute-start.6 = (f16[128,256]{1,0:T(8,128)(2,1)S(1)}, f16[128,256]{1,0:T(8,128)(2,1)S(1)}, u32[]{:S(2)}, u32[]{:S(2)}) collective-permute-start(f16[128,256]{1,0:T(8,128)(2,1)S(1)} %get-tuple-element.53), channel_id=1, source_target_pairs={{0,8},{2,10},{4,12},{6,14},{8,0},{10,2},{12,4},{14,6},{1,9},{3,11}... | collective-permute-start | bytes 196616 | tf_op jit(solution)/shard_map/ppermute | solution.py:28
  25.1 9.6 %collective-permute-start.16 = (f16[32,128]{1,0:T(8,128)(2,1)S(1)}, f16[32,128]{1,0:T(8,128)(2,1)S(1)}, u32[]{:S(2)}, u32[]{:S(2)}) collective-permute-start(f16[32,128]{1,0:T(8,128)(2,1)S(1)} %get-tuple-element.71), channel_id=1, source_target_pairs={{0,2},{2,0},{4,6},{6,4},{8,10},{10,8},{12,14},{14,12},{1,3},{3,1},... | collective-permute-start | bytes 24584 | tf_op jit(solution)/shard_map/ppermute | solution.py:28
  28.6 4.0 %collective-permute-start.9 = (f16[2,32,256]{2,1,0:T(8,128)(2,1)S(1)}, f16[2,32,256]{2,1,0:T(8,128)(2,1)S(1)}, u32[]{:S(2)}, u32[]{:S(2)}) collective-permute-start(f16[2,32,256]{2,1,0:T(8,128)(2,1)S(1)} %get-tuple-element.59), channel_id=1, source_target_pairs={{0,1},{1,0},{2,3},{3,2},{4,5},{5,4},{6,7},{7,6},{8,9},{9,8},{10,11... | collective-permute-start | bytes 98312 | tf_op jit(solution)/shard_map/ppermute | solution.py:28
  32.7 5.3 %collective-permute-start.15 = (f16[2,32,256]{2,1,0:T(8,128)(2,1)S(1)}, f16[2,32,256]{2,1,0:T(8,128)(2,1)S(1)}, u32[]{:S(2)}, u32[]{:S(2)}) collective-permute-start(f16[2,32,256]{2,1,0:T(8,128)(2,1)S(1)} %pad_maximum_fusion.5), channel_id=1, source_target_pairs={{0,2},{2,0},{4,6},{6,4},{8,10},{10,8},{12,14},{14,12},{1,3},{3,1},... | collective-permute-start | bytes 98312 | tf_op jit(solution)/shard_map/ppermute | solution.py:28
  32.8 3.7 %collective-permute-start.17 = (f16[32,128]{1,0:T(8,128)(2,1)S(1)}, f16[32,128]{1,0:T(8,128)(2,1)S(1)}, u32[]{:S(2)}, u32[]{:S(2)}) collective-permute-start(f16[32,128]{1,0:T(8,128)(2,1)S(1)} %get-tuple-element.70), channel_id=1, source_target_pairs={{0,1},{1,0},{2,3},{3,2},{4,5},{5,4},{6,7},{7,6},{8,9},{9,8},{10,11... | collective-permute-start | bytes 24584 | tf_op jit(solution)/shard_map/ppermute | solution.py:28
  34.3 3.1 %collective-permute-start.18 = (f16[32,128]{1,0:T(8,128)(2,1)S(1)}, f16[32,128]{1,0:T(8,128)(2,1)S(1)}, u32[]{:S(2)}, u32[]{:S(2)}) collective-permute-start(f16[32,128]{1,0:T(8,128)(2,1)S(1)} %get-tuple-element.69), channel_id=1, source_target_pairs={{0,3},{1,2},{2,1},{3,0},{4,7},{5,6},{6,5},{7,4},{8,11},{9,10},{10,... | collective-permute-start | bytes 24584 | tf_op jit(solution)/shard_map/ppermute | solution.py:28

commit v6 on v4

--- a/solution.py
+++ b/solution.py
@@ -108,7 +108,7 @@
         name="fetch",
     )(*[pltpu.with_memory_space_constraint(v, pltpu.HBM) for v in (value, *others)])
     count = 2 * len(bounds)
-    return outs[0:count:2], outs[1:count:2]
+    return outs[0:count:2], outs[1:count:2], *outs[count:]
 
 
 def pick(at, options):
@@ -119,8 +119,8 @@
 
 
 FIRST = 2
-EARLY = "213"
-REST = ((2, 1), (3, 1), (1, 1))
+EARLY = "21"
+REST = ((3, 0), (2, 1), (3, 1), (1, 1))
 
 
 def chunk_bounds(share):
@@ -149,7 +149,7 @@
 
         first_core = core == 0
         at_pair = [pair == i for i in range(pair_n)]
-        mine, others = fetch(amplitudes, bounds)
+        mine, others, kept_tiles = fetch(amplitudes, bounds, kept_tiles)
         mine, others, first_core, at_pair = lax.optimization_barrier((list(mine), list(others), first_core, at_pair))
         far, near = [], []
         for a, b in zip(mine, others):

time: 42.8 us -> 42.1 us (0.984)
  other arithmetic: 2.24 us -> 1.53 us
    mul x2, other arithmetic: 0.73 us -> 0.01 us  [screened(): keep = jnp.repeat(tiles.astype(jnp.bfloat16) * SCALE, tile, axis=1)]
  transfers between devices with their start and end apart: 19 -> 19, of which waited for: 7 -> 7; matrix products, arithmetic and copies ran while one was open for 9% -> 7% of each run, Pallas kernels for 1% -> 1%
where the time goes in v6:
time: 42.1 us; the launch traced here: 41.9 us
  starting transfers between devices  18.3 us (43%)
  waiting for transfers between devices  16.7 us (40%)
  Pallas kernels  3.07 us (7%)
  other arithmetic  1.53 us (4%)
  matrix products  1.18 us (3%)
  local copies, waits for them, and re-layouts  0.65 us (2%)
    ppermute x19, starting transfers between devices, flip(): return lax.ppermute(value, axes, pairs)  18.3 us
    ppermute x19, waiting for transfers between devices, flip(): return lax.ppermute(value, axes, pairs)  16.7 us
    pallas_call x3, Pallas kernels, update_call(): pl.pallas_call(kernel, out_shape=jax.ShapeDtypeStruct((rows, columns), jn...  2.03 us
    dot_general x4, matrix products, dot(): jnp.dot(a, b, preferred_element_type=jnp.float32)  1.18 us
    mul x2, other arithmetic, screened(): values = values * jnp.repeat(keep, tile, axis=0)  1.14 us
    pallas_call x1, Pallas kernels, fetch(): pl.pallas_call(functools.partial(fetch_kernel, columns // 2, bounds), out...  1.05 us
  transfers between devices with their start and end apart: 19, of which 7 were waited for; matrix products, arithmetic and copies ran while one was open for 7% of the time, Pallas kernels for 1%

profile of v6, /device:TPU:0, one launch (start us, length us, event | category | flops | bytes accessed | tf_op | source)
XLA Modules:
  0.0 41.9 jit_solution(4807688747364733581)
XLA Ops:
  0.0 1.0 %fetch.1 = (bf16[256,256]{1,0:T(8,128)(2,1)S(1)}, bf16[256,256]{1,0:T(8,128)(2,1)S(1)}, bf16[256,128]{1,0:T(8,128)(2,1)S(1)}, bf16[256,128]{1,0:T(8,128)(2,1)S(1)}, s32[32,32]{1,0:T(8,128)S(1)}) custom-call(bf16[256,768]{1,0:T(8,128)(2,1)} %whole.1, s32[32,32]{1,0:T(8,128)} %refs_0_.1), custom_call_target="tpu_custom_call" | custom-call | tf_op jit(solution)/shard_map/fetch/pallas_call | solution.py:101
  1.1 2.5 %collective-permute-start.11 = (bf16[256,128]{1,0:T(8,128)(2,1)S(1)}, bf16[256,128]{1,0:T(8,128)(2,1)S(1)}, u32[]{:S(2)}, u32[]{:S(2)}) collective-permute-start(bf16[256,128]{1,0:T(8,128)(2,1)S(1)} %get-tuple-element.30), channel_id=1, source_target_pairs={{0,18},{2,16},{4,22},{6,20},{8,26},{10,24},{12,30},{14,28},{16,2},... | collective-permute-start | bytes 196616 | tf_op jit(solution)/shard_map/ppermute | solution.py:28
  3.5 0.7 %collective-permute-start.3 = (bf16[256,128]{1,0:T(8,128)(2,1)S(1)}, bf16[256,128]{1,0:T(8,128)(2,1)S(1)}, u32[]{:S(2)}, u32[]{:S(2)}) collective-permute-start(bf16[256,128]{1,0:T(8,128)(2,1)S(1)} %get-tuple-element.30), channel_id=1, source_target_pairs={{0,2},{2,0},{4,6},{6,4},{8,10},{10,8},{12,14},{14,12},{1,3},{3,1},... | collective-permute-start | bytes 196616 | tf_op jit(solution)/shard_map/ppermute | solution.py:28
  4.2 0.5 %collective-permute-start = (bf16[512,512]{1,0:T(8,128)(2,1)}, bf16[512,512]{1,0:T(8,128)(2,1)S(1)}, u32[]{:S(2)}, u32[]{:S(2)}) collective-permute-start(bf16[512,512]{1,0:T(8,128)(2,1)} %param.7), channel_id=1, source_target_pairs={{0,2},{2,0},{4,6},{6,4},{8,10},{10,8},{12,14},{14,12},{1,3},{3,1},... | collective-permute-start | bytes 1572872 | tf_op jit(solution)/shard_map/ppermute | solution.py:28
  5.0 1.1 %bitcast_multiply_fusion.1 = bf16[512,512]{1,0:T(8,128)(2,1)S(1)} fusion(bf16[512,512]{1,0:T(8,128)(2,1)} %param.7, bf16[32,512]{1,0:T(8,128)(2,1)S(1)} %copy.9), kind=kLoop, calls=%fused_computation.5 | loop fusion | flops 262144 | bytes 1081344 | tf_op jit(solution)/shard_map/mul | solution.py:171
  6.2 0.2 collective-permute-start.5
  6.4 0.1 copy.10
  6.6 2.0 %collective-permute-start.10 = (bf16[256,128]{1,0:T(8,128)(2,1)S(1)}, bf16[256,128]{1,0:T(8,128)(2,1)S(1)}, u32[]{:S(2)}, u32[]{:S(2)}) collective-permute-start(bf16[256,128]{1,0:T(8,128)(2,1)S(1)} %get-tuple-element.29), channel_id=1, source_target_pairs={{0,16},{2,18},{4,20},{6,22},{8,24},{10,26},{12,28},{14,30},{16,0},... | collective-permute-start | bytes 196616 | tf_op jit(solution)/shard_map/ppermute | solution.py:28
  8.9 0.1 collective-permute-start.4
  9.0 0.3 fusion.3
  9.4 0.3 fusion.2
  9.7 6.6 %collective-permute-done.4 = bf16[256,256]{1,0:T(8,128)(2,1)S(1)} collective-permute-done((bf16[256,256]{1,0:T(8,128)(2,1)S(1)}, bf16[256,256]{1,0:T(8,128)(2,1)S(1)}, u32[]{:S(2)}, u32[]{:S(2)}) %collective-permute-start.4) | collective-permute-done | bytes 131104 | tf_op jit(solution)/shard_map/ppermute | solution.py:28
  16.3 0.3 fusion
  16.7 2.7 %collective-permute-start.12 = (f16[128,128]{1,0:T(8,128)(2,1)S(1)}, f16[128,128]{1,0:T(8,128)(2,1)S(1)}, u32[]{:S(2)}, u32[]{:S(2)}) collective-permute-start(f16[128,128]{1,0:T(8,128)(2,1)S(1)} %get-tuple-element.54), channel_id=1, source_target_pairs={{0,8},{2,10},{4,12},{6,14},{8,0},{10,2},{12,4},{14,6},{1,9},{3,11}... | collective-permute-start | bytes 98312 | tf_op jit(solution)/shard_map/ppermute | solution.py:28
  19.3 1.4 %collective-permute-start.13 = (f16[128,128]{1,0:T(8,128)(2,1)S(1)}, f16[128,128]{1,0:T(8,128)(2,1)S(1)}, u32[]{:S(2)}, u32[]{:S(2)}) collective-permute-start(f16[128,128]{1,0:T(8,128)(2,1)S(1)} %get-tuple-element.56), channel_id=1, source_target_pairs={{0,12},{2,14},{4,8},{6,10},{8,4},{10,6},{12,0},{14,2},{1,13},{3,15... | collective-permute-start | bytes 98312 | tf_op jit(solution)/shard_map/ppermute | solution.py:28
  20.7 0.2 collective-permute-start.14
  20.9 0.3 fusion.1
  21.3 2.9 %collective-permute-start.6 = (f16[128,256]{1,0:T(8,128)(2,1)S(1)}, f16[128,256]{1,0:T(8,128)(2,1)S(1)}, u32[]{:S(2)}, u32[]{:S(2)}) collective-permute-start(f16[128,256]{1,0:T(8,128)(2,1)S(1)} %get-tuple-element.51), channel_id=1, source_target_pairs={{0,8},{2,10},{4,12},{6,14},{8,0},{10,2},{12,4},{14,6},{1,9},{3,11}... | collective-permute-start | bytes 196616 | tf_op jit(solution)/shard_map/ppermute | solution.py:28
  24.2 0.7 %collective-permute-start.7 = (f16[128,256]{1,0:T(8,128)(2,1)S(1)}, f16[128,256]{1,0:T(8,128)(2,1)S(1)}, u32[]{:S(2)}, u32[]{:S(2)}) collective-permute-start(f16[128,256]{1,0:T(8,128)(2,1)S(1)} %get-tuple-element.53), channel_id=1, source_target_pairs={{0,4},{2,6},{4,0},{6,2},{8,12},{10,14},{12,8},{14,10},{1,5},{3,7},... | collective-permute-start | bytes 196616 | tf_op jit(solution)/shard_map/ppermute | solution.py:28
  24.9 0.9 %collective-permute-start.8 = (f16[128,256]{1,0:T(8,128)(2,1)S(1)}, f16[128,256]{1,0:T(8,128)(2,1)S(1)}, u32[]{:S(2)}, u32[]{:S(2)}) collective-permute-start(f16[128,256]{1,0:T(8,128)(2,1)S(1)} %get-tuple-element.52), channel_id=1, source_target_pairs={{0,12},{2,14},{4,8},{6,10},{8,4},{10,6},{12,0},{14,2},{1,13},{3,15... | collective-permute-start | bytes 196616 | tf_op jit(solution)/shard_map/ppermute | solution.py:28
  25.9 1.1 %collective-permute-done.6 = f16[128,256]{1,0:T(8,128)(2,1)S(1)} collective-permute-done((f16[128,256]{1,0:T(8,128)(2,1)S(1)}, f16[128,256]{1,0:T(8,128)(2,1)S(1)}, u32[]{:S(2)}, u32[]{:S(2)}) %collective-permute-start.6) | collective-permute-done | bytes 65568 | tf_op jit(solution)/shard_map/ppermute | solution.py:28
  27.1 2.0 %collective-permute-done.7 = f16[128,256]{1,0:T(8,128)(2,1)S(1)} collective-permute-done((f16[128,256]{1,0:T(8,128)(2,1)S(1)}, f16[128,256]{1,0:T(8,128)(2,1)S(1)}, u32[]{:S(2)}, u32[]{:S(2)}) %collective-permute-start.7) | collective-permute-done | bytes 65568 | tf_op jit(solution)/shard_map/ppermute | solution.py:28
  29.0 1.9 %collective-permute-done.8 = f16[128,256]{1,0:T(8,128)(2,1)S(1)} collective-permute-done((f16[128,256]{1,0:T(8,128)(2,1)S(1)}, f16[128,256]{1,0:T(8,128)(2,1)S(1)}, u32[]{:S(2)}, u32[]{:S(2)}) %collective-permute-start.8) | collective-permute-done | bytes 65568 | tf_op jit(solution)/shard_map/ppermute | solution.py:28
  31.0 1.6 %collective-permute-start.9 = (f16[2,32,256]{2,1,0:T(8,128)(2,1)S(1)}, f16[2,32,256]{2,1,0:T(8,128)(2,1)S(1)}, u32[]{:S(2)}, u32[]{:S(2)}) collective-permute-start(f16[2,32,256]{2,1,0:T(8,128)(2,1)S(1)} %get-tuple-element.57), channel_id=1, source_target_pairs={{0,1},{1,0},{2,3},{3,2},{4,5},{5,4},{6,7},{7,6},{8,9},{9,8},{10,11... | collective-permute-start | bytes 98312 | tf_op jit(solution)/shard_map/ppermute | solution.py:28
  32.6 2.4 %collective-permute-done.9 = f16[2,32,256]{2,1,0:T(8,128)(2,1)S(1)} collective-permute-done((f16[2,32,256]{2,1,0:T(8,128)(2,1)S(1)}, f16[2,32,256]{2,1,0:T(8,128)(2,1)S(1)}, u32[]{:S(2)}, u32[]{:S(2)}) %collective-permute-start.9) | collective-permute-done | bytes 32800 | tf_op jit(solution)/shard_map/ppermute | solution.py:28
  35.1 1.6 %collective-permute-start.17 = (f16[32,128]{1,0:T(8,128)(2,1)S(1)}, f16[32,128]{1,0:T(8,128)(2,1)S(1)}, u32[]{:S(2)}, u32[]{:S(2)}) collective-permute-start(f16[32,128]{1,0:T(8,128)(2,1)S(1)} %get-tuple-element.68), channel_id=1, source_target_pairs={{0,1},{1,0},{2,3},{3,2},{4,5},{5,4},{6,7},{7,6},{8,9},{9,8},{10,11... | collective-permute-start | bytes 24584 | tf_op jit(solution)/shard_map/ppermute | solution.py:28
  36.7 0.3 collective-permute-start.18
  37.1 1.8 %collective-permute-done.17 = f16[32,128]{1,0:T(8,128)(2,1)S(1)} collective-permute-done((f16[32,128]{1,0:T(8,128)(2,1)S(1)}, f16[32,128]{1,0:T(8,128)(2,1)S(1)}, u32[]{:S(2)}, u32[]{:S(2)}) %collective-permute-start.17) | collective-permute-done | bytes 8224 | tf_op jit(solution)/shard_map/ppermute | solution.py:28
  38.9 1.0 %collective-permute-done.18 = f16[32,128]{1,0:T(8,128)(2,1)S(1)} collective-permute-done((f16[32,128]{1,0:T(8,128)(2,1)S(1)}, f16[32,128]{1,0:T(8,128)(2,1)S(1)}, u32[]{:S(2)}, u32[]{:S(2)}) %collective-permute-start.18) | collective-permute-done | bytes 8224 | tf_op jit(solution)/shard_map/ppermute | solution.py:28
  39.9 0.5 %shard_map.73.refs_3_ = f32[32,1536]{1,0:T(8,128)S(1)} custom-call(bf16[32,1536]{1,0:T(8,128)(2,1)S(1)} %copy-done, f32[1,32]{1,0:T(1,128)S(1)} %bitcast.52, f32[1,1536]{1,0:T(1,128)S(1)} %broadcast_in_dim.19.occ, bf16[1536,1536]{1,0:T(8,128)(2,1)S(1)} %bitcast.51, f32[32,256]{1,0:T(8,128)S(1)} %get-tuple-element.64.refs_0_, ...), custom_call_target="tpu_custom_call" | custom-call | tf_op jit(solution)/shard_map/pallas_call | solution.py:71
  40.4 0.5 %shard_map.74.refs_8_ = f32[32,1536]{1,0:T(8,128)S(1)} custom-call(bf16[32,1536]{1,0:T(8,128)(2,1)S(1)} %copy-done, f32[1,32]{1,0:T(1,128)S(1)} %bitcast.53, f32[1,1536]{1,0:T(1,128)S(1)} %broadcast_in_dim.19.occ, bf16[1536,1536]{1,0:T(8,128)(2,1)S(1)} %bitcast.51, f32[32,256]{1,0:T(8,128)S(1)} %get-tuple-element.62.refs_0_.refs_3_, ...), custom_call_target="tpu_custom_call" | custom-call | tf_op jit(solution)/shard_map/pallas_call | solution.py:71
  40.9 1.0 %shard_map.75 = f32[32,1536]{1,0:T(8,128)} custom-call(bf16[32,1536]{1,0:T(8,128)(2,1)S(1)} %copy-done, f32[1,32]{1,0:T(1,128)S(1)} %bitcast.54, f32[1,1536]{1,0:T(1,128)S(1)} %broadcast_in_dim.19.occ, bf16[1536,1536]{1,0:T(8,128)(2,1)S(1)} %bitcast.51, f32[32,256]{1,0:T(8,128)S(1)} %get-tuple-element.64.refs_0_, f32[32,256]{1,0:T(8,128)S(1)} %get-tuple-element.66.refs_1_, ...), custom_call_target="tpu_custom_call" | custom-call | tf_op jit(solution)/shard_map/pallas_call | solution.py:71
  (58 shorter events, 1.2 us)
Async XLA Ops:
  1.1 15.2 %collective-permute-start.11 = (bf16[256,128]{1,0:T(8,128)(2,1)S(1)}, bf16[256,128]{1,0:T(8,128)(2,1)S(1)}, u32[]{:S(2)}, u32[]{:S(2)}) collective-permute-start(bf16[256,128]{1,0:T(8,128)(2,1)S(1)} %get-tuple-element.30), channel_id=1, source_target_pairs={{0,18},{2,16},{4,22},{6,20},{8,26},{10,24},{12,30},{14,28},{16,2},... | collective-permute-start | bytes 196616 | tf_op jit(solution)/shard_map/ppermute | solution.py:28
  3.5 5.8 %collective-permute-start.3 = (bf16[256,128]{1,0:T(8,128)(2,1)S(1)}, bf16[256,128]{1,0:T(8,128)(2,1)S(1)}, u32[]{:S(2)}, u32[]{:S(2)}) collective-permute-start(bf16[256,128]{1,0:T(8,128)(2,1)S(1)} %get-tuple-element.30), channel_id=1, source_target_pairs={{0,2},{2,0},{4,6},{6,4},{8,10},{10,8},{12,14},{14,12},{1,3},{3,1},... | collective-permute-start | bytes 196616 | tf_op jit(solution)/shard_map/ppermute | solution.py:28
  4.2 2.0 %collective-permute-start.1 = (s32[32,32]{1,0:T(8,128)S(1)}, s32[32,32]{1,0:T(8,128)S(1)}, u32[]{:S(2)}, u32[]{:S(2)}) collective-permute-start(s32[32,32]{1,0:T(8,128)S(1)} %get-tuple-element.26), channel_id=1, source_target_pairs={{0,2},{2,0},{4,6},{6,4},{8,10},{10,8},{12,14},{14,12},{1,3},{3,1},... | collective-permute-start | bytes 12296 | tf_op jit(solution)/shard_map/ppermute | solution.py:28
  4.2 2.4 %collective-permute-start = (bf16[512,512]{1,0:T(8,128)(2,1)}, bf16[512,512]{1,0:T(8,128)(2,1)S(1)}, u32[]{:S(2)}, u32[]{:S(2)}) collective-permute-start(bf16[512,512]{1,0:T(8,128)(2,1)} %param.7), channel_id=1, source_target_pairs={{0,2},{2,0},{4,6},{6,4},{8,10},{10,8},{12,14},{14,12},{1,3},{3,1},... | collective-permute-start | bytes 1572872 | tf_op jit(solution)/shard_map/ppermute | solution.py:28
  4.7 4.2 %collective-permute-start.2 = (bf16[256,256]{1,0:T(8,128)(2,1)S(1)}, bf16[256,256]{1,0:T(8,128)(2,1)S(1)}, u32[]{:S(2)}, u32[]{:S(2)}) collective-permute-start(bf16[256,256]{1,0:T(8,128)(2,1)S(1)} %get-tuple-element.28), channel_id=1, source_target_pairs={{0,2},{2,0},{4,6},{6,4},{8,10},{10,8},{12,14},{14,12},{1,3},{3,1},... | collective-permute-start | bytes 393224 | tf_op jit(solution)/shard_map/ppermute | solution.py:28
  6.2 10.1 %collective-permute-start.5 = (bf16[256,256]{1,0:T(8,128)(2,1)S(1)}, bf16[256,256]{1,0:T(8,128)(2,1)S(1)}, u32[]{:S(2)}, u32[]{:S(2)}) collective-permute-start(bf16[256,256]{1,0:T(8,128)(2,1)S(1)} %get-tuple-element.28), channel_id=1, source_target_pairs={{0,18},{2,16},{4,22},{6,20},{8,26},{10,24},{12,30},{14,28},{16,2},... | collective-permute-start | bytes 393224 | tf_op jit(solution)/shard_map/ppermute | solution.py:28
  6.6 9.7 %collective-permute-start.10 = (bf16[256,128]{1,0:T(8,128)(2,1)S(1)}, bf16[256,128]{1,0:T(8,128)(2,1)S(1)}, u32[]{:S(2)}, u32[]{:S(2)}) collective-permute-start(bf16[256,128]{1,0:T(8,128)(2,1)S(1)} %get-tuple-element.29), channel_id=1, source_target_pairs={{0,16},{2,18},{4,20},{6,22},{8,24},{10,26},{12,28},{14,30},{16,0},... | collective-permute-start | bytes 196616 | tf_op jit(solution)/shard_map/ppermute | solution.py:28
  8.7 31.2 %slice-start = ((s8[4718592]{0:T(1024)(128)(4,1)}), s8[4194304]{0:T(1024)(128)(4,1)S(1)}, s32[]{:S(2)}) async-start(s8[4718592]{0:T(1024)(128)(4,1)} %bitcast.50), calls=%async_computation | async-start | bytes 8388608
  8.9 7.3 %collective-permute-start.4 = (bf16[256,256]{1,0:T(8,128)(2,1)S(1)}, bf16[256,256]{1,0:T(8,128)(2,1)S(1)}, u32[]{:S(2)}, u32[]{:S(2)}) collective-permute-start(bf16[256,256]{1,0:T(8,128)(2,1)S(1)} %get-tuple-element.27), channel_id=1, source_target_pairs={{0,16},{2,18},{4,20},{6,22},{8,24},{10,26},{12,28},{14,30},{16,0},... | collective-permute-start | bytes 393224 | tf_op jit(solution)/shard_map/ppermute | solution.py:28
  9.0 28.0 %copy-start.2 = (f32[1536]{0:T(1024)S(1)}, f32[1536]{0:T(1024)}, u32[]{:S(2)}) copy-start(f32[1536]{0:T(1024)} %param.12) | copy-start | bytes 18436
  9.3 30.5 %slice-start.1 = ((s8[4718592]{0:T(1024)(128)(4,1)}), s8[524288]{0:T(1024)(128)(4,1)S(1)}, s32[]{:S(2)}) async-start(s8[4718592]{0:T(1024)(128)(4,1)} %bitcast.50), calls=%async_computation.1 | async-start | bytes 1048576
  9.3 30.5 %copy-start = (bf16[32,1536]{1,0:T(8,128)(2,1)S(1)}, bf16[32,1536]{1,0:T(8,128)(2,1)}, u32[]{:S(2)}) copy-start(bf16[32,1536]{1,0:T(8,128)(2,1)} %driver.5) | copy-start | bytes 294916
  9.4 30.5 %copy-start.1 = (f32[32]{0:T(128)S(1)}, f32[32]{0:T(128)}, u32[]{:S(2)}) copy-start(f32[32]{0:T(128)} %param.11) | copy-start | bytes 388
  16.7 8.2 %collective-permute-start.12 = (f16[128,128]{1,0:T(8,128)(2,1)S(1)}, f16[128,128]{1,0:T(8,128)(2,1)S(1)}, u32[]{:S(2)}, u32[]{:S(2)}) collective-permute-start(f16[128,128]{1,0:T(8,128)(2,1)S(1)} %get-tuple-element.54), channel_id=1, source_target_pairs={{0,8},{2,10},{4,12},{6,14},{8,0},{10,2},{12,4},{14,6},{1,9},{3,11}... | collective-permute-start | bytes 98312 | tf_op jit(solution)/shard_map/ppermute | solution.py:28
  19.3 6.5 %collective-permute-start.13 = (f16[128,128]{1,0:T(8,128)(2,1)S(1)}, f16[128,128]{1,0:T(8,128)(2,1)S(1)}, u32[]{:S(2)}, u32[]{:S(2)}) collective-permute-start(f16[128,128]{1,0:T(8,128)(2,1)S(1)} %get-tuple-element.56), channel_id=1, source_target_pairs={{0,12},{2,14},{4,8},{6,10},{8,4},{10,6},{12,0},{14,2},{1,13},{3,15... | collective-permute-start | bytes 98312 | tf_op jit(solution)/shard_map/ppermute | solution.py:28
  20.7 5.1 %collective-permute-start.14 = (f16[128,128]{1,0:T(8,128)(2,1)S(1)}, f16[128,128]{1,0:T(8,128)(2,1)S(1)}, u32[]{:S(2)}, u32[]{:S(2)}) collective-permute-start(f16[128,128]{1,0:T(8,128)(2,1)S(1)} %get-tuple-element.55), channel_id=1, source_target_pairs={{0,4},{2,6},{4,0},{6,2},{8,12},{10,14},{12,8},{14,10},{1,5},{3,7},... | collective-permute-start | bytes 98312 | tf_op jit(solution)/shard_map/ppermute | solution.py:28
  21.3 5.7 %collective-permute-start.6 = (f16[128,256]{1,0:T(8,128)(2,1)S(1)}, f16[128,256]{1,0:T(8,128)(2,1)S(1)}, u32[]{:S(2)}, u32[]{:S(2)}) collective-permute-start(f16[128,256]{1,0:T(8,128)(2,1)S(1)} %get-tuple-element.51), channel_id=1, source_target_pairs={{0,8},{2,10},{4,12},{6,14},{8,0},{10,2},{12,4},{14,6},{1,9},{3,11}... | collective-permute-start | bytes 196616 | tf_op jit(solution)/shard_map/ppermute | solution.py:28
  24.2 4.8 %collective-permute-start.7 = (f16[128,256]{1,0:T(8,128)(2,1)S(1)}, f16[128,256]{1,0:T(8,128)(2,1)S(1)}, u32[]{:S(2)}, u32[]{:S(2)}) collective-permute-start(f16[128,256]{1,0:T(8,128)(2,1)S(1)} %get-tuple-element.53), channel_id=1, source_target_pairs={{0,4},{2,6},{4,0},{6,2},{8,12},{10,14},{12,8},{14,10},{1,5},{3,7},... | collective-permute-start | bytes 196616 | tf_op jit(solution)/shard_map/ppermute | solution.py:28
  24.9 6.1 %collective-permute-start.8 = (f16[128,256]{1,0:T(8,128)(2,1)S(1)}, f16[128,256]{1,0:T(8,128)(2,1)S(1)}, u32[]{:S(2)}, u32[]{:S(2)}) collective-permute-start(f16[128,256]{1,0:T(8,128)(2,1)S(1)} %get-tuple-element.52), channel_id=1, source_target_pairs={{0,12},{2,14},{4,8},{6,10},{8,4},{10,6},{12,0},{14,2},{1,13},{3,15... | collective-permute-start | bytes 196616 | tf_op jit(solution)/shard_map/ppermute | solution.py:28
  25.9 11.2 %collective-permute-start.16 = (f16[32,128]{1,0:T(8,128)(2,1)S(1)}, f16[32,128]{1,0:T(8,128)(2,1)S(1)}, u32[]{:S(2)}, u32[]{:S(2)}) collective-permute-start(f16[32,128]{1,0:T(8,128)(2,1)S(1)} %get-tuple-element.69), channel_id=1, source_target_pairs={{0,2},{2,0},{4,6},{6,4},{8,10},{10,8},{12,14},{14,12},{1,3},{3,1},... | collective-permute-start | bytes 24584 | tf_op jit(solution)/shard_map/ppermute | solution.py:28
  31.0 4.0 %collective-permute-start.9 = (f16[2,32,256]{2,1,0:T(8,128)(2,1)S(1)}, f16[2,32,256]{2,1,0:T(8,128)(2,1)S(1)}, u32[]{:S(2)}, u32[]{:S(2)}) collective-permute-start(f16[2,32,256]{2,1,0:T(8,128)(2,1)S(1)} %get-tuple-element.57), channel_id=1, source_target_pairs={{0,1},{1,0},{2,3},{3,2},{4,5},{5,4},{6,7},{7,6},{8,9},{9,8},{10,11... | collective-permute-start | bytes 98312 | tf_op jit(solution)/shard_map/ppermute | solution.py:28
  35.0 5.3 %collective-permute-start.15 = (f16[2,32,256]{2,1,0:T(8,128)(2,1)S(1)}, f16[2,32,256]{2,1,0:T(8,128)(2,1)S(1)}, u32[]{:S(2)}, u32[]{:S(2)}) collective-permute-start(f16[2,32,256]{2,1,0:T(8,128)(2,1)S(1)} %pad_maximum_fusion.8), channel_id=1, source_target_pairs={{0,2},{2,0},{4,6},{6,4},{8,10},{10,8},{12,14},{14,12},{1,3},{3,1},... | collective-permute-start | bytes 98312 | tf_op jit(solution)/shard_map/ppermute | solution.py:28
  35.1 3.7 %collective-permute-start.17 = (f16[32,128]{1,0:T(8,128)(2,1)S(1)}, f16[32,128]{1,0:T(8,128)(2,1)S(1)}, u32[]{:S(2)}, u32[]{:S(2)}) collective-permute-start(f16[32,128]{1,0:T(8,128)(2,1)S(1)} %get-tuple-element.68), channel_id=1, source_target_pairs={{0,1},{1,0},{2,3},{3,2},{4,5},{5,4},{6,7},{7,6},{8,9},{9,8},{10,11... | collective-permute-start | bytes 24584 | tf_op jit(solution)/shard_map/ppermute | solution.py:28
  36.7 3.1 %collective-permute-start.18 = (f16[32,128]{1,0:T(8,128)(2,1)S(1)}, f16[32,128]{1,0:T(8,128)(2,1)S(1)}, u32[]{:S(2)}, u32[]{:S(2)}) collective-permute-start(f16[32,128]{1,0:T(8,128)(2,1)S(1)} %get-tuple-element.67), channel_id=1, source_target_pairs={{0,3},{1,2},{2,1},{3,0},{4,7},{5,6},{6,5},{7,4},{8,11},{9,10},{10,... | collective-permute-start | bytes 24584 | tf_op jit(solution)/shard_map/ppermute | solution.py:28
